TPU v7x, 256 devices: a whole 4x4x8 slice. The times are simulated.
256 devices in a mesh: head: 8 (over z), page: 32 (over y, x, core).
Axes of the slice: x: 4, y: 4, z: 8, core: 2. Of those that a mesh axis runs over, the one named last changes fastest.
Arguments:
- doc_states: bfloat16 [2048, 2048], P('page'), may hold values from -6 to 6
- gain_attn: float32 [2048], replicated, may hold values from 0.1 to 1.9
- query_weight: bfloat16 [2048, 2048], P(None, 'head'), may hold values from -0.125 to 0.125
- cache_keys: bfloat16 [64, 128, 2048], P('page', None, 'head'), may hold values from -144 to 144
- cache_values: bfloat16 [64, 128, 2048], P('page', None, 'head'), may hold values from -6 to 6
- rel_bucket: int32 [64, 128], P('page'), may hold values from 0 to 31
- bias_table: float32 [32, 32], P(None, 'head'), may hold values from -4 to 4
- out_weight: bfloat16 [2048, 2048], P('head'), may hold values from -0.125 to 0.125
- gain_ffn: float32 [2048], replicated, may hold values from 0.1 to 1.9
- wi_gate: bfloat16 [2048, 5120], P(None, 'head'), may hold values from -0.125 to 0.125
- wi_up: bfloat16 [2048, 5120], P(None, 'head'), may hold values from -0.125 to 0.125
- wo_ffn: bfloat16 [5120, 2048], P('head'), may hold values from -0.078125 to 0.078125
- score_vector: float32 [2048], replicated, may hold values from -0.125 to 0.125
- query_lengths: int32 [8], replicated, may hold values from 1 to 1024
- doc_query: int32 [256], replicated, may hold values from 0 to 7
- doc_of_token: int32 [2048], replicated, may hold values from 0 to 255, as said below
- page_table: int32 [64], replicated, may hold values from 0 to 63, each once
Outputs:
- doc_scores: float32 [256], P('page')
Inputs may be any that keep to these rules, and one draw needn't show every extreme that they name: page_table lists every physical page once. `doc_of_token`: the tokens of each document form one contiguous run of 1 to 256 tokens; every document has one run, and some document has exactly 256 tokens.
All inputs are finite; a program needn't handle non-finite values.
Results may differ from a plain program's by a relative error of at most 0.03.
Values may be sent and summed in bfloat16 or wider, within the bound.
No kernel may reach another device: no remote copies, remote signals or barrier semaphores. Data moves between devices by JAX's collectives and lax.ppermute only.
A program may use at most 320 MiB of HBM per device.

v0:
```python
import jax
import jax.numpy as jnp
from jax import lax
from jax.sharding import PartitionSpec as P

NQ = 8


def combined_all(value, axis, join):
    pieces = jax.tree.map(lambda part: lax.all_gather(part, axis), value)
    head = jax.tree.map(lambda part: part[0], pieces)
    tail = jax.tree.map(lambda part: part[1:], pieces)
    so_far, _ = lax.scan(lambda so_far, section: (join(so_far, section), None), head, tail)
    return so_far


def rms_scale(values, gain):
    values = values.astype(jnp.float32)
    return values * lax.rsqrt(jnp.mean(values * values, axis=-1, keepdims=True) + 1e-06) * gain


def combine_parts(first, second):
    top_a, total_a, sums_a = first
    top_b, total_b, sums_b = second
    top = jnp.maximum(top_a, top_b)
    scale_a = jnp.exp(top_a - top)
    scale_b = jnp.exp(top_b - top)
    depth = sums_a.shape[1] // top.shape[1]
    sums = sums_a * jnp.repeat(scale_a, depth, axis=1) + sums_b * jnp.repeat(scale_b, depth, axis=1)
    return (top, total_a * scale_a + total_b * scale_b, sums)


def per_device(
    doc_states,
    gain_attn,
    query_weight,
    cache_keys,
    cache_values,
    rel_bucket,
    bias_table,
    out_weight,
    gain_ffn,
    wi_gate,
    wi_up,
    wo_ffn,
    score_vector,
    query_lengths,
    doc_query,
    doc_of_token,
    page_table,
):
    tok_dev = doc_states.shape[0]
    local_pages, page_len, local_width = cache_keys.shape
    local_heads = bias_table.shape[1]
    depth = local_width // local_heads
    key_count = local_pages * page_len
    all_pages = page_table.shape[0]
    max_pages = all_pages // NQ
    page_rank = lax.axis_index("page")
    normed = rms_scale(doc_states, gain_attn).astype(jnp.bfloat16)
    queries = jnp.dot(normed, query_weight, preferred_element_type=jnp.float32).astype(jnp.bfloat16)
    gathered = lax.all_gather(queries, "page", axis=0, tiled=True)
    total_rows = gathered.shape[0]
    doc_ids = jnp.arange(doc_query.shape[0], dtype=jnp.int32)
    tok_query = jnp.sum(
        jnp.where(doc_of_token[:, None] == doc_ids[None, :], doc_query[None, :], 0), axis=1
    )
    page_ids = page_rank * local_pages + jnp.arange(local_pages, dtype=jnp.int32)
    slots = jnp.arange(all_pages, dtype=jnp.int32)
    located = jnp.sum(
        jnp.where(page_table[None, :] == page_ids[:, None], slots[None, :], 0), axis=1
    )
    owner = located // max_pages
    logical = located % max_pages
    query_ids = jnp.arange(NQ, dtype=jnp.int32)
    owner_len = jnp.sum(
        jnp.where(owner[:, None] == query_ids[None, :], query_lengths[None, :], 0), axis=1
    )
    position = logical[:, None] * page_len + jnp.arange(page_len, dtype=jnp.int32)[None, :]
    key_query = jnp.where(position < owner_len[:, None], owner[:, None], -1).reshape(key_count)
    buckets = jnp.arange(bias_table.shape[0], dtype=jnp.int32)
    onehot = (rel_bucket.reshape(key_count)[None, :] == buckets[:, None]).astype(jnp.float32)
    key_bias = jnp.dot(bias_table.T, onehot, precision=lax.Precision.HIGHEST)
    keys = cache_keys.reshape(key_count, local_heads, depth)
    values = cache_values.reshape(key_count, local_heads, depth)
    block = min(512, total_rows)
    count = total_rows // block

    def partial_block(pair):
        rows, owners = pair
        heads = rows.reshape(block, local_heads, depth)
        scores = (
            jnp.einsum("rhd,khd->rhk", heads, keys, preferred_element_type=jnp.float32)
            + key_bias[None]
        )
        mask = (owners[:, None] == key_query[None, :])[:, None, :]
        top = jnp.max(jnp.where(mask, scores, -1e30), axis=-1)
        weights = jnp.where(mask, jnp.exp(scores - top[..., None]), 0.0)
        total = jnp.sum(weights, axis=-1)
        summed = jnp.einsum(
            "rhk,khd->rhd", weights.astype(jnp.bfloat16), values, preferred_element_type=jnp.float32
        )
        return (top, total, summed.reshape(block, local_width))

    tops, totals, summed = lax.map(
        partial_block,
        (gathered.reshape(count, block, local_width), tok_query.reshape(count, block)),
    )
    tops = tops.reshape(total_rows, local_heads)
    totals = totals.reshape(total_rows, local_heads)
    summed = summed.reshape(total_rows, local_width)
    row_start = page_rank * tok_dev
    joined_top, joined_total, joined_sums = combined_all(
        (tops, totals, summed), "page", combine_parts
    )
    own_total = lax.dynamic_slice_in_dim(joined_total, row_start, tok_dev, 0)
    own_sums = lax.dynamic_slice_in_dim(joined_sums, row_start, tok_dev, 0)
    context = (own_sums / jnp.repeat(own_total, depth, axis=1)).astype(jnp.bfloat16)
    projected = lax.psum(
        jnp.dot(context, out_weight, preferred_element_type=jnp.float32).astype(jnp.bfloat16),
        "head",
    ).astype(jnp.float32)
    hidden = doc_states.astype(jnp.float32) + projected
    normed_two = rms_scale(hidden, gain_ffn).astype(jnp.bfloat16)
    gate = jnp.dot(normed_two, wi_gate, preferred_element_type=jnp.float32)
    upper = jnp.dot(normed_two, wi_up, preferred_element_type=jnp.float32)
    middle = (jax.nn.gelu(gate, approximate=True) * upper).astype(jnp.bfloat16)
    ffn_part = jnp.dot(middle, wo_ffn, preferred_element_type=jnp.float32)
    final = hidden + lax.psum(ffn_part.astype(jnp.bfloat16), "head").astype(jnp.float32)
    tok_score = jnp.dot(final, score_vector, precision=lax.Precision.HIGHEST)
    own_docs = lax.dynamic_slice_in_dim(doc_of_token, row_start, tok_dev, 0)
    member = (own_docs[:, None] == doc_ids[None, :]).astype(jnp.float32)
    doc_sums = jnp.dot(tok_score, member, precision=lax.Precision.HIGHEST)
    pooled = lax.psum_scatter(doc_sums, "page", scatter_dimension=0, tiled=True)
    doc_dev = pooled.shape[0]
    mine = page_rank * doc_dev + jnp.arange(doc_dev, dtype=jnp.int32)
    counts = jnp.sum((doc_of_token[:, None] == mine[None, :]).astype(jnp.float32), axis=0)
    return pooled / counts


def solution(mesh):
    return jax.shard_map(
        per_device,
        mesh=mesh,
        in_specs=(
            P("page", None),
            P(),
            P(None, "head"),
            P("page", None, "head"),
            P("page", None, "head"),
            P("page", None),
            P(None, "head"),
            P("head", None),
            P(),
            P(None, "head"),
            P(None, "head"),
            P("head", None),
            P(),
            P(),
            P(),
            P(),
            P(),
        ),
        out_specs=P("page"),
        check_vma=False,
    )
```

profile of v0, /device:TPU:32, one launch (start us, length us, event | category | flops | bytes accessed | tf_op | source)
XLA Modules:
  0.0 1017.7 jit_solution(12967437557516146246)
XLA Ops:
  14.0 46.7 %all-gather.5.cloned.1.call-done = bf16[2048,256]{1,0:T(8,128)(2,1)} async-done(((bf16[64,256]{1,0:T(8,128)(2,1)}), bf16[2048,256]{1,0:T(8,128)(2,1)}) %all-gather.5.cloned.1.call-update) | async-done | bytes 1048592 | tf_op jit(solution)/shard_map/all_gather | solution.py:62
  60.7 41.0 %while.30 = (s32[]{:T(128)}, f32[4,512,4]{1,2,0:T(4,128)}, f32[4,512,4]{1,2,0:T(4,128)}, f32[4,512,256]{2,1,0:T(8,128)}, s32[4,512]{1,0:T(4,128)S(1)}, /*index=5...) while((s32[]{:T(128)}, f32[4,512,4]{1,2,0:T(4,128)}, ...), condition=%wide.region_7.8_spmd.clone, body=%wide.region_4.7_spmd.clone.sunk | while | flops 140112640 | bytes 19551472 | solution.py:105
  103.1 46.0 %all-gather.7.cloned.1.call-done = f32[32,2048,4]{1,2,0:T(4,128)} async-done(((f32[1,2048,4]{1,2,0:T(4,128)}), f32[32,2048,4]{1,2,0:T(4,128)}) %all-gather.7.cloned.1.call-update) | async-done | bytes 1048592 | tf_op jit(solution)/shard_map/all_gather | solution.py:10
  151.3 47.5 %all-gather.9.cloned.1.call-done = f32[32,2048,4]{1,2,0:T(4,128)} async-done(((f32[1,2048,4]{1,2,0:T(4,128)}), f32[32,2048,4]{1,2,0:T(4,128)}) %all-gather.9.cloned.1.call-update) | async-done | bytes 1048592 | tf_op jit(solution)/shard_map/all_gather | solution.py:10
  202.7 204.0 %all-gather.11.cloned.1.call-done = f32[32,2048,256]{2,1,0:T(8,128)} async-done(((f32[1,2048,256]{2,1,0:T(8,128)}), f32[32,2048,256]{2,1,0:T(8,128)}) %all-gather.11.cloned.1.call-update) | async-done | bytes 67108880 | tf_op jit(solution)/shard_map/all_gather | solution.py:10
  406.8 3.0 slice_bitcast_fusion
  412.7 43.9 %slice.29 = f32[31,2048,256]{2,1,0:T(8,128)} slice(f32[32,2048,256]{2,1,0:T(8,128)} %all-gather.11.cloned.1.call-done), slice={[1:32], [0:2048], [0:256]} | slice | bytes 130023424 | tf_op jit(solution)/shard_map/slice | solution.py:12
  456.6 335.9 %while.29 = (s32[]{:T(128)}, f32[2048,4]{0,1:T(4,128)S(1)}, f32[2048,4]{0,1:T(4,128)S(1)}, f32[2048,256]{0,1:T(8,128)}, f32[31,2048,4]{1,2,0:T(4,128)}, /*index=...) while((s32[]{:T(128)}, f32[2048,4]{0,1:T(4,128)S(1)}, f32[2048,4]{0,1:T(4,128)S(1)}, ...), condition=%wide.region_9.10_spmd, body=%wide.region_8.9_spmd.sunk | while | flops 1622018 | bytes 15007837 | solution.py:13
  457.5 3.0 constant_dynamic-slice_fusion.7
  463.5 4.0 fusion.75
  468.3 3.0 constant_dynamic-slice_fusion.7
  474.3 4.0 fusion.75
  479.2 3.0 constant_dynamic-slice_fusion.7
  485.1 4.0 fusion.75
  490.0 3.0 constant_dynamic-slice_fusion.7
  496.0 4.0 fusion.75
  506.8 4.0 fusion.75
  517.6 4.0 fusion.75
  528.5 4.0 fusion.75
  539.3 4.0 fusion.75
  550.2 4.0 fusion.75
  561.0 4.0 fusion.75
  571.8 4.0 fusion.75
  582.7 4.0 fusion.75
  593.5 4.0 fusion.75
  604.3 4.0 fusion.75
  615.2 4.0 fusion.75
  626.0 4.0 fusion.75
  636.8 4.0 fusion.75
  641.7 3.0 constant_dynamic-slice_fusion.7
  647.7 4.0 fusion.75
  658.5 4.0 fusion.75
  669.3 4.0 fusion.75
  680.2 4.0 fusion.75
  691.0 4.0 fusion.75
  701.8 4.0 fusion.75
  712.7 4.0 fusion.75
  723.5 4.0 fusion.75
  734.3 4.0 fusion.75
  745.2 4.0 fusion.75
  756.0 4.0 fusion.75
  766.8 4.0 fusion.75
  777.7 4.0 fusion.75
  788.5 4.0 fusion.75
  796.0 71.5 %all-reduce.4.cloned.1.call-done = bf16[64,2048]{1,0:T(8,128)(2,1)} async-done(((bf16[64,2048]{1,0:T(8,128)(2,1)}), bf16[64,2048]{1,0:T(8,128)(2,1)}) %all-reduce.4.cloned.1.call-update) | async-done | bytes 262160 | tf_op jit(solution)/shard_map/psum | solution.py:119
  871.2 3.6 convolution_convert_fusion
  876.4 69.5 %all-reduce.6.cloned.1.call-done = bf16[64,2048]{1,0:T(8,128)(2,1)} async-done(((bf16[64,2048]{1,0:T(8,128)(2,1)}), bf16[64,2048]{1,0:T(8,128)(2,1)}) %all-reduce.6.cloned.1.call-update) | async-done | bytes 262160 | tf_op jit(solution)/shard_map/psum | solution.py:129
  947.6 62.7 %all-reduce = f32[256]{0:T(256)S(1)} all-reduce(f32[256]{0:T(256)S(1)} %bitcast.123), channel_id=2, replica_groups=mesh['head'=8,'page'=32] {'page'}, use_global_device_ids=true, to_apply=%region_13.14.clone | all-reduce | flops 256 | bytes 2048
  (231 shorter events, 264.2 us)
Async XLA Ops:
  6.5 864.6 %copy-start = (bf16[640,2048]{1,0:T(8,128)(2,1)S(1)}, bf16[640,2048]{1,0:T(8,128)(2,1)}, u32[]{:S(2)}) copy-start(bf16[640,2048]{1,0:T(8,128)(2,1)} %param.32) | copy-start | bytes 7864324
  6.5 4.9 copy-start.4
  6.5 5.1 copy-start.11
  6.5 5.1 copy-start.8
  6.5 5.9 copy-start.14
  6.5 6.6 copy-start.15
  6.6 7.4 copy-start.13
  6.6 7.3 copy-start.12
  6.6 54.2 %all-gather.5.cloned.1.call-start = ((), (), s32[]{:S(2)}) async-start(), calls=%async_computation | async-start | bytes 1081344 | tf_op jit(solution)/shard_map/all_gather | solution.py:62
  10.2 138.9 %all-gather.7.cloned.1.call-start = ((), (), s32[]{:S(2)}) async-start(), calls=%async_computation.1 | async-start | bytes 1081344 | tf_op jit(solution)/shard_map/all_gather | solution.py:10
  60.7 0.9 copy-start.5
  63.4 1.3 copy-start.1
  68.2 2.8 copy-start.6
  71.0 0.9 copy-start.5
  73.6 1.3 copy-start.1
  78.5 2.8 copy-start.6
  81.2 0.9 copy-start.5
  83.9 1.3 copy-start.1
  88.7 2.8 copy-start.6
  91.5 0.9 copy-start.5
  94.1 1.3 copy-start.1
  99.0 2.8 copy-start.6
  101.7 97.1 %all-gather.9.cloned.1.call-start = ((), (), s32[]{:S(2)}) async-start(), calls=%async_computation.2 | async-start | bytes 1081344 | tf_op jit(solution)/shard_map/all_gather | solution.py:10
  102.5 304.3 %all-gather.11.cloned.1.call-start = ((), (), s32[]{:S(2)}) async-start(), calls=%async_computation.3 | async-start | bytes 69206016 | tf_op jit(solution)/shard_map/all_gather | solution.py:10
  103.0 764.4 %all-reduce.4.cloned.1.call-start = ((), (), s32[]{:S(2)}) async-start(), calls=%async_computation.4 | async-start | bytes 524288 | tf_op jit(solution)/shard_map/psum | solution.py:119
  456.6 410.8 %copy-start.2 = (bf16[64,2048]{1,0:T(8,128)(2,1)S(1)}, bf16[64,2048]{1,0:T(8,128)(2,1)}, u32[]{:S(2)}) copy-start(bf16[64,2048]{1,0:T(8,128)(2,1)} %param.21) | copy-start | bytes 786436
  792.5 76.1 %copy-start.7 = (f32[2048]{0:T(1024)S(1)}, f32[2048]{0:T(1024)}, u32[]{:S(2)}) copy-start(f32[2048]{0:T(1024)} %param.29) | copy-start | bytes 24580
  795.9 150.0 %all-reduce.6.cloned.1.call-start = ((), (), s32[]{:S(2)}) async-start(), calls=%async_computation.5 | async-start | bytes 524288 | tf_op jit(solution)/shard_map/psum | solution.py:129
  867.5 3.7 copy-start.3
  871.2 3.6 copy-start.9
  871.2 3.7 copy-start.16
  871.2 74.7 %copy-start.10 = (f32[2048]{0:T(1024)S(1)}, f32[2048]{0:T(1024)}, u32[]{:S(2)}) copy-start(f32[2048]{0:T(1024)} %param.33) | copy-start | bytes 24580
Sparse Core Ops, SparseCore 0:
  10.3 50.3 all-gather.4
  101.9 47.1 all-gather.6
  151.6 47.1 all-gather.8
  201.3 205.4 all-gather.10
  796.0 71.3 all-reduce.3
  874.9 70.8 all-reduce.5
where the time goes:
time: 1020 us
  waiting for transfers between devices  487 us (48%)
  local copies, waits for them, and re-layouts  264 us (26%)
  other arithmetic  170 us (17%)
  blocking collectives  62.7 us (6%)
  matrix products  20.4 us (2%)
  between operations  14.4 us (1%)
    all_gather x3, waiting for transfers between devices, combined_all(): pieces = jax.tree.map(lambda part: lax.all_gather(part, axis), value)  298 us
    dynamic_slice x62, local copies, waits for them, and re-layouts, combined_all(): lax.scan(lambda so_far, section: (join(so_far, section), None), head, tail)  185 us
    add x31, other arithmetic, combine_parts(): sums_a * jnp.repeat(scale_a, depth, axis=1)  125 us
    psum x1, waiting for transfers between devices, per_device(): lax.psum(jnp.dot(context, out_weight, preferred_element_type=jnp.float32)...  71.5 us
    psum x1, waiting for transfers between devices, per_device(): lax.psum(ffn_part.astype(jnp.bfloat16), 'head').astype(jnp.float32)  69.5 us
    unnamed x1, blocking collectives  62.7 us
    slice x3, local copies, waits for them, and re-layouts, combined_all(): tail = jax.tree.map(lambda part: part[1:], pieces)  48.5 us
    all_gather x1, waiting for transfers between devices, per_device(): gathered = lax.all_gather(queries, 'page', axis=0, tiled=True)  46.7 us
  transfers between devices with their start and end apart: 6, of which 6 were waited for; matrix products, arithmetic and copies ran while one was open for 1% of the time, Pallas kernels for 0%

commit v1 on v0

v1 whole, which is shorter than its diff:
```python
import jax
import jax.numpy as jnp
from jax import lax
from jax.experimental import pallas as pl
from jax.experimental.pallas import tpu as pltpu
from jax.sharding import PartitionSpec as P

NQ = 8
MASKED = -1e30
BF = jnp.bfloat16
F32 = jnp.float32


def rms_scale(values, gain):
    values = values.astype(F32)
    return values * lax.rsqrt(jnp.mean(values * values, axis=-1, keepdims=True) + 1e-06) * gain


def split_three(value):
    first = value.astype(BF)
    rest = value - first.astype(F32)
    second = rest.astype(BF)
    third = (rest - second.astype(F32)).astype(BF)
    return first, second, third


def attention_kernel(page_info, queries, keys_a, keys_b, values_a, values_b, buckets_a, buckets_b,
                     bias_table, tok_query, out, bias_wide, key_query, values_t):
    chips, tok_dev, width = queries.shape
    pages, page_len, _ = keys_a.shape
    heads = bias_table.shape[1]
    depth = width // heads
    keys_all = 2 * pages * page_len
    bucket_count = bias_table.shape[0]
    pieces = split_three(bias_table[...])
    stacked = jnp.concatenate([piece.astype(F32) for piece in pieces], axis=0)
    spread = jnp.concatenate(
        [jnp.broadcast_to(stacked[:, h : h + 1], (3 * bucket_count, 128)) for h in range(heads)], axis=1
    ).astype(BF)
    row = lax.broadcasted_iota(jnp.int32, (3 * bucket_count, page_len), 0) % bucket_count
    slot = lax.broadcasted_iota(jnp.int32, (page_len, 128), 0)
    for part, (buckets, values) in enumerate(((buckets_a, values_a), (buckets_b, values_b))):
        for page in range(pages):
            local = part * pages + page
            span = pl.ds(local * page_len, page_len)
            onehot = (jnp.broadcast_to(buckets[page : page + 1, :], row.shape) == row).astype(F32).astype(BF)
            bias_wide[span, :] = lax.dot_general(
                onehot, spread, (((0,), (0,)), ((), ())), preferred_element_type=F32
            )
            key_query[span, :] = jnp.where(slot < page_info[1, local], page_info[0, local], -1)
            values_t[:, span] = values[page].astype(F32).T.astype(BF)
    tile_chips = 4
    tile = tile_chips * tok_dev
    lane = lax.broadcasted_iota(jnp.int32, (1, 128), 1)
    left = lane < tok_dev

    def one_tile(step, carry):
        rows = queries[pl.ds(step * tile_chips, tile_chips)].reshape(tile, width)
        owner = tok_query[pl.ds(step, 1), :]
        sums = []
        logs = []
        for h in range(heads):
            cols = slice(h * depth, (h + 1) * depth)
            rows_h = rows[:, cols]
            scores = jnp.concatenate(
                [
                    lax.dot_general(
                        keys[...].reshape(pages * page_len, width)[:, cols],
                        rows_h,
                        (((1,), (1,)), ((), ())),
                        preferred_element_type=F32,
                    )
                    for keys in (keys_a, keys_b)
                ],
                axis=0,
            )
            bias = jnp.concatenate([bias_wide[:, h * 128 : (h + 1) * 128]] * (tile // 128), axis=1)
            holder = jnp.concatenate([key_query[...]] * (tile // 128), axis=1)
            scores = jnp.where(holder == owner, scores + bias, MASKED)
            top = jnp.max(scores, axis=0, keepdims=True)
            weights = jnp.exp(scores - top)
            total = jnp.sum(weights, axis=0, keepdims=True)
            summed = jnp.dot(values_t[cols, :], weights.astype(BF), preferred_element_type=F32)
            sums.append(summed / total)
            logs.append(top + jnp.log(total))
        for half in range(tile // 128):
            lanes = slice(half * 128, (half + 1) * 128)
            upper = jnp.concatenate([sums[0][:, lanes], sums[1][:, lanes]], axis=0)
            lower = jnp.concatenate([sums[2][:, lanes], sums[3][:, lanes]], axis=0)
            first = jnp.where(left, upper, pltpu.roll(lower, tok_dev, 1))
            second = jnp.where(left, pltpu.roll(upper, tok_dev, 1), lower)
            stat_u = jnp.concatenate([logs[0][:, lanes], logs[1][:, lanes]] + [jnp.zeros((6, 128), F32)], axis=0)
            stat_l = jnp.concatenate([logs[2][:, lanes], logs[3][:, lanes]] + [jnp.zeros((6, 128), F32)], axis=0)
            stat_1 = jnp.where(left, stat_u, pltpu.roll(stat_l, tok_dev, 1))
            stat_2 = jnp.where(left, pltpu.roll(stat_u, tok_dev, 1), stat_l)
            for which, (block, stat) in enumerate(((first, stat_1), (second, stat_2))):
                chip = step * tile_chips + half * 2 + which
                out[chip, 0:128, :] = block.astype(BF)
                a, b, c = split_three(stat)
                packed = jnp.concatenate(
                    [a[0:2].astype(F32), b[0:2].astype(F32), c[0:2].astype(F32), jnp.zeros((10, 128), F32)], axis=0
                )
                out[chip, 128:144, :] = packed.astype(BF)
        return carry

    lax.fori_loop(0, chips // tile_chips, one_tile, 0)


def combine_kernel(parts, out_weight, out):
    chips = parts.shape[0]
    logs = []
    for chip in range(chips):
        stat = parts[chip, 128:144, :].astype(F32)
        logs.append(stat[0:2] + stat[2:4] + stat[4:6])
    top = logs[0]
    for chip in range(1, chips):
        top = jnp.maximum(top, logs[chip])
    scales = [jnp.exp(log - top) for log in logs]
    whole = scales[0]
    for chip in range(1, chips):
        whole = whole + scales[chip]
    sums = [jnp.zeros((64, 128), F32), jnp.zeros((64, 128), F32)]
    for chip in range(chips):
        share = scales[chip] / whole
        for r in range(2):
            sums[r] = sums[r] + share[r : r + 1] * parts[chip, r * 64 : (r + 1) * 64, :].astype(F32)
    joined = jnp.concatenate(sums, axis=0).T
    context = jnp.concatenate([joined[0:64], joined[64:128]], axis=1).astype(BF)
    out[...] = jnp.dot(context, out_weight[...], preferred_element_type=F32).astype(BF)


def vmem():
    return pl.BlockSpec(memory_space=pltpu.VMEM)


def per_device(
    doc_states,
    gain_attn,
    query_weight,
    cache_keys,
    cache_values,
    rel_bucket,
    bias_table,
    out_weight,
    gain_ffn,
    wi_gate,
    wi_up,
    wo_ffn,
    score_vector,
    query_lengths,
    doc_query,
    doc_of_token,
    page_table,
):
    tok_dev, model = doc_states.shape
    local_pages, page_len, local_width = cache_keys.shape
    page_size = lax.axis_size("page")
    head_size = lax.axis_size("head")
    chips = page_size // 2
    all_pages = page_table.shape[0]
    max_pages = all_pages // NQ
    page_rank = lax.axis_index("page")
    head_rank = lax.axis_index("head")
    core = page_rank % 2
    swap = [(i, i ^ 1) for i in range(page_size)]
    chip_groups = [[2 * i + c for i in range(chips)] for c in range(2)]

    other_keys = lax.ppermute(cache_keys, "page", swap)
    other_values = lax.ppermute(cache_values, "page", swap)
    other_bucket = lax.ppermute(rel_bucket, "page", swap)

    normed = rms_scale(doc_states, gain_attn).astype(BF)
    queries = jnp.dot(normed, query_weight, preferred_element_type=F32).astype(BF)
    copies = jnp.broadcast_to(queries[None], (chips, tok_dev, local_width))
    gathered = lax.all_to_all(copies, "page", 0, 0, axis_index_groups=chip_groups, tiled=True)

    doc_ids = jnp.arange(doc_query.shape[0], dtype=jnp.int32)
    served = lax.dynamic_slice_in_dim(doc_of_token.reshape(chips, 2, tok_dev), core, 1, 1).reshape(chips // 4, 4 * tok_dev)
    tok_query = jnp.sum(
        jnp.where(served[None] == doc_ids[:, None, None], doc_query[:, None, None], 0), axis=0
    )
    ours = page_rank * local_pages + jnp.arange(local_pages, dtype=jnp.int32)
    theirs = (page_rank ^ 1) * local_pages + jnp.arange(local_pages, dtype=jnp.int32)
    page_ids = jnp.concatenate([ours, theirs])
    slots = jnp.arange(all_pages, dtype=jnp.int32)
    located = jnp.sum(jnp.where(page_table[None, :] == page_ids[:, None], slots[None, :], 0), axis=1)
    owner = located // max_pages
    query_ids = jnp.arange(NQ, dtype=jnp.int32)
    owner_len = jnp.sum(jnp.where(owner[:, None] == query_ids[None, :], query_lengths[None, :], 0), axis=1)
    page_info = jnp.stack([owner, owner_len - (located % max_pages) * page_len])

    key_count = 2 * local_pages * page_len
    local_heads = bias_table.shape[1]
    partials = pl.pallas_call(
        attention_kernel,
        out_shape=jax.ShapeDtypeStruct((chips, 144, 128), BF),
        in_specs=[pl.BlockSpec(memory_space=pltpu.SMEM)] + [vmem()] * 9,
        out_specs=vmem(),
        scratch_shapes=[
            pltpu.VMEM((key_count, local_heads * 128), F32),
            pltpu.VMEM((key_count, 128), jnp.int32),
            pltpu.VMEM((local_width, key_count), BF),
        ],
        compiler_params=pltpu.CompilerParams(vmem_limit_bytes=32 << 20),
        name="attention",
    )(page_info, gathered, cache_keys, other_keys, cache_values, other_values, rel_bucket, other_bucket,
      bias_table, tok_query)
    returned = lax.all_to_all(partials, "page", 0, 0, axis_index_groups=chip_groups, tiled=True)
    projected = pl.pallas_call(
        combine_kernel,
        out_shape=jax.ShapeDtypeStruct((tok_dev, model), BF),
        in_specs=[vmem(), vmem()],
        out_specs=vmem(),
        compiler_params=pltpu.CompilerParams(vmem_limit_bytes=32 << 20),
        name="combine",
    )(returned, out_weight)

    own = tok_dev // head_size
    terms = lax.all_to_all(projected.reshape(head_size, own, model), "head", 0, 0, tiled=True)
    own_states = lax.dynamic_slice_in_dim(doc_states, head_rank * own, own, 0)
    hidden = own_states.astype(F32) + jnp.sum(terms.astype(F32), axis=0)
    normed_two = rms_scale(hidden, gain_ffn).astype(BF)
    hidden_score = jnp.sum(hidden * score_vector, axis=-1)
    spread = jnp.broadcast_to(normed_two[None], (head_size, own, model))
    rows = lax.all_to_all(spread, "head", 0, 0, tiled=True).reshape(tok_dev, model)
    gate = jnp.dot(rows, wi_gate, preferred_element_type=F32)
    upper = jnp.dot(rows, wi_up, preferred_element_type=F32)
    middle = (jax.nn.gelu(gate, approximate=True) * upper).astype(BF)
    down_score = jnp.sum(wo_ffn.astype(F32) * score_vector, axis=-1)
    tok_part = jnp.sum(middle.astype(F32) * down_score, axis=-1)
    tok_ids = jnp.arange(tok_dev, dtype=jnp.int32)
    mine = tok_ids[:, None] == head_rank * own + jnp.arange(own, dtype=jnp.int32)[None, :]
    tok_part = tok_part + jnp.sum(jnp.where(mine, hidden_score[None, :], 0.0), axis=1)

    doc_dev = doc_query.shape[0] // page_size
    own_docs = lax.dynamic_slice_in_dim(doc_of_token, page_rank * tok_dev, tok_dev, 0)
    doc_lanes = jnp.arange(page_size * 128, dtype=jnp.int32).reshape(page_size, 128)
    doc_at = jnp.where(doc_lanes % 128 < doc_dev, (doc_lanes // 128) * doc_dev + doc_lanes % 128, -1)
    doc_sums = jnp.sum(
        jnp.where(own_docs[:, None, None] == doc_at[None], tok_part[:, None, None], 0.0), axis=0
    )
    arrived = lax.all_to_all(doc_sums, "page", 0, 0, tiled=True)
    pooled = lax.psum(jnp.sum(arrived, axis=0), "head")[:doc_dev]
    mine_docs = page_rank * doc_dev + jnp.arange(doc_dev, dtype=jnp.int32)
    counts = jnp.sum((doc_of_token[:, None] == mine_docs[None, :]).astype(F32), axis=0)
    return pooled / counts


def solution(mesh):
    return jax.shard_map(
        per_device,
        mesh=mesh,
        in_specs=(
            P("page", None),
            P(),
            P(None, "head"),
            P("page", None, "head"),
            P("page", None, "head"),
            P("page", None),
            P(None, "head"),
            P("head", None),
            P(),
            P(None, "head"),
            P(None, "head"),
            P("head", None),
            P(),
            P(),
            P(),
            P(),
            P(),
        ),
        out_specs=P("page"),
        check_vma=False,
    )
```

time: 1020 us -> 115 us (0.11)
  waiting for transfers between devices: 487 us -> 26.7 us
  local copies, waits for them, and re-layouts: 264 us -> 7.56 us
  other arithmetic: 170 us -> 10.8 us
  blocking collectives: 62.7 us -> 31.9 us
  starting transfers between devices: 0.24 us -> 25.2 us
  matrix products: 20.4 us -> 2.86 us
  between operations: 14.4 us -> 0.18 us
    all_gather x4 -> x0, waiting for transfers between devices: 344 us -> none  [the longest x3 298 us: combined_all(): pieces = jax.tree.map(lambda part: lax.all_gather(part, axis), value)]
    dynamic_slice x76 -> x2, local copies, waits for them, and re-layouts: 190 us -> 0.68 us  [the longest x1 0.6 us: per_device(): lax.dynamic_slice_in_dim(doc_of_token.reshape(chips, 2, tok_dev), core, 1...]
    add x64 -> x4, other arithmetic: 151 us -> 0.02 us  [the longest x1 0.01 us: per_device(): tok_part + jnp.sum(jnp.where(mine, hidden_score[None, :], 0.0), axis=1)]
    psum x2 -> x0, waiting for transfers between devices: 141 us -> none  [the longest x1 71.5 us: per_device(): lax.psum(jnp.dot(context, out_weight, preferred_element_type=jnp.float32)...]
    unnamed x1 -> x0, blocking collectives: 62.7 us -> none
    slice x3 -> x0, local copies, waits for them, and re-layouts: 48.5 us -> none  [combined_all(): tail = jax.tree.map(lambda part: part[1:], pieces)]
    all_to_all x0 -> x4, waiting for transfers between devices: none -> 26.7 us  [the longest x1 9.47 us: per_device(): lax.all_to_all(projected.reshape(head_size, own, model), 'head', 0, 0, ti...]
    all_to_all x0 -> x4, starting transfers between devices: none -> 24.5 us  [the longest x1 8.6 us: per_device(): lax.all_to_all(projected.reshape(head_size, own, model), 'head', 0, 0, ti...]
  transfers between devices with their start and end apart: 6 -> 7, of which waited for: 6 -> 4; matrix products, arithmetic and copies ran while one was open for 1% -> 8% of each run, Pallas kernels for 0% -> 0%
where the time goes in v1:
time: 115 us; the launch traced here: 114 us
  blocking collectives  31.9 us (28%)
  waiting for transfers between devices  26.7 us (23%)
  starting transfers between devices  25.2 us (22%)
  other arithmetic  10.8 us (9%)
  Pallas kernels  9.26 us (8%)
  local copies, waits for them, and re-layouts  7.56 us (7%)
  matrix products  2.86 us (2%)
    all_to_all x1, blocking collectives, per_device(): lax.all_to_all(partials, 'page', 0, 0, axis_index_groups=chip_groups, til...  16.3 us
    psum x1, blocking collectives, per_device(): pooled = lax.psum(jnp.sum(arrived, axis=0), 'head')[:doc_dev]  15.6 us
    all_to_all x1, waiting for transfers between devices, per_device(): lax.all_to_all(projected.reshape(head_size, own, model), 'head', 0, 0, ti...  9.47 us
    all_to_all x1, starting transfers between devices, per_device(): lax.all_to_all(projected.reshape(head_size, own, model), 'head', 0, 0, ti...  8.6 us
    pallas_call x1, Pallas kernels, per_device(): pl.pallas_call(attention_kernel, out_shape=jax.ShapeDtypeStruct((chips, 1...  8.08 us
    all_to_all x1, waiting for transfers between devices, per_device(): arrived = lax.all_to_all(doc_sums, 'page', 0, 0, tiled=True)  7.15 us
    all_to_all x1, starting transfers between devices, per_device(): lax.all_to_all(copies, 'page', 0, 0, axis_index_groups=chip_groups, tiled...  7.03 us
    all_to_all x1, waiting for transfers between devices, per_device(): lax.all_to_all(spread, 'head', 0, 0, tiled=True).reshape(tok_dev, model)  6.38 us
  transfers between devices with their start and end apart: 7, of which 4 were waited for; matrix products, arithmetic and copies ran while one was open for 8% of the time, Pallas kernels for 0%

profile of v1, /device:TPU:32, one launch (start us, length us, event | category | flops | bytes accessed | tf_op | source)
XLA Modules:
  0.0 114.4 jit_solution(334445209937466085)
XLA Ops:
  0.0 1.3 %fusion.4 = f32[64]{0:T(128)S(1)} fusion(bf16[64,2048]{1,0:T(8,128)(2,1)} %param.17), kind=kLoop, calls=%fused_computation.12 | loop fusion | flops 393152 | bytes 262400 | tf_op jit(solution)/shard_map/reduce_sum | solution.py:16
  1.3 1.7 %convolution_convert_fusion = bf16[64,256]{1,0:T(8,128)(2,1)S(1)} fusion(bf16[2048,256]{1,0:T(8,128)(2,1)} %param.19, bf16[64,2048]{1,0:T(8,128)(2,1)} %param.17, f32[2048]{0:T(1024)} %param.18, f32[64]{0:T(128)S(1)} %add_rsqrt_fusion.1), kind=kOutput, calls=%fused_computation.6 | convolution fusion | flops 67649536 | bytes 1351936 | tf_op jit(solution)/shard_map/dot_general | solution.py:173
  3.0 0.8 broadcast_in_dim.66
  3.8 7.0 %all-to-all-start = ((bf16[16,64,256]{2,1,0:T(8,128)(2,1)}), bf16[16,64,256]{2,1,0:T(8,128)(2,1)S(1)}, u32[]{:S(2)}, u32[]{:S(2)}) async-start(bf16[16,64,256]{2,1,0:T(8,128)(2,1)} %broadcast_in_dim.66), calls=%async_computation | async-start | bytes 1048576 | tf_op jit(solution)/shard_map/all_to_all | solution.py:175
  10.9 0.1 collective-permute-start
  11.0 0.5 collective-permute-start.1
  11.5 0.1 collective-permute-start.2
  11.6 0.1 pad_add_fusion.1
  11.7 0.2 select_reduce_fusion.4
  11.9 0.5 copy-done.10
  12.4 0.7 select_reduce_fusion.3
  13.1 0.8 reshape.202
  13.9 0.6 dynamic-slice_reduce_fusion
  14.5 0.8 eq.96
  15.2 0.7 and_select_fusion.2
  15.9 1.5 %select_reduce_fusion.1.tok_query = s32[4,256]{1,0:T(4,128)} fusion(s32[256]{0:T(256)} %param.31, s32[4,256]{1,0:T(4,128)S(1)} %eq.96), kind=kLoop, calls=%fused_computation.8 | loop fusion | flops 785408 | bytes 9216 | tf_op jit(solution)/shard_map/reduce_sum | solution.py:179
  17.4 0.5 pad_add_fusion.page_info
  17.9 0.8 copy.22.bias_table
  18.7 0.0 collective-permute-done.2.buckets_b
  18.7 3.7 %all-to-all-done.queries = bf16[16,64,256]{2,1,0:T(8,128)(2,1)S(1)} async-done(((bf16[16,64,256]{2,1,0:T(8,128)(2,1)}), bf16[16,64,256]{2,1,0:T(8,128)(2,1)S(1)}, u32[]{:S(2)}, u32[]{:S(2)}) %all-to-all-start) | async-done | bytes 524320 | tf_op jit(solution)/shard_map/all_to_all | solution.py:175
  22.4 0.7 copy-done.4
  23.1 0.6 copy-done.5
  23.7 8.1 %attention.1 = bf16[16,144,128]{2,1,0:T(8,128)(2,1)S(1)} custom-call(s32[2,4]{1,0:T(2,128)S(1)} %copy-done.5, bf16[16,64,256]{2,1,0:T(8,128)(2,1)S(1)} %all-to-all-done.queries, bf16[2,128,256]{2,1,0:T(8,128)(2,1)S(1)} %copy-done.2, bf16[2,128,256]{2,1,0:T(8,128)(2,1)S(1)} %collective-permute-done.keys_b, bf16[2,128,256]{2,1,0:T(8,128)(2,1)S(1)} %copy-done.3, ...), custom_call_target="tpu_custom_call" | custom-call | tf_op jit(solution)/shard_map/attention/pallas_call | solution.py:194
  31.8 0.0 copy-start.8
  31.8 0.0 copy-start.7
  31.8 0.0 copy-start.9
  31.8 16.3 %all_to_all.29.parts = bf16[16,144,128]{2,1,0:T(8,128)(2,1)S(1)} all-to-all(bf16[16,144,128]{2,1,0:T(8,128)(2,1)S(1)} %attention.1), channel_id=1, replica_groups={{0,2,4,6,8,10,12,14,16,18,20,22,24,26,28,30},{1,3,5,7,9,11,13,15,17,19,..., dimensions={0} | all-to-all | bytes 1179648 | tf_op jit(solution)/shard_map/all_to_all | solution.py:208
  48.1 1.2 %combine.1 = bf16[64,2048]{1,0:T(8,128)(2,1)} custom-call(bf16[16,144,128]{2,1,0:T(8,128)(2,1)S(1)} %all_to_all.29.parts, bf16[256,2048]{1,0:T(8,128)(2,1)S(1)} %copy-done.1), custom_call_target="tpu_custom_call" | custom-call | tf_op jit(solution)/shard_map/combine/pallas_call | solution.py:209
  49.3 8.6 %all-to-all-start.2 = ((bf16[8,8,2048]{2,1,0:T(8,128)(2,1)}), bf16[8,8,2048]{2,1,0:T(8,128)(2,1)S(1)}, u32[]{:S(2)}, u32[]{:S(2)}) async-start(bf16[8,8,2048]{2,1,0:T(8,128)(2,1)} %bitcast.2), calls=%async_computation.2 | async-start | bytes 524288 | tf_op jit(solution)/shard_map/all_to_all | solution.py:219
  57.9 0.1 dynamic_slice.9
  58.0 9.5 %all-to-all-done.2 = bf16[8,8,2048]{2,1,0:T(8,128)(2,1)S(1)} async-done(((bf16[8,8,2048]{2,1,0:T(8,128)(2,1)}), bf16[8,8,2048]{2,1,0:T(8,128)(2,1)S(1)}, u32[]{:S(2)}, u32[]{:S(2)}) %all-to-all-start.2) | async-done | bytes 262176 | tf_op jit(solution)/shard_map/all_to_all | solution.py:219
  67.5 0.9 multiply_reduce_fusion.1
  68.5 0.8 multiply_convert_fusion
  69.3 0.7 broadcast_in_dim.104
  70.0 4.8 %all-to-all-start.3 = ((bf16[8,8,2048]{2,1,0:T(8,128)(2,1)}), bf16[8,8,2048]{2,1,0:T(8,128)(2,1)S(1)}, u32[]{:S(2)}, u32[]{:S(2)}) async-start(bf16[8,8,2048]{2,1,0:T(8,128)(2,1)} %broadcast_in_dim.104), calls=%async_computation.3 | async-start | bytes 524288 | tf_op jit(solution)/shard_map/all_to_all | solution.py:225
  74.8 2.3 %multiply_reduce_fusion = f32[640]{0:T(1024)S(1)} fusion(bf16[640,2048]{1,0:T(8,128)(2,1)} %param.28, f32[2048]{0:T(1024)S(1)} %copy-done.7), kind=kLoop, calls=%fused_computation | loop fusion | flops 3931520 | bytes 2632192 | tf_op jit(solution)/shard_map/reduce_sum | solution.py:229
  77.2 0.1 select_reduce_fusion.2
  77.2 6.4 %all-to-all-done.3 = bf16[8,8,2048]{2,1,0:T(8,128)(2,1)S(1)} async-done(((bf16[8,8,2048]{2,1,0:T(8,128)(2,1)}), bf16[8,8,2048]{2,1,0:T(8,128)(2,1)S(1)}, u32[]{:S(2)}, u32[]{:S(2)}) %all-to-all-start.3) | async-done | bytes 262176 | tf_op jit(solution)/shard_map/all_to_all | solution.py:225
  83.6 0.5 fusion.19
  84.2 1.2 %copy-done.6 = bf16[2048,640]{1,0:T(8,128)(2,1)S(1)} copy-done((bf16[2048,640]{1,0:T(8,128)(2,1)S(1)}, bf16[2048,640]{1,0:T(8,128)(2,1)}, u32[]{:S(2)}) %copy-start.6) | copy-done | bytes 2621464
  85.4 0.6 fusion.3
  86.0 0.8 select_reduce_fusion
  86.8 4.1 %all-to-all-start.4 = ((f32[32,1,128]{2,1,0:T(1,128)}), f32[32,1,128]{2,1,0:T(1,128)S(1)}, u32[]{:S(2)}, u32[]{:S(2)}) async-start(f32[32,1,128]{2,1,0:T(1,128)} %bitcast.5), calls=%async_computation.4 | async-start | bytes 32768 | tf_op jit(solution)/shard_map/all_to_all | solution.py:242
  90.9 0.2 convert_reduce_fusion.1
  91.1 7.2 %all-to-all-done.4 = f32[32,1,128]{2,1,0:T(1,128)S(1)} async-done(((f32[32,1,128]{2,1,0:T(1,128)}), f32[32,1,128]{2,1,0:T(1,128)S(1)}, u32[]{:S(2)}, u32[]{:S(2)}) %all-to-all-start.4) | async-done | bytes 16416 | tf_op jit(solution)/shard_map/all_to_all | solution.py:242
  98.3 0.1 reduce_sum.134
  98.3 15.6 %psum.7 = f32[128]{0:T(128)S(1)} all-reduce(f32[128]{0:T(128)S(1)} %reduce_sum.134), channel_id=1, replica_groups=mesh['head'=8,'page'=32] {'head'}, use_global_device_ids=true, to_apply=%region_12.13 | all-reduce | flops 128 | bytes 1024 | tf_op jit(solution)/shard_map/psum | solution.py:243
  113.9 0.5 slice_divide_fusion
  (30 shorter events, 0.1 us)
Async XLA Ops:
  0.0 83.6 %copy-start = (bf16[2048,640]{1,0:T(8,128)(2,1)S(1)}, bf16[2048,640]{1,0:T(8,128)(2,1)}, u32[]{:S(2)}) copy-start(bf16[2048,640]{1,0:T(8,128)(2,1)} %param.26) | copy-start | bytes 7864324
  0.0 10.9 %copy-start.2 = (bf16[2,128,256]{2,1,0:T(8,128)(2,1)S(1)}, bf16[2,128,256]{2,1,0:T(8,128)(2,1)}, u32[]{:S(2)}) copy-start(bf16[2,128,256]{2,1,0:T(8,128)(2,1)} %keys_a.1) | copy-start | bytes 393220
  0.0 11.0 %copy-start.3 = (bf16[2,128,256]{2,1,0:T(8,128)(2,1)S(1)}, bf16[2,128,256]{2,1,0:T(8,128)(2,1)}, u32[]{:S(2)}) copy-start(bf16[2,128,256]{2,1,0:T(8,128)(2,1)} %values_a.1) | copy-start | bytes 393220
  0.0 11.7 %copy-start.11 = (s32[64]{0:T(128)S(1)}, s32[64]{0:T(128)}, u32[]{:S(2)}) copy-start(s32[64]{0:T(128)} %param.33) | copy-start | bytes 772
  0.0 12.4 %copy-start.12 = (s32[8]{0:T(128)S(1)}, s32[8]{0:T(128)}, u32[]{:S(2)}) copy-start(s32[8]{0:T(128)} %param.30) | copy-start | bytes 100
  3.8 18.6 %all-to-all-start = ((bf16[16,64,256]{2,1,0:T(8,128)(2,1)}), bf16[16,64,256]{2,1,0:T(8,128)(2,1)S(1)}, u32[]{:S(2)}, u32[]{:S(2)}) async-start(bf16[16,64,256]{2,1,0:T(8,128)(2,1)} %broadcast_in_dim.66), calls=%async_computation | async-start | bytes 1048576 | tf_op jit(solution)/shard_map/all_to_all | solution.py:175
  10.9 7.8 %collective-permute-start = (bf16[2,128,256]{2,1,0:T(8,128)(2,1)S(1)}, bf16[2,128,256]{2,1,0:T(8,128)(2,1)S(1)}, u32[]{:S(2)}, u32[]{:S(2)}) collective-permute-start(bf16[2,128,256]{2,1,0:T(8,128)(2,1)S(1)} %copy-done.2), channel_id=1, source_target_pairs={{0,1},{1,0},{2,3},{3,2},{4,5},{5,4},{6,7},{7,6},{8,9},{9,8},{10,11... | collective-permute-start | bytes 393224 | tf_op jit(solution)/shard_map/ppermute | solution.py:168
  11.0 7.7 %collective-permute-start.1 = (bf16[2,128,256]{2,1,0:T(8,128)(2,1)S(1)}, bf16[2,128,256]{2,1,0:T(8,128)(2,1)}, u32[]{:S(2)}, u32[]{:S(2)}) collective-permute-start(bf16[2,128,256]{2,1,0:T(8,128)(2,1)S(1)} %copy-done.3), channel_id=1, source_target_pairs={{0,1},{1,0},{2,3},{3,2},{4,5},{5,4},{6,7},{7,6},{8,9},{9,8},{10,11... | collective-permute-start | bytes 393224 | tf_op jit(solution)/shard_map/ppermute | solution.py:169
  11.5 7.2 %collective-permute-start.2 = (s32[2,128]{1,0:T(2,128)}, s32[2,128]{1,0:T(2,128)}, u32[]{:S(2)}, u32[]{:S(2)}) collective-permute-start(s32[2,128]{1,0:T(2,128)} %buckets_a.1), channel_id=1, source_target_pairs={{0,1},{1,0},{2,3},{3,2},{4,5},{5,4},{6,7},{7,6},{8,9},{9,8},{10,11... | collective-permute-start | bytes 3080 | tf_op jit(solution)/shard_map/ppermute | solution.py:170
  11.8 0.5 copy-start.10
  22.4 0.7 copy-start.4
  23.1 0.6 copy-start.5
  23.7 24.4 %copy-start.1 = (bf16[256,2048]{1,0:T(8,128)(2,1)S(1)}, bf16[256,2048]{1,0:T(8,128)(2,1)}, u32[]{:S(2)}) copy-start(bf16[256,2048]{1,0:T(8,128)(2,1)} %out_weight.1) | copy-start | bytes 3145732
  31.8 26.1 %copy-start.8 = (s32[2048]{0:T(1024)S(1)}, s32[2048]{0:T(1024)}, u32[]{:S(2)}) copy-start(s32[2048]{0:T(1024)} %param.32) | copy-start | bytes 24580
  31.8 35.7 %copy-start.7 = (f32[2048]{0:T(1024)S(1)}, f32[2048]{0:T(1024)}, u32[]{:S(2)}) copy-start(f32[2048]{0:T(1024)} %param.29) | copy-start | bytes 24580
  31.8 36.7 %copy-start.9 = (f32[2048]{0:T(1024)S(1)}, f32[2048]{0:T(1024)}, u32[]{:S(2)}) copy-start(f32[2048]{0:T(1024)} %param.25) | copy-start | bytes 24580
  49.3 18.2 %all-to-all-start.2 = ((bf16[8,8,2048]{2,1,0:T(8,128)(2,1)}), bf16[8,8,2048]{2,1,0:T(8,128)(2,1)S(1)}, u32[]{:S(2)}, u32[]{:S(2)}) async-start(bf16[8,8,2048]{2,1,0:T(8,128)(2,1)} %bitcast.2), calls=%async_computation.2 | async-start | bytes 524288 | tf_op jit(solution)/shard_map/all_to_all | solution.py:219
  70.0 13.6 %all-to-all-start.3 = ((bf16[8,8,2048]{2,1,0:T(8,128)(2,1)}), bf16[8,8,2048]{2,1,0:T(8,128)(2,1)S(1)}, u32[]{:S(2)}, u32[]{:S(2)}) async-start(bf16[8,8,2048]{2,1,0:T(8,128)(2,1)} %broadcast_in_dim.104), calls=%async_computation.3 | async-start | bytes 524288 | tf_op jit(solution)/shard_map/all_to_all | solution.py:225
  83.6 1.7 %copy-start.6 = (bf16[2048,640]{1,0:T(8,128)(2,1)S(1)}, bf16[2048,640]{1,0:T(8,128)(2,1)}, u32[]{:S(2)}) copy-start(bf16[2048,640]{1,0:T(8,128)(2,1)} %param.27) | copy-start | bytes 7864324
  86.8 11.5 %all-to-all-start.4 = ((f32[32,1,128]{2,1,0:T(1,128)}), f32[32,1,128]{2,1,0:T(1,128)S(1)}, u32[]{:S(2)}, u32[]{:S(2)}) async-start(f32[32,1,128]{2,1,0:T(1,128)} %bitcast.5), calls=%async_computation.4 | async-start | bytes 32768 | tf_op jit(solution)/shard_map/all_to_all | solution.py:242

commit v2 on v1

v2 whole, which is shorter than its diff:
```python
import jax
import jax.numpy as jnp
from jax import lax
from jax.experimental import pallas as pl
from jax.experimental.pallas import tpu as pltpu
from jax.sharding import PartitionSpec as P

NQ = 8
MASKED = -1e30
BF = jnp.bfloat16
F32 = jnp.float32


def rms_scale(values, gain):
    values = values.astype(F32)
    return values * lax.rsqrt(jnp.mean(values * values, axis=-1, keepdims=True) + 1e-06) * gain


def split_three(value):
    first = value.astype(BF)
    rest = value - first.astype(F32)
    second = rest.astype(BF)
    third = (rest - second.astype(F32)).astype(BF)
    return first, second, third


def project_kernel(states, gain, weight, out, states_here, gain_here, weight_here, arrivals):
    pairs = ((states, states_here), (gain, gain_here), (weight, weight_here))
    copies = [pltpu.make_async_copy(there, here, arrivals.at[i]) for i, (there, here) in enumerate(pairs)]
    for copy in copies:
        copy.start()
    copies[0].wait()
    copies[1].wait()
    normed = rms_scale(states_here[...], gain_here[...]).astype(BF)
    copies[2].wait()
    queries = jnp.dot(normed, weight_here[...], preferred_element_type=F32).astype(BF)
    for chip in range(out.shape[0]):
        out[chip] = queries


def prepare_kernel(rank, page_table, query_lengths, k0, k1, k2, k3, v0, v1, v2, v3, b01, b23, bias_table, doc_query,
                   doc_rows, keys_aug, values_t, extra, info, held_caches, arrivals):
    pages, page_len, width = k0.shape
    heads = bias_table.shape[0]
    depth = width // heads
    bucket_count = bias_table.shape[1]
    slot_count = page_table.shape[0]
    max_pages = slot_count // NQ
    tokens = extra.shape[0]
    tok_dev = doc_rows.shape[1] // 2
    row_chips = 4
    copies = [
        pltpu.make_async_copy(cache, held_caches.at[i], arrivals.at[i])
        for i, cache in enumerate((k0, k1, k2, k3, v0, v1, v2, v3))
    ]
    for copy in copies:
        copy.start()
    core = rank[0] % 2
    chip = rank[0] // 2
    pair = chip - chip % 2
    base = (chip // row_chips * row_chips + chip % 2) * 2 * pages
    held = 4 * pages
    for s in range(slot_count):
        place = page_table[s] - base
        near = (place >= 0) & (place < 2 * pages)
        far = (place >= 4 * pages) & (place < 6 * pages)
        place = jnp.where(near, place, jnp.where(far, place - 2 * pages, held))
        info[0, place] = s // max_pages
        info[1, place] = query_lengths[s // max_pages] - (s % max_pages) * page_len
    doc_count = doc_query.shape[1]
    left = lax.broadcasted_iota(jnp.int32, (1, 128), 1) < tok_dev
    doc_id = lax.broadcasted_iota(jnp.int32, (doc_count, 128), 0)
    blocks = []
    for y in range(tokens // (2 * tok_dev)):
        two = doc_rows[pl.ds(y * row_chips + pair % row_chips, 2), :]
        turned = pltpu.roll(two, tok_dev, 1)
        row = jnp.where(
            left,
            jnp.where(core == 0, two[0:1], turned[0:1]),
            jnp.where(core == 0, turned[1:2], two[1:2]),
        )
        blocks.append((doc_id == row).astype(F32).astype(BF))
    member = jnp.concatenate(blocks, axis=1)
    asked = jnp.broadcast_to(doc_query[...].astype(F32), (128, doc_count)).astype(BF)
    tok_query = jnp.dot(asked, member, preferred_element_type=F32)
    mark = lax.broadcasted_iota(jnp.int32, (128, tokens), 0) % 64
    columns = jnp.where(
        mark < NQ,
        jnp.where(tok_query == mark.astype(F32), 0.0, MASKED),
        jnp.where(mark == NQ, MASKED, jnp.where(mark < NQ + 4, 1.0, 0.0)),
    )
    extra[...] = columns.T.astype(BF)
    low = lax.broadcasted_iota(jnp.int32, (1, 128), 1) < depth
    table = jnp.concatenate([bias_table[...], jnp.zeros((8 - heads, bucket_count), F32)], axis=0).T
    col = lax.broadcasted_iota(jnp.int32, (bucket_count, 128), 1) % 64
    spreads = []
    for h in range(heads):
        a, b, c = split_three(jnp.broadcast_to(table[:, h : h + 1], (bucket_count, 128)))
        third = jnp.where(col == NQ + 3, c.astype(F32), 0.0)
        spreads.append(
            jnp.where(col == NQ + 1, a.astype(F32), jnp.where(col == NQ + 2, b.astype(F32), third)).astype(BF)
        )
    spread = jnp.concatenate(spreads, axis=1)
    bucket_row = lax.broadcasted_iota(jnp.int32, (bucket_count, page_len), 0)
    slot = lax.broadcasted_iota(jnp.int32, (page_len, 128), 0)
    key_col = lax.broadcasted_iota(jnp.int32, (page_len, 128), 1) % 64
    mine = ((chip % row_chips // 2) * 2 + core) * pages
    for copy in copies:
        copy.wait()
    for part, (buckets, first) in enumerate(((b01, 0), (b01, pages), (b23, 0), (b23, pages))):
        for page in range(pages):
            place = (mine ^ (part * pages)) + page
            span = pl.ds((part * pages + page) * page_len, page_len)
            bucket = buckets[first + page : first + page + 1, :]
            onehot = (jnp.broadcast_to(bucket, bucket_row.shape) == bucket_row).astype(F32).astype(BF)
            bias = lax.dot_general(onehot, spread, (((0,), (0,)), ((), ())), preferred_element_type=F32)
            holder = jnp.where(slot < info[1, place], info[0, place], NQ)
            marks = (key_col == holder).astype(F32)
            key = held_caches[part, page].astype(F32)
            for h in range(heads):
                keep = low if h % 2 == 0 else jnp.logical_not(low)
                half = key[:, (h // 2) * 128 : (h // 2 + 1) * 128]
                keys_aug[h, span, :] = jnp.where(keep, half, bias[:, h * 128 : (h + 1) * 128] + marks).astype(BF)
            values_t[:, span] = held_caches[4 + part, page].astype(F32).T.astype(BF)


def attention_kernel(queries, keys_aug, values_t, extra, out, rows_aug):
    chips, tok_dev, width = queries.shape
    heads = keys_aug.shape[0]
    depth = width // heads
    low = lax.broadcasted_iota(jnp.int32, (1, 128), 1) < depth
    left = lax.broadcasted_iota(jnp.int32, (1, 128), 1) < tok_dev
    rows = queries[...].reshape(chips * tok_dev, width)
    for h in range(heads):
        half = rows[:, (h // 2) * 128 : (h // 2 + 1) * 128].astype(F32)
        keep = low if h % 2 == 0 else jnp.logical_not(low)
        rows_aug[h] = jnp.where(keep, half, extra[...].astype(F32)).astype(BF)
    sums = []
    logs = []
    for h in range(heads):
        scores = lax.dot_general(
            keys_aug[h], rows_aug[h], (((1,), (1,)), ((), ())), preferred_element_type=F32
        )
        top = jnp.max(scores, axis=0, keepdims=True)
        weights = jnp.exp(scores - top)
        total = jnp.sum(weights, axis=0, keepdims=True)
        summed = jnp.dot(
            values_t[h * depth : (h + 1) * depth, :], weights.astype(BF), preferred_element_type=F32
        )
        sums.append(summed / total)
        logs.append(top + jnp.log(total))
    for duo in range(chips // 2):
        lanes = slice(duo * 128, (duo + 1) * 128)
        pad = [jnp.zeros((6, 128), F32)]
        upper = jnp.concatenate([sums[0][:, lanes], sums[1][:, lanes]], axis=0)
        lower = jnp.concatenate([sums[2][:, lanes], sums[3][:, lanes]], axis=0)
        stat_upper = jnp.concatenate([logs[0][:, lanes], logs[1][:, lanes]] + pad, axis=0)
        stat_lower = jnp.concatenate([logs[2][:, lanes], logs[3][:, lanes]] + pad, axis=0)
        block = (
            jnp.where(left, upper, pltpu.roll(lower, tok_dev, 1)),
            jnp.where(left, pltpu.roll(upper, tok_dev, 1), lower),
        )
        stat = (
            jnp.where(left, stat_upper, pltpu.roll(stat_lower, tok_dev, 1)),
            jnp.where(left, pltpu.roll(stat_upper, tok_dev, 1), stat_lower),
        )
        for which in range(2):
            a, b, c = split_three(stat[which])
            packed = [a[0:2].astype(F32), b[0:2].astype(F32), c[0:2].astype(F32), jnp.zeros((2, 128), F32)]
            out[duo * 2 + which, 0:128, :] = block[which].astype(BF)
            out[duo * 2 + which, 128:136, :] = jnp.concatenate(packed, axis=0).astype(BF)


def combine_kernel(parts, out_weight, out):
    chips = parts.shape[0]
    logs = []
    for chip in range(chips):
        stat = parts[chip, 128:136, :].astype(F32)
        logs.append(stat[0:2] + stat[2:4] + stat[4:6])
    top = logs[0]
    for chip in range(1, chips):
        top = jnp.maximum(top, logs[chip])
    scales = [jnp.exp(log - top) for log in logs]
    whole = scales[0]
    for chip in range(1, chips):
        whole = whole + scales[chip]
    sums = [jnp.zeros((64, 128), F32), jnp.zeros((64, 128), F32)]
    for chip in range(chips):
        share = scales[chip] / whole
        for r in range(2):
            sums[r] = sums[r] + share[r : r + 1] * parts[chip, r * 64 : (r + 1) * 64, :].astype(F32)
    joined = jnp.concatenate(sums, axis=0).T
    context = jnp.concatenate([joined[0:64], joined[64:128]], axis=1).astype(BF)
    out[...] = jnp.dot(context, out_weight[...], preferred_element_type=F32).astype(BF)


def norm_kernel(terms, states, gain, score_vector, out, score):
    hidden = states[...].astype(F32)
    for source in range(terms.shape[0]):
        hidden = hidden + terms[source].astype(F32)
    normed = rms_scale(hidden, gain[...]).astype(BF)
    for target in range(out.shape[0]):
        out[target] = normed
    score[...] = jnp.broadcast_to(jnp.sum(hidden * score_vector[...], axis=-1, keepdims=True), score.shape)


def feed_kernel(rows, gate_weight, up_weight, down_score, own_score, own_docs, out, gate, upper):
    step = pl.program_id(0)

    @pl.when(step == 0)
    def _():
        gate[...] = jnp.zeros_like(gate)
        upper[...] = jnp.zeros_like(upper)

    part = rows[...]
    gate[...] += jnp.dot(part, gate_weight[...], preferred_element_type=F32)
    upper[...] += jnp.dot(part, up_weight[...], preferred_element_type=F32)

    @pl.when(step == pl.num_programs(0) - 1)
    def _():
        middle = (jax.nn.gelu(gate[...], approximate=True) * upper[...]).astype(BF).astype(F32)
        tok_score = jnp.sum(middle * down_score[...], axis=-1, keepdims=True) + own_score[...]
        docs = own_docs[...]
        doc_dev = 256 // out.shape[0]
        lane = lax.broadcasted_iota(jnp.int32, (docs.shape[0], 128), 1)
        holder = (docs // doc_dev == lane).astype(F32).astype(BF)
        placed = jnp.where(docs % doc_dev == lane, tok_score, 0.0)
        sums = jnp.zeros((128, 128), F32)
        for piece in split_three(placed):
            sums += lax.dot_general(holder, piece, (((0,), (0,)), ((), ())), preferred_element_type=F32)
        out[...] = sums[0 : out.shape[0]]


def vmem():
    return pl.BlockSpec(memory_space=pltpu.VMEM)


def smem():
    return pl.BlockSpec(memory_space=pltpu.SMEM)


def hbm():
    return pl.BlockSpec(memory_space=pltpu.HBM)


def anywhere():
    return pl.BlockSpec(memory_space=pl.ANY)


def call(kernel, name, shapes, specs, scratch=()):
    single = not isinstance(shapes, (list, tuple))
    return pl.pallas_call(
        kernel,
        out_shape=shapes,
        in_specs=specs,
        out_specs=vmem() if single else [vmem()] * len(shapes),
        scratch_shapes=list(scratch),
        compiler_params=pltpu.CompilerParams(vmem_limit_bytes=40 << 20),
        name=name,
    )


def per_device(
    doc_states,
    gain_attn,
    query_weight,
    cache_keys,
    cache_values,
    rel_bucket,
    bias_table,
    out_weight,
    gain_ffn,
    wi_gate,
    wi_up,
    wo_ffn,
    score_vector,
    query_lengths,
    doc_query,
    doc_of_token,
    page_table,
):
    shape = jax.ShapeDtypeStruct
    tok_dev, model = doc_states.shape
    local_pages, page_len, local_width = cache_keys.shape
    local_heads = bias_table.shape[1]
    page_size = lax.axis_size("page")
    head_size = lax.axis_size("head")
    page_rank = lax.axis_index("page")
    head_rank = lax.axis_index("head")
    group = page_size // 4
    groups = [
        [y * 8 + (x + side) * 2 + core for y in range(4) for side in range(2)] for x in (0, 2) for core in range(2)
    ]
    core_swap = [(i, i ^ 1) for i in range(page_size)]
    side_swap = [(i, i ^ 4) for i in range(page_size)]

    def swap(value, pairs):
        return lax.ppermute(value, "page", pairs)

    keys_side = swap(cache_keys, side_swap)
    values_side = swap(cache_values, side_swap)
    keys_core = swap(cache_keys, core_swap)
    values_core = swap(cache_values, core_swap)
    bucket_pair = jnp.concatenate([rel_bucket, swap(rel_bucket, core_swap)])
    bucket_side = swap(bucket_pair, side_swap)
    keys_far = swap(keys_side, core_swap)
    values_far = swap(values_side, core_swap)

    copies = call(
        project_kernel, "project", shape((group, tok_dev, local_width), BF), [hbm()] * 3,
        [
            pltpu.VMEM((tok_dev, model), BF),
            pltpu.VMEM((1, model), F32),
            pltpu.VMEM((model, local_width), BF),
            pltpu.SemaphoreType.DMA((3,)),
        ],
    )(doc_states, gain_attn.reshape(1, model), query_weight)
    gathered = lax.all_to_all(copies, "page", 0, 0, axis_index_groups=groups, tiled=True)

    key_count = 4 * local_pages * page_len
    keys_aug, values_t, extra = call(
        prepare_kernel,
        "prepare",
        [
            shape((local_heads, key_count, 128), BF),
            shape((local_width, key_count), BF),
            shape((group * tok_dev, 128), BF),
        ],
        [smem()] * 3 + [hbm()] + [anywhere()] * 3 + [hbm()] + [anywhere()] * 3 + [vmem()] * 5,
        [
            pltpu.SMEM((2, 4 * local_pages + 1), jnp.int32),
            pltpu.VMEM((8, local_pages, page_len, local_width), BF),
            pltpu.SemaphoreType.DMA((8,)),
        ],
    )(
        page_rank.reshape(1),
        page_table,
        query_lengths,
        cache_keys,
        keys_core,
        keys_side,
        keys_far,
        cache_values,
        values_core,
        values_side,
        values_far,
        bucket_pair,
        bucket_side,
        bias_table.T,
        doc_query.reshape(1, -1),
        doc_of_token.reshape(-1, 2 * tok_dev),
    )
    partials = call(
        attention_kernel,
        "attention",
        shape((group, 136, 128), BF),
        [vmem()] * 4,
        [pltpu.VMEM((local_heads, group * tok_dev, 128), BF)],
    )(gathered, keys_aug, values_t, extra)
    returned = lax.all_to_all(partials, "page", 0, 0, axis_index_groups=groups, tiled=True)
    projected = call(combine_kernel, "combine", shape((tok_dev, model), BF), [vmem()] * 2)(returned, out_weight)

    own = tok_dev // head_size
    terms = lax.all_to_all(projected.reshape(head_size, own, model), "head", 0, 0, tiled=True)
    own_states = lax.dynamic_slice_in_dim(doc_states, head_rank * own, own, 0)
    spread, hidden_score = call(
        norm_kernel,
        "norm",
        [shape((head_size, own, model), BF), shape((own, 128), F32)],
        [vmem()] * 4,
    )(terms, own_states, gain_ffn.reshape(1, model), score_vector.reshape(1, model))
    rows = lax.all_to_all(spread, "head", 0, 0, tiled=True).reshape(tok_dev, model)
    down_score = jnp.sum(wo_ffn.astype(F32) * score_vector, axis=-1)
    token = jnp.arange(tok_dev, dtype=jnp.int32)[:, None]
    own_score = jnp.where(token // own == head_rank, jnp.tile(hidden_score[:, :1], (head_size, 1)), 0.0)
    own_docs = lax.dynamic_slice_in_dim(doc_of_token, page_rank * tok_dev, tok_dev, 0)[:, None]
    doc_dev = doc_query.shape[0] // page_size
    hidden_units = wi_gate.shape[1]
    steps = 4
    doc_sums = pl.pallas_call(
        feed_kernel,
        out_shape=shape((page_size, 128), F32),
        grid=(steps,),
        in_specs=[
            pl.BlockSpec((tok_dev, model // steps), lambda i: (0, i)),
            pl.BlockSpec((model // steps, hidden_units), lambda i: (i, 0)),
            pl.BlockSpec((model // steps, hidden_units), lambda i: (i, 0)),
            pl.BlockSpec((1, hidden_units), lambda i: (0, 0)),
            pl.BlockSpec((tok_dev, 1), lambda i: (0, 0)),
            pl.BlockSpec((tok_dev, 1), lambda i: (0, 0)),
        ],
        out_specs=pl.BlockSpec((page_size, 128), lambda i: (0, 0)),
        scratch_shapes=[pltpu.VMEM((tok_dev, hidden_units), F32)] * 2,
        compiler_params=pltpu.CompilerParams(vmem_limit_bytes=40 << 20),
        name="feed",
    )(rows, wi_gate, wi_up, down_score.reshape(1, -1), own_score, own_docs)
    doc_sums = doc_sums.reshape(page_size, 1, 128)
    arrived = lax.all_to_all(doc_sums, "page", 0, 0, tiled=True)
    pooled = jnp.broadcast_to(jnp.sum(arrived, axis=0), (head_size, 1, 128))
    pooled = jnp.sum(lax.all_to_all(pooled, "head", 0, 0, tiled=True), axis=(0, 1))[:doc_dev]
    mine_docs = page_rank * doc_dev + jnp.arange(doc_dev, dtype=jnp.int32)
    counts = jnp.sum((doc_of_token[:, None] == mine_docs[None, :]).astype(F32), axis=0)
    return pooled / counts


def solution(mesh):
    return jax.shard_map(
        per_device,
        mesh=mesh,
        in_specs=(
            P("page", None),
            P(),
            P(None, "head"),
            P("page", None, "head"),
            P("page", None, "head"),
            P("page", None),
            P(None, "head"),
            P("head", None),
            P(),
            P(None, "head"),
            P(None, "head"),
            P("head", None),
            P(),
            P(),
            P(),
            P(),
            P(),
        ),
        out_specs=P("page"),
        check_vma=False,
    )
```

time: 115 us -> 112 us (0.974); the launches traced: 114 us -> 110 us
  blocking collectives: 31.9 us -> 13.1 us
  starting transfers between devices: 25.2 us -> 36.2 us
  other arithmetic: 10.8 us -> 3.82 us
  local copies, waits for them, and re-layouts: 7.56 us -> 12.7 us
  waiting for transfers between devices: 26.7 us -> 31.1 us
  Pallas kernels: 9.26 us -> 12.9 us
  matrix products: 2.86 us -> 0 us
    psum x1 -> x0, blocking collectives: 15.6 us -> none  [per_device(): pooled = lax.psum(jnp.sum(arrived, axis=0), 'head')[:doc_dev]]
    unnamed x27 -> x32, local copies, waits for them, and re-layouts: 3.79 us -> 11 us
    ppermute x3 -> x8, starting transfers between devices: 0.69 us -> 7.37 us  [swap(): return lax.ppermute(value, 'page', pairs)]
    reduce_sum x9 -> x2, other arithmetic: 5.54 us -> 0.07 us  [the longest x1 0.05 us: per_device(): pooled = jnp.broadcast_to(jnp.sum(arrived, axis=0), (head_size, 1, 128))]
    pallas_call x2 -> x6, Pallas kernels: 9.26 us -> 12.9 us  [the longest x1 3.86 us: per_device(): call(attention_kernel, 'attention', shape((group, 136, 128), BF), [vmem()...]
    ppermute x3 -> x8, waiting for transfers between devices: 0.01 us -> 3.63 us  [swap(): return lax.ppermute(value, 'page', pairs)]
    all_to_all x1 -> x2, starting transfers between devices: 7.03 us -> 10.4 us  [the longest x1 5.41 us: per_device(): lax.all_to_all(copies, 'page', 0, 0, axis_index_groups=groups, tiled=True)]
    all_to_all x1, blocking collectives: 16.3 us -> 13.1 us  [per_device(): lax.all_to_all(partials, 'page', 0, 0, axis_index_groups=groups, tiled=True)]
  transfers between devices with their start and end apart: 7 -> 13, of which waited for: 4 -> 6; matrix products, arithmetic and copies ran while one was open for 8% -> 4% of each run, Pallas kernels for 0% -> 4%
where the time goes in v2:
time: 112 us; the launch traced here: 110 us
  starting transfers between devices  36.2 us (32%)
  waiting for transfers between devices  31.1 us (28%)
  blocking collectives  13.1 us (12%)
  Pallas kernels  12.9 us (12%)
  local copies, waits for them, and re-layouts  12.7 us (11%)
  other arithmetic  3.82 us (3%)
    all_to_all x1, blocking collectives, per_device(): lax.all_to_all(partials, 'page', 0, 0, axis_index_groups=groups, tiled=True)  13.1 us
    unnamed x32, local copies, waits for them, and re-layouts  11 us
    all_to_all x1, starting transfers between devices, per_device(): lax.all_to_all(projected.reshape(head_size, own, model), 'head', 0, 0, ti...  8.57 us
    all_to_all x1, waiting for transfers between devices, per_device(): lax.all_to_all(projected.reshape(head_size, own, model), 'head', 0, 0, ti...  8.27 us
    ppermute x8, starting transfers between devices, swap(): return lax.ppermute(value, 'page', pairs)  7.37 us
    all_to_all x1, waiting for transfers between devices, per_device(): arrived = lax.all_to_all(doc_sums, 'page', 0, 0, tiled=True)  7.34 us
    all_to_all x1, waiting for transfers between devices, per_device(): lax.all_to_all(pooled, 'head', 0, 0, tiled=True)  6.04 us
    all_to_all x1, waiting for transfers between devices, per_device(): lax.all_to_all(spread, 'head', 0, 0, tiled=True).reshape(tok_dev, model)  5.87 us
  transfers between devices with their start and end apart: 13, of which 6 were waited for; matrix products, arithmetic and copies ran while one was open for 4% of the time, Pallas kernels for 4%

profile of v2, /device:TPU:32, one launch (start us, length us, event | category | flops | bytes accessed | tf_op | source)
XLA Modules:
  0.0 110.1 jit_solution(1741712697710639431)
XLA Ops:
  0.0 3.0 %collective-permute-start.1 = (bf16[2,128,256]{2,1,0:T(8,128)(2,1)}, bf16[2,128,256]{2,1,0:T(8,128)(2,1)S(1)}, u32[]{:S(2)}, u32[]{:S(2)}) collective-permute-start(bf16[2,128,256]{2,1,0:T(8,128)(2,1)} %k0.1), channel_id=1, source_target_pairs={{0,4},{1,5},{2,6},{3,7},{4,0},{5,1},{6,2},{7,3},{8,12},{9,13},{10,... | collective-permute-start | bytes 393224 | tf_op jit(solution)/shard_map/ppermute | solution.py:298
  3.0 0.5 collective-permute-start.4
  3.5 1.2 %copy-done.2 = bf16[2048,256]{1,0:T(8,128)(2,1)S(1)} copy-done((bf16[2048,256]{1,0:T(8,128)(2,1)S(1)}, bf16[2048,256]{1,0:T(8,128)(2,1)}, u32[]{:S(2)}) %copy-start.2) | copy-done | bytes 1048600
  4.8 0.9 copy-done.4
  5.7 0.7 copy-done.10
  6.4 1.3 %project.1 = bf16[8,64,256]{2,1,0:T(8,128)(2,1)} custom-call(bf16[64,2048]{1,0:T(8,128)(2,1)S(1)} %copy-done.4, f32[1,2048]{1,0:T(1,128)S(1)} %bitcast.18, bf16[2048,256]{1,0:T(8,128)(2,1)S(1)} %copy-done.2), custom_call_target="tpu_custom_call" | custom-call | tf_op jit(solution)/shard_map/project/pallas_call | solution.py:309
  7.7 5.4 %all-to-all-start = ((bf16[8,64,256]{2,1,0:T(8,128)(2,1)}), bf16[8,64,256]{2,1,0:T(8,128)(2,1)S(1)}, u32[]{:S(2)}, u32[]{:S(2)}) async-start(bf16[8,64,256]{2,1,0:T(8,128)(2,1)} %project.1), calls=%async_computation | async-start | bytes 524288 | tf_op jit(solution)/shard_map/all_to_all | solution.py:318
  13.1 0.5 collective-permute-start.3
  13.6 0.1 collective-permute-start.2
  13.7 0.4 collective-permute-start.5
  14.1 0.1 collective-permute-start.6
  14.2 1.3 %collective-permute-done.6 = s32[2,128]{1,0:T(2,128)S(1)} collective-permute-done((s32[2,128]{1,0:T(2,128)}, s32[2,128]{1,0:T(2,128)S(1)}, u32[]{:S(2)}, u32[]{:S(2)}) %collective-permute-start.6) | collective-permute-done | bytes 1056 | tf_op jit(solution)/shard_map/ppermute | solution.py:298
  15.5 0.7 pad_add_fusion.b01
  16.2 2.7 %collective-permute-start.7 = (s32[4,128]{1,0:T(4,128)S(1)}, s32[4,128]{1,0:T(4,128)S(1)}, u32[]{:S(2)}, u32[]{:S(2)}) collective-permute-start(s32[4,128]{1,0:T(4,128)S(1)} %pad_add_fusion.b01), channel_id=1, source_target_pairs={{0,4},{1,5},{2,6},{3,7},{4,0},{5,1},{6,2},{7,3},{8,12},{9,13},{10,... | collective-permute-start | bytes 6152 | tf_op jit(solution)/shard_map/ppermute | solution.py:298
  18.9 2.4 %collective-permute-done.7.b23 = s32[4,128]{1,0:T(4,128)S(1)} collective-permute-done((s32[4,128]{1,0:T(4,128)S(1)}, s32[4,128]{1,0:T(4,128)S(1)}, u32[]{:S(2)}, u32[]{:S(2)}) %collective-permute-start.7) | collective-permute-done | bytes 2080 | tf_op jit(solution)/shard_map/ppermute | solution.py:298
  21.3 0.9 copy-done.5
  22.2 0.9 copy-done.6
  23.1 0.7 copy-done.8
  23.8 0.7 copy-done.12
  24.5 0.7 copy-done.13
  25.2 0.7 copy-done.14
  25.8 0.7 copy-done.15
  26.5 3.3 %prepare.1 = (bf16[4,1024,128]{2,1,0:T(8,128)(2,1)S(1)}, bf16[256,1024]{1,0:T(8,128)(2,1)S(1)}, bf16[512,128]{1,0:T(8,128)(2,1)S(1)}) custom-call(s32[1]{0:T(128)} %bitcast.1.rank, s32[64]{0:T(128)S(1)} %copy-done.14, s32[8]{0:T(128)S(1)} %copy-done.15, bf16[2,128,256]{2,1,0:T(8,128)(2,1)S(1)} %copy-done.5, ...), custom_call_target="tpu_custom_call" | custom-call | tf_op jit(solution)/shard_map/prepare/pallas_call | solution.py:321
  29.8 3.9 %attention.1 = bf16[8,136,128]{2,1,0:T(8,128)(2,1)S(1)} custom-call(bf16[8,64,256]{2,1,0:T(8,128)(2,1)S(1)} %all-to-all-done.queries, bf16[4,1024,128]{2,1,0:T(8,128)(2,1)S(1)} %get-tuple-element.10.keys_aug, bf16[256,1024]{1,0:T(8,128)(2,1)S(1)} %get-tuple-element.11.values_t, bf16[512,128]{1,0:T(8,128)(2,1)S(1)} %get-tuple-element.12.extra), custom_call_target="tpu_custom_call" | custom-call | tf_op jit(solution)/shard_map/attention/pallas_call | solution.py:353
  33.7 13.1 %all_to_all.30.parts = bf16[8,136,128]{2,1,0:T(8,128)(2,1)S(1)} all-to-all(bf16[8,136,128]{2,1,0:T(8,128)(2,1)S(1)} %attention.1), channel_id=1, replica_groups={{0,2,8,10,16,18,24,26},{1,3,9,11,17,19,25,27},{4,6,12,14,20,22,28,30},{..., dimensions={0} | all-to-all | bytes 557056 | tf_op jit(solution)/shard_map/all_to_all | solution.py:360
  46.8 1.2 %copy-done.3 = bf16[256,2048]{1,0:T(8,128)(2,1)S(1)} copy-done((bf16[256,2048]{1,0:T(8,128)(2,1)S(1)}, bf16[256,2048]{1,0:T(8,128)(2,1)}, u32[]{:S(2)}) %copy-start.3) | copy-done | bytes 1048600
  48.1 1.1 %combine.1 = bf16[64,2048]{1,0:T(8,128)(2,1)} custom-call(bf16[8,136,128]{2,1,0:T(8,128)(2,1)S(1)} %all_to_all.30.parts, bf16[256,2048]{1,0:T(8,128)(2,1)S(1)} %copy-done.3), custom_call_target="tpu_custom_call" | custom-call | tf_op jit(solution)/shard_map/combine/pallas_call | solution.py:361
  49.2 8.6 %all-to-all-start.2 = ((bf16[8,8,2048]{2,1,0:T(8,128)(2,1)}), bf16[8,8,2048]{2,1,0:T(8,128)(2,1)S(1)}, u32[]{:S(2)}, u32[]{:S(2)}) async-start(bf16[8,8,2048]{2,1,0:T(8,128)(2,1)} %bitcast.5), calls=%async_computation.2 | async-start | bytes 524288 | tf_op jit(solution)/shard_map/all_to_all | solution.py:364
  57.7 0.8 constant_dynamic-slice_fusion.states
  58.5 8.3 %all-to-all-done.2.terms = bf16[8,8,2048]{2,1,0:T(8,128)(2,1)S(1)} async-done(((bf16[8,8,2048]{2,1,0:T(8,128)(2,1)}), bf16[8,8,2048]{2,1,0:T(8,128)(2,1)S(1)}, u32[]{:S(2)}, u32[]{:S(2)}) %all-to-all-start.2) | async-done | bytes 262176 | tf_op jit(solution)/shard_map/all_to_all | solution.py:364
  66.8 0.8 norm.1
  67.6 4.8 %all-to-all-start.3 = ((bf16[8,8,2048]{2,1,0:T(8,128)(2,1)}), bf16[8,8,2048]{2,1,0:T(8,128)(2,1)S(1)}, u32[]{:S(2)}, u32[]{:S(2)}) async-start(bf16[8,8,2048]{2,1,0:T(8,128)(2,1)} %get-tuple-element.13), calls=%async_computation.3 | async-start | bytes 524288 | tf_op jit(solution)/shard_map/all_to_all | solution.py:372
  72.4 2.3 %multiply_reduce_fusion = f32[640]{0:T(1024)S(1)} fusion(bf16[640,2048]{1,0:T(8,128)(2,1)} %param.28, f32[2048]{0:T(1024)S(1)} %copy-done.7), kind=kLoop, calls=%fused_computation | loop fusion | flops 3931520 | bytes 2632192 | tf_op jit(solution)/shard_map/reduce_sum | solution.py:373
  74.7 0.1 dynamic-slice_bitcast_fusion
  74.8 0.1 copy.29.own_docs
  74.9 0.1 slice_reduce_fusion
  75.0 0.1 tile.14
  75.1 5.9 %all-to-all-done.3 = bf16[8,8,2048]{2,1,0:T(8,128)(2,1)S(1)} async-done(((bf16[8,8,2048]{2,1,0:T(8,128)(2,1)}), bf16[8,8,2048]{2,1,0:T(8,128)(2,1)S(1)}, u32[]{:S(2)}, u32[]{:S(2)}) %all-to-all-start.3) | async-done | bytes 262176 | tf_op jit(solution)/shard_map/all_to_all | solution.py:372
  81.0 1.7 %copy-done.1 = bf16[2048,640]{1,0:T(8,128)(2,1)S(1)} copy-done((bf16[2048,640]{1,0:T(8,128)(2,1)S(1)}, bf16[2048,640]{1,0:T(8,128)(2,1)}, u32[]{:S(2)}) %copy-start.1) | copy-done | bytes 2621464
  82.7 2.5 %feed.1 = f32[32,128]{1,0:T(8,128)} custom-call(bf16[64,2048]{1,0:T(8,128)(2,1)S(1)} %bitcast.15, bf16[2048,640]{1,0:T(8,128)(2,1)S(1)} %copy-done, bf16[2048,640]{1,0:T(8,128)(2,1)S(1)} %copy-done.1, f32[1,640]{1,0:T(1,128)S(1)} %reshape.127.down_score, f32[64,1]{1,0:T(8,128)S(1)} %fusion.4.own_score, s32[64,1]{1,0:T(8,128)S(1)} %copy.29.own_docs), custom_call_target="tpu_custom_call" | custom-call | tf_op jit(solution)/shard_map/feed/pallas_call | solution.py:380
  85.3 5.0 %all-to-all-start.4 = ((f32[32,1,128]{2,1,0:T(1,128)}), f32[32,1,128]{2,1,0:T(1,128)S(1)}, u32[]{:S(2)}, u32[]{:S(2)}) async-start(f32[32,1,128]{2,1,0:T(1,128)} %bitcast.11), calls=%async_computation.4 | async-start | bytes 32768 | tf_op jit(solution)/shard_map/all_to_all | solution.py:398
  90.3 7.3 %all-to-all-done.4 = f32[32,1,128]{2,1,0:T(1,128)S(1)} async-done(((f32[32,1,128]{2,1,0:T(1,128)}), f32[32,1,128]{2,1,0:T(1,128)S(1)}, u32[]{:S(2)}, u32[]{:S(2)}) %all-to-all-start.4) | async-done | bytes 16416 | tf_op jit(solution)/shard_map/all_to_all | solution.py:398
  97.7 0.1 reduce_sum.37
  97.7 0.6 broadcast_in_dim.16
  98.3 5.0 %all-to-all-start.5 = ((f32[8,1,128]{2,1,0:T(1,128)}), f32[8,1,128]{2,1,0:T(1,128)S(1)}, u32[]{:S(2)}, u32[]{:S(2)}) async-start(f32[8,1,128]{2,1,0:T(1,128)} %broadcast_in_dim.16), calls=%async_computation.5 | async-start | bytes 8192 | tf_op jit(solution)/shard_map/all_to_all | solution.py:400
  103.3 0.2 convert_reduce_fusion
  103.5 6.0 %all-to-all-done.5 = f32[8,1,128]{2,1,0:T(1,128)S(1)} async-done(((f32[8,1,128]{2,1,0:T(1,128)}), f32[8,1,128]{2,1,0:T(1,128)S(1)}, u32[]{:S(2)}, u32[]{:S(2)}) %all-to-all-start.5) | async-done | bytes 4128 | tf_op jit(solution)/shard_map/all_to_all | solution.py:400
  109.6 0.5 slice_divide_fusion
  (33 shorter events, 0.1 us)
Async XLA Ops:
  0.0 13.6 %collective-permute-start.1 = (bf16[2,128,256]{2,1,0:T(8,128)(2,1)}, bf16[2,128,256]{2,1,0:T(8,128)(2,1)S(1)}, u32[]{:S(2)}, u32[]{:S(2)}) collective-permute-start(bf16[2,128,256]{2,1,0:T(8,128)(2,1)} %k0.1), channel_id=1, source_target_pairs={{0,4},{1,5},{2,6},{3,7},{4,0},{5,1},{6,2},{7,3},{8,12},{9,13},{10,... | collective-permute-start | bytes 393224 | tf_op jit(solution)/shard_map/ppermute | solution.py:298
  3.0 10.7 %collective-permute-start.4 = (bf16[2,128,256]{2,1,0:T(8,128)(2,1)}, bf16[2,128,256]{2,1,0:T(8,128)(2,1)S(1)}, u32[]{:S(2)}, u32[]{:S(2)}) collective-permute-start(bf16[2,128,256]{2,1,0:T(8,128)(2,1)} %v0.1), channel_id=1, source_target_pairs={{0,4},{1,5},{2,6},{3,7},{4,0},{5,1},{6,2},{7,3},{8,12},{9,13},{10,... | collective-permute-start | bytes 393224 | tf_op jit(solution)/shard_map/ppermute | solution.py:298
  3.5 1.2 %copy-start.2 = (bf16[2048,256]{1,0:T(8,128)(2,1)S(1)}, bf16[2048,256]{1,0:T(8,128)(2,1)}, u32[]{:S(2)}) copy-start(bf16[2048,256]{1,0:T(8,128)(2,1)} %weight.1) | copy-start | bytes 3145732
  4.8 0.9 copy-start.4
  5.7 0.7 copy-start.10
  7.7 22.1 %all-to-all-start = ((bf16[8,64,256]{2,1,0:T(8,128)(2,1)}), bf16[8,64,256]{2,1,0:T(8,128)(2,1)S(1)}, u32[]{:S(2)}, u32[]{:S(2)}) async-start(bf16[8,64,256]{2,1,0:T(8,128)(2,1)} %project.1), calls=%async_computation | async-start | bytes 524288 | tf_op jit(solution)/shard_map/all_to_all | solution.py:318
  13.1 8.2 %collective-permute-start = (bf16[2,128,256]{2,1,0:T(8,128)(2,1)}, bf16[2,128,256]{2,1,0:T(8,128)(2,1)S(1)}, u32[]{:S(2)}, u32[]{:S(2)}) collective-permute-start(bf16[2,128,256]{2,1,0:T(8,128)(2,1)} %k0.1), channel_id=1, source_target_pairs={{0,1},{1,0},{2,3},{3,2},{4,5},{5,4},{6,7},{7,6},{8,9},{9,8},{10,11... | collective-permute-start | bytes 393224 | tf_op jit(solution)/shard_map/ppermute | solution.py:298
  13.1 8.2 %collective-permute-start.3 = (bf16[2,128,256]{2,1,0:T(8,128)(2,1)}, bf16[2,128,256]{2,1,0:T(8,128)(2,1)S(1)}, u32[]{:S(2)}, u32[]{:S(2)}) collective-permute-start(bf16[2,128,256]{2,1,0:T(8,128)(2,1)} %v0.1), channel_id=1, source_target_pairs={{0,1},{1,0},{2,3},{3,2},{4,5},{5,4},{6,7},{7,6},{8,9},{9,8},{10,11... | collective-permute-start | bytes 393224 | tf_op jit(solution)/shard_map/ppermute | solution.py:298
  13.6 7.7 %collective-permute-start.2 = (bf16[2,128,256]{2,1,0:T(8,128)(2,1)S(1)}, bf16[2,128,256]{2,1,0:T(8,128)(2,1)S(1)}, u32[]{:S(2)}, u32[]{:S(2)}) collective-permute-start(bf16[2,128,256]{2,1,0:T(8,128)(2,1)S(1)} %collective-permute-done.1.k2), channel_id=1, source_target_pairs={{0,1},{1,0},{2,3},{3,2},{4,5},{5,4},{6,7},{7,6},{8,9},{9,8},{10,11... | collective-permute-start | bytes 393224 | tf_op jit(solution)/shard_map/ppermute | solution.py:298
  13.7 7.6 %collective-permute-start.5 = (bf16[2,128,256]{2,1,0:T(8,128)(2,1)S(1)}, bf16[2,128,256]{2,1,0:T(8,128)(2,1)S(1)}, u32[]{:S(2)}, u32[]{:S(2)}) collective-permute-start(bf16[2,128,256]{2,1,0:T(8,128)(2,1)S(1)} %collective-permute-done.4.v2), channel_id=1, source_target_pairs={{0,1},{1,0},{2,3},{3,2},{4,5},{5,4},{6,7},{7,6},{8,9},{9,8},{10,11... | collective-permute-start | bytes 393224 | tf_op jit(solution)/shard_map/ppermute | solution.py:298
  14.1 1.4 %collective-permute-start.6 = (s32[2,128]{1,0:T(2,128)}, s32[2,128]{1,0:T(2,128)S(1)}, u32[]{:S(2)}, u32[]{:S(2)}) collective-permute-start(s32[2,128]{1,0:T(2,128)} %param.22), channel_id=1, source_target_pairs={{0,1},{1,0},{2,3},{3,2},{4,5},{5,4},{6,7},{7,6},{8,9},{9,8},{10,11... | collective-permute-start | bytes 3080 | tf_op jit(solution)/shard_map/ppermute | solution.py:298
  16.2 5.1 %collective-permute-start.7 = (s32[4,128]{1,0:T(4,128)S(1)}, s32[4,128]{1,0:T(4,128)S(1)}, u32[]{:S(2)}, u32[]{:S(2)}) collective-permute-start(s32[4,128]{1,0:T(4,128)S(1)} %pad_add_fusion.b01), channel_id=1, source_target_pairs={{0,4},{1,5},{2,6},{3,7},{4,0},{5,1},{6,2},{7,3},{8,12},{9,13},{10,... | collective-permute-start | bytes 6152 | tf_op jit(solution)/shard_map/ppermute | solution.py:298
  21.3 0.9 copy-start.5
  22.2 0.9 copy-start.6
  23.1 0.7 copy-start.8
  23.8 0.7 copy-start.12
  24.5 0.7 copy-start.13
  25.1 0.7 copy-start.14
  25.8 0.7 copy-start.15
  29.8 37.0 %copy-start.7 = (f32[2048]{0:T(1024)S(1)}, f32[2048]{0:T(1024)}, u32[]{:S(2)}) copy-start(f32[2048]{0:T(1024)} %param.29) | copy-start | bytes 24580
  29.8 37.0 %copy-start.11 = (f32[2048]{0:T(1024)S(1)}, f32[2048]{0:T(1024)}, u32[]{:S(2)}) copy-start(f32[2048]{0:T(1024)} %param.25) | copy-start | bytes 24580
  46.8 1.2 %copy-start.3 = (bf16[256,2048]{1,0:T(8,128)(2,1)S(1)}, bf16[256,2048]{1,0:T(8,128)(2,1)}, u32[]{:S(2)}) copy-start(bf16[256,2048]{1,0:T(8,128)(2,1)} %out_weight.1) | copy-start | bytes 3145732
  48.1 26.7 %copy-start.9 = (s32[2048]{0:T(1024)S(1)}, s32[2048]{0:T(1024)}, u32[]{:S(2)}) copy-start(s32[2048]{0:T(1024)} %param.32) | copy-start | bytes 24580
  48.1 32.9 %copy-start = (bf16[2048,640]{1,0:T(8,128)(2,1)S(1)}, bf16[2048,640]{1,0:T(8,128)(2,1)}, u32[]{:S(2)}) copy-start(bf16[2048,640]{1,0:T(8,128)(2,1)} %gate_weight.1) | copy-start | bytes 7864324
  49.2 17.6 %all-to-all-start.2 = ((bf16[8,8,2048]{2,1,0:T(8,128)(2,1)}), bf16[8,8,2048]{2,1,0:T(8,128)(2,1)S(1)}, u32[]{:S(2)}, u32[]{:S(2)}) async-start(bf16[8,8,2048]{2,1,0:T(8,128)(2,1)} %bitcast.5), calls=%async_computation.2 | async-start | bytes 524288 | tf_op jit(solution)/shard_map/all_to_all | solution.py:364
  67.6 13.4 %all-to-all-start.3 = ((bf16[8,8,2048]{2,1,0:T(8,128)(2,1)}), bf16[8,8,2048]{2,1,0:T(8,128)(2,1)S(1)}, u32[]{:S(2)}, u32[]{:S(2)}) async-start(bf16[8,8,2048]{2,1,0:T(8,128)(2,1)} %get-tuple-element.13), calls=%async_computation.3 | async-start | bytes 524288 | tf_op jit(solution)/shard_map/all_to_all | solution.py:372
  81.0 1.7 %copy-start.1 = (bf16[2048,640]{1,0:T(8,128)(2,1)S(1)}, bf16[2048,640]{1,0:T(8,128)(2,1)}, u32[]{:S(2)}) copy-start(bf16[2048,640]{1,0:T(8,128)(2,1)} %up_weight.1) | copy-start | bytes 7864324
  85.3 12.4 %all-to-all-start.4 = ((f32[32,1,128]{2,1,0:T(1,128)}), f32[32,1,128]{2,1,0:T(1,128)S(1)}, u32[]{:S(2)}, u32[]{:S(2)}) async-start(f32[32,1,128]{2,1,0:T(1,128)} %bitcast.11), calls=%async_computation.4 | async-start | bytes 32768 | tf_op jit(solution)/shard_map/all_to_all | solution.py:398
  98.3 11.3 %all-to-all-start.5 = ((f32[8,1,128]{2,1,0:T(1,128)}), f32[8,1,128]{2,1,0:T(1,128)S(1)}, u32[]{:S(2)}, u32[]{:S(2)}) async-start(f32[8,1,128]{2,1,0:T(1,128)} %broadcast_in_dim.16), calls=%async_computation.5 | async-start | bytes 8192 | tf_op jit(solution)/shard_map/all_to_all | solution.py:400

commit v3 on v2

v3 whole, which is shorter than its diff:
```python
import functools

import jax
import jax.numpy as jnp
from jax import lax
from jax.experimental import pallas as pl
from jax.experimental.pallas import tpu as pltpu
from jax.sharding import PartitionSpec as P

NQ = 8
DOCS = 256
MASKED = -1e30
BF = jnp.bfloat16
F32 = jnp.float32


def rms_scale(values, gain):
    values = values.astype(F32)
    return values * lax.rsqrt(jnp.mean(values * values, axis=-1, keepdims=True) + 1e-06) * gain


def split_three(value):
    first = value.astype(BF)
    rest = value - first.astype(F32)
    second = rest.astype(BF)
    third = (rest - second.astype(F32)).astype(BF)
    return first, second, third


def project_kernel(states, gain, weight, out, states_here, gain_here, weight_here, arrivals):
    pairs = ((states, states_here), (gain, gain_here), (weight, weight_here))
    copies = [pltpu.make_async_copy(there, here, arrivals.at[i]) for i, (there, here) in enumerate(pairs)]
    for copy in copies:
        copy.start()
    copies[0].wait()
    copies[1].wait()
    normed = rms_scale(states_here[...], gain_here[...]).astype(BF)
    copies[2].wait()
    queries = jnp.dot(normed, weight_here[...], preferred_element_type=F32).astype(BF)
    for chip in range(out.shape[0]):
        out[chip] = queries


def columns_kernel(rank, doc_query, doc_rows, extra, query_here, rows_here, arrivals):
    copies = [
        pltpu.make_async_copy(doc_query, query_here, arrivals.at[0]),
        pltpu.make_async_copy(doc_rows, rows_here, arrivals.at[1]),
    ]
    for copy in copies:
        copy.start()
    tokens = extra.shape[0]
    tok_dev = doc_rows.shape[1] // 2
    row_chips = 4
    core = rank[0] % 2
    chip = rank[0] // 2
    pair = chip - chip % 2
    doc_count = doc_query.shape[1]
    left = lax.broadcasted_iota(jnp.int32, (1, 128), 1) < tok_dev
    doc_id = lax.broadcasted_iota(jnp.int32, (doc_count, 128), 0)
    for copy in copies:
        copy.wait()
    blocks = []
    for y in range(tokens // (2 * tok_dev)):
        two = rows_here[pl.ds(y * row_chips + pair % row_chips, 2), :]
        turned = pltpu.roll(two, tok_dev, 1)
        row = jnp.where(
            left,
            jnp.where(core == 0, two[0:1], turned[0:1]),
            jnp.where(core == 0, turned[1:2], two[1:2]),
        )
        blocks.append((doc_id == row).astype(F32).astype(BF))
    member = jnp.concatenate(blocks, axis=1)
    asked = jnp.broadcast_to(query_here[...].astype(F32), (128, doc_count)).astype(BF)
    tok_query = jnp.dot(asked, member, preferred_element_type=F32)
    mark = lax.broadcasted_iota(jnp.int32, (128, tokens), 0) % 64
    columns = jnp.where(
        mark < NQ,
        jnp.where(tok_query == mark.astype(F32), 0.0, MASKED),
        jnp.where(mark == NQ, MASKED, jnp.where(mark < NQ + 4, 1.0, 0.0)),
    )
    extra[...] = columns.T.astype(BF)


def prepare_kernel(rank, k0, k1, v0, v1, b0, b1, bias_table, page_table, query_lengths, keys_aug, values_t,
                   held, bucket_here, table_here, slots_here, lengths_here, info, arrivals, *, side):
    pages, page_len, width = k0.shape
    heads, bucket_count = bias_table.shape
    depth = width // heads
    slot_count = page_table.shape[0]
    max_pages = slot_count // NQ
    row_chips = 4
    pairs = [(page_table, slots_here), (query_lengths, lengths_here), (bias_table, table_here)]
    pairs += [(b0, bucket_here.at[0]), (b1, bucket_here.at[1])]
    pairs += [(cache, held.at[i]) for i, cache in enumerate((k0, k1, v0, v1))]
    copies = [pltpu.make_async_copy(there, here, arrivals.at[i]) for i, (there, here) in enumerate(pairs)]
    for copy in copies:
        copy.start()
    core = rank[0] % 2
    chip = rank[0] // 2
    base = (chip // row_chips * row_chips + chip % 2) * 2 * pages
    count = 4 * pages
    copies[0].wait()
    copies[1].wait()
    for s in range(slot_count):
        place = slots_here[s] - base
        near = (place >= 0) & (place < 2 * pages)
        far = (place >= 4 * pages) & (place < 6 * pages)
        place = jnp.where(near, place, jnp.where(far, place - 2 * pages, count))
        info[0, place] = s // max_pages
        info[1, place] = lengths_here[s // max_pages] - (s % max_pages) * page_len
    low = lax.broadcasted_iota(jnp.int32, (1, 128), 1) < depth
    col = lax.broadcasted_iota(jnp.int32, (bucket_count, 128), 1) % 64
    copies[2].wait()
    table = jnp.concatenate([table_here[...], jnp.zeros((8 - heads, bucket_count), F32)], axis=0).T
    spreads = []
    for h in range(heads):
        a, b, c = split_three(jnp.broadcast_to(table[:, h : h + 1], (bucket_count, 128)))
        third = jnp.where(col == NQ + 3, c.astype(F32), 0.0)
        spreads.append(
            jnp.where(col == NQ + 1, a.astype(F32), jnp.where(col == NQ + 2, b.astype(F32), third)).astype(BF)
        )
    spread = jnp.concatenate(spreads, axis=1)
    bucket_row = lax.broadcasted_iota(jnp.int32, (bucket_count, page_len), 0)
    slot = lax.broadcasted_iota(jnp.int32, (page_len, 128), 0)
    key_col = lax.broadcasted_iota(jnp.int32, (page_len, 128), 1) % 64
    mine = ((chip % row_chips // 2) * 2 + core) * pages
    for copy in copies[3:]:
        copy.wait()
    for part in range(2):
        for page in range(pages):
            place = (mine ^ ((2 * side + part) * pages)) + page
            span = pl.ds((part * pages + page) * page_len, page_len)
            bucket = bucket_here[part, page : page + 1, :]
            onehot = (jnp.broadcast_to(bucket, bucket_row.shape) == bucket_row).astype(F32).astype(BF)
            bias = lax.dot_general(onehot, spread, (((0,), (0,)), ((), ())), preferred_element_type=F32)
            holder = jnp.where(slot < info[1, place], info[0, place], NQ)
            marks = (key_col == holder).astype(F32)
            key = held[part, page].astype(F32)
            for h in range(heads):
                keep = low if h % 2 == 0 else jnp.logical_not(low)
                half = key[:, (h // 2) * 128 : (h // 2 + 1) * 128]
                keys_aug[h, span, :] = jnp.where(keep, half, bias[:, h * 128 : (h + 1) * 128] + marks).astype(BF)
            values_t[:, span] = held[2 + part, page].astype(F32).T.astype(BF)


def attention_kernel(queries, keys_near, keys_far, values_near, values_far, extra, out, rows_aug):
    chips, tok_dev, width = queries.shape
    heads = keys_near.shape[0]
    depth = width // heads
    low = lax.broadcasted_iota(jnp.int32, (1, 128), 1) < depth
    left = lax.broadcasted_iota(jnp.int32, (1, 128), 1) < tok_dev
    rows = queries[...].reshape(chips * tok_dev, width)
    for h in range(heads):
        half = rows[:, (h // 2) * 128 : (h // 2 + 1) * 128].astype(F32)
        keep = low if h % 2 == 0 else jnp.logical_not(low)
        rows_aug[h] = jnp.where(keep, half, extra[...].astype(F32)).astype(BF)
    sums = []
    logs = []
    for h in range(heads):
        span = slice(h * depth, (h + 1) * depth)
        scores = [
            lax.dot_general(keys[h], rows_aug[h], (((1,), (1,)), ((), ())), preferred_element_type=F32)
            for keys in (keys_near, keys_far)
        ]
        top = jnp.maximum(
            jnp.max(scores[0], axis=0, keepdims=True), jnp.max(scores[1], axis=0, keepdims=True)
        )
        total = jnp.zeros_like(top)
        summed = jnp.zeros((depth, chips * tok_dev), F32)
        for part, values in zip(scores, (values_near, values_far)):
            weights = jnp.exp(part - top)
            total += jnp.sum(weights, axis=0, keepdims=True)
            summed += jnp.dot(values[span, :], weights.astype(BF), preferred_element_type=F32)
        sums.append(summed / total)
        logs.append(top + jnp.log(total))
    for duo in range(chips // 2):
        lanes = slice(duo * 128, (duo + 1) * 128)
        pad = [jnp.zeros((6, 128), F32)]
        upper = jnp.concatenate([sums[0][:, lanes], sums[1][:, lanes]], axis=0)
        lower = jnp.concatenate([sums[2][:, lanes], sums[3][:, lanes]], axis=0)
        stat_upper = jnp.concatenate([logs[0][:, lanes], logs[1][:, lanes]] + pad, axis=0)
        stat_lower = jnp.concatenate([logs[2][:, lanes], logs[3][:, lanes]] + pad, axis=0)
        block = (
            jnp.where(left, upper, pltpu.roll(lower, tok_dev, 1)),
            jnp.where(left, pltpu.roll(upper, tok_dev, 1), lower),
        )
        stat = (
            jnp.where(left, stat_upper, pltpu.roll(stat_lower, tok_dev, 1)),
            jnp.where(left, pltpu.roll(stat_upper, tok_dev, 1), stat_lower),
        )
        for which in range(2):
            a, b, c = split_three(stat[which])
            packed = [a[0:2].astype(F32), b[0:2].astype(F32), c[0:2].astype(F32), jnp.zeros((2, 128), F32)]
            out[duo * 2 + which, 0:128, :] = block[which].astype(BF)
            out[duo * 2 + which, 128:136, :] = jnp.concatenate(packed, axis=0).astype(BF)


def combine_kernel(parts, out_weight, out, weight_here, arrival):
    copy = pltpu.make_async_copy(out_weight, weight_here, arrival)
    copy.start()
    chips = parts.shape[0]
    logs = []
    for chip in range(chips):
        stat = parts[chip, 128:136, :].astype(F32)
        logs.append(stat[0:2] + stat[2:4] + stat[4:6])
    top = logs[0]
    for chip in range(1, chips):
        top = jnp.maximum(top, logs[chip])
    scales = [jnp.exp(log - top) for log in logs]
    whole = scales[0]
    for chip in range(1, chips):
        whole = whole + scales[chip]
    sums = [jnp.zeros((64, 128), F32), jnp.zeros((64, 128), F32)]
    for chip in range(chips):
        share = scales[chip] / whole
        for r in range(2):
            sums[r] = sums[r] + share[r : r + 1] * parts[chip, r * 64 : (r + 1) * 64, :].astype(F32)
    joined = jnp.concatenate(sums, axis=0).T
    context = jnp.concatenate([joined[0:64], joined[64:128]], axis=1).astype(BF)
    copy.wait()
    out[...] = jnp.dot(context, weight_here[...], preferred_element_type=F32).astype(BF)


def norm_kernel(terms, states, gain, score_vector, out, score):
    hidden = states[...].astype(F32)
    for source in range(terms.shape[0]):
        hidden = hidden + terms[source].astype(F32)
    normed = rms_scale(hidden, gain[...]).astype(BF)
    for target in range(out.shape[0]):
        out[target] = normed
    score[...] = jnp.broadcast_to(jnp.sum(hidden * score_vector[...], axis=-1, keepdims=True), score.shape)


def feed_kernel(rows, gate_weight, up_weight, down_score, own_score, own_docs, out, gate_here, up_here, arrivals):
    steps = gate_here.shape[0]
    size = rows.shape[1] // steps
    copies = []
    for i in range(steps):
        for j, (there, here) in enumerate(((gate_weight, gate_here), (up_weight, up_here))):
            copies.append(
                pltpu.make_async_copy(there.at[pl.ds(i * size, size)], here.at[i], arrivals.at[2 * i + j])
            )
    for copy in copies:
        copy.start()
    gate = jnp.zeros((rows.shape[0], gate_weight.shape[1]), F32)
    upper = gate
    for i in range(steps):
        part = rows[:, i * size : (i + 1) * size]
        copies[2 * i].wait()
        gate += jnp.dot(part, gate_here[i], preferred_element_type=F32)
        copies[2 * i + 1].wait()
        upper += jnp.dot(part, up_here[i], preferred_element_type=F32)
    middle = (jax.nn.gelu(gate, approximate=True) * upper).astype(BF).astype(F32)
    tok_score = jnp.sum(middle * down_score[...], axis=-1, keepdims=True) + own_score[...]
    docs = own_docs[...]
    doc_dev = DOCS // out.shape[0]
    lane = lax.broadcasted_iota(jnp.int32, (docs.shape[0], 128), 1)
    holder = (docs // doc_dev == lane).astype(F32).astype(BF)
    placed = jnp.where(docs % doc_dev == lane, tok_score, 0.0)
    sums = jnp.zeros((128, 128), F32)
    for piece in split_three(placed):
        sums += lax.dot_general(holder, piece, (((0,), (0,)), ((), ())), preferred_element_type=F32)
    out[...] = sums[0 : out.shape[0]]


def fold_kernel(terms, out):
    out[...] = jnp.broadcast_to(jnp.sum(terms[...], axis=0, keepdims=True), out.shape)


def vmem():
    return pl.BlockSpec(memory_space=pltpu.VMEM)


def smem():
    return pl.BlockSpec(memory_space=pltpu.SMEM)


def in_hbm(value):
    return pltpu.with_memory_space_constraint(value, pltpu.HBM)


def hbm():
    return pl.BlockSpec(memory_space=pltpu.HBM)


def anywhere():
    return pl.BlockSpec(memory_space=pl.ANY)


def call(kernel, name, shapes, specs, scratch=()):
    single = not isinstance(shapes, (list, tuple))
    return pl.pallas_call(
        kernel,
        out_shape=shapes,
        in_specs=specs,
        out_specs=vmem() if single else [vmem()] * len(shapes),
        scratch_shapes=list(scratch),
        compiler_params=pltpu.CompilerParams(vmem_limit_bytes=40 << 20),
        name=name,
    )


def per_device(
    doc_states,
    gain_attn,
    query_weight,
    cache_keys,
    cache_values,
    rel_bucket,
    bias_table,
    out_weight,
    gain_ffn,
    wi_gate,
    wi_up,
    wo_ffn,
    score_vector,
    query_lengths,
    doc_query,
    doc_of_token,
    page_table,
):
    shape = jax.ShapeDtypeStruct
    tok_dev, model = doc_states.shape
    local_pages, page_len, local_width = cache_keys.shape
    local_heads = bias_table.shape[1]
    page_size = lax.axis_size("page")
    head_size = lax.axis_size("head")
    page_rank = lax.axis_index("page")
    head_rank = lax.axis_index("head")
    group = page_size // 4
    groups = [
        [y * 8 + (x + side) * 2 + core for y in range(4) for side in range(2)] for x in (0, 2) for core in range(2)
    ]
    core_swap = [(i, i ^ 1) for i in range(page_size)]
    side_swap = [(i, i ^ 4) for i in range(page_size)]

    def swap(value, pairs):
        return lax.ppermute(value, "page", pairs)

    far_swap = [(i, i ^ 5) for i in range(page_size)]
    copies = call(
        project_kernel, "project", shape((group, tok_dev, local_width), BF), [hbm()] * 3,
        [
            pltpu.VMEM((tok_dev, model), BF),
            pltpu.VMEM((1, model), F32),
            pltpu.VMEM((model, local_width), BF),
            pltpu.SemaphoreType.DMA((3,)),
        ],
    )(in_hbm(doc_states), in_hbm(gain_attn.reshape(1, model)), in_hbm(query_weight))
    sent_keys, sent_values, copies = lax.optimization_barrier((cache_keys, cache_values, copies))
    keys_side = swap(sent_keys, side_swap)
    values_side = swap(sent_values, side_swap)
    keys_core = swap(cache_keys, core_swap)
    values_core = swap(cache_values, core_swap)
    bucket_core = swap(rel_bucket, core_swap)
    bucket_side = swap(rel_bucket, side_swap)
    bucket_far = swap(rel_bucket, far_swap)
    keys_far = swap(keys_side, core_swap)
    values_far = swap(values_side, core_swap)
    gathered = lax.all_to_all(copies, "page", 0, 0, axis_index_groups=groups, tiled=True)

    rank = page_rank.reshape(1)
    doc_rows = doc_of_token.reshape(-1, 2 * tok_dev)
    extra = call(
        columns_kernel, "columns", shape((group * tok_dev, 128), BF), [smem()] + [hbm()] * 2,
        [
            pltpu.VMEM((1, doc_query.shape[0]), jnp.int32),
            pltpu.VMEM(doc_rows.shape, jnp.int32),
            pltpu.SemaphoreType.DMA((2,)),
        ],
    )(rank, in_hbm(doc_query.reshape(1, -1)), in_hbm(doc_rows))
    key_count = 2 * local_pages * page_len

    def prepared(side, caches, buckets):
        return call(
            functools.partial(prepare_kernel, side=side),
            "prepare",
            [shape((local_heads, key_count, 128), BF), shape((local_width, key_count), BF)],
            [smem()] + [anywhere()] * 6 + [hbm()] * 3,
            [
                pltpu.VMEM((4, local_pages, page_len, local_width), BF),
                pltpu.VMEM((2, local_pages, page_len), jnp.int32),
                pltpu.VMEM(bias_table.T.shape, F32),
                pltpu.SMEM(page_table.shape, jnp.int32),
                pltpu.SMEM(query_lengths.shape, jnp.int32),
                pltpu.SMEM((2, 4 * local_pages + 1), jnp.int32),
                pltpu.SemaphoreType.DMA((9,)),
            ],
        )(rank, *caches, *buckets, in_hbm(bias_table.T), in_hbm(page_table), in_hbm(query_lengths))

    near = (in_hbm(cache_keys), keys_core, in_hbm(cache_values), values_core)
    keys_near, values_near = prepared(0, near, (in_hbm(rel_bucket), bucket_core))
    keys_away, values_away = prepared(1, (keys_side, keys_far, values_side, values_far), (bucket_side, bucket_far))
    partials = call(
        attention_kernel,
        "attention",
        shape((group, 136, 128), BF),
        [vmem()] * 6,
        [pltpu.VMEM((local_heads, group * tok_dev, 128), BF)],
    )(gathered, keys_near, keys_away, values_near, values_away, extra)
    returned = lax.all_to_all(partials, "page", 0, 0, axis_index_groups=groups, tiled=True)
    projected = call(
        combine_kernel, "combine", shape((tok_dev, model), BF), [vmem(), hbm()],
        [pltpu.VMEM((local_width, model), BF), pltpu.SemaphoreType.DMA(())],
    )(returned, in_hbm(out_weight))

    own = tok_dev // head_size
    terms = lax.all_to_all(projected.reshape(head_size, own, model), "head", 0, 0, tiled=True)
    own_states = lax.dynamic_slice_in_dim(doc_states, head_rank * own, own, 0)
    spread, hidden_score = call(
        norm_kernel,
        "norm",
        [shape((head_size, own, model), BF), shape((own, 128), F32)],
        [vmem()] * 4,
    )(terms, own_states, gain_ffn.reshape(1, model), score_vector.reshape(1, model))
    rows = lax.all_to_all(spread, "head", 0, 0, tiled=True).reshape(tok_dev, model)
    down_score = jnp.sum(wo_ffn.astype(F32) * score_vector, axis=-1)
    token = jnp.arange(tok_dev, dtype=jnp.int32)[:, None]
    own_score = jnp.where(token // own == head_rank, jnp.tile(hidden_score[:, :1], (head_size, 1)), 0.0)
    own_docs = lax.dynamic_slice_in_dim(doc_of_token, page_rank * tok_dev, tok_dev, 0)[:, None]
    doc_dev = doc_query.shape[0] // page_size
    steps = 4
    weight_slices = pltpu.VMEM((steps, model // steps, wi_gate.shape[1]), BF)
    doc_sums = call(
        feed_kernel, "feed", shape((page_size, 128), F32), [vmem(), hbm(), hbm(), vmem(), vmem(), vmem()],
        [weight_slices, weight_slices, pltpu.SemaphoreType.DMA((2 * steps,))],
    )(rows, in_hbm(wi_gate), in_hbm(wi_up), down_score.reshape(1, -1), own_score, own_docs)
    doc_sums = doc_sums.reshape(page_size, 1, 128)
    arrived = lax.all_to_all(doc_sums, "page", 0, 0, tiled=True)
    pooled = call(fold_kernel, "fold", shape((head_size, 1, 128), F32), [vmem()])(arrived)
    pooled = jnp.sum(lax.all_to_all(pooled, "head", 0, 0, tiled=True), axis=(0, 1))[:doc_dev]
    mine_docs = page_rank * doc_dev + jnp.arange(doc_dev, dtype=jnp.int32)
    counts = jnp.sum((doc_of_token[:, None] == mine_docs[None, :]).astype(F32), axis=0)
    return pooled / counts


def solution(mesh):
    return jax.shard_map(
        per_device,
        mesh=mesh,
        in_specs=(
            P("page", None),
            P(),
            P(None, "head"),
            P("page", None, "head"),
            P("page", None, "head"),
            P("page", None),
            P(None, "head"),
            P("head", None),
            P(),
            P(None, "head"),
            P(None, "head"),
            P("head", None),
            P(),
            P(),
            P(),
            P(),
            P(),
        ),
        out_specs=P("page"),
        check_vma=False,
    )
```

time: 112 us -> 105 us (0.938)
  local copies, waits for them, and re-layouts: 12.7 us -> 1.16 us
  Pallas kernels: 12.9 us -> 18.6 us
  other arithmetic: 3.82 us -> 1.34 us
  waiting for transfers between devices: 31.1 us -> 32.8 us
    unnamed x32 -> x8, local copies, waits for them, and re-layouts: 11 us -> 0.02 us
    pallas_call x3 -> x6, Pallas kernels: 6.94 us -> 11.5 us  [the longest x1 4.17 us: per_device(): call(feed_kernel, 'feed', shape((page_size, 128), F32), [vmem(), hbm(), h...]
    all_to_all x1, waiting for transfers between devices: 5.87 us -> 7.7 us  [per_device(): lax.all_to_all(spread, 'head', 0, 0, tiled=True).reshape(tok_dev, model)]
    reduce_sum x1, other arithmetic: 2.33 us -> 0.58 us  [per_device(): down_score = jnp.sum(wo_ffn.astype(F32) * score_vector, axis=-1)]
    ppermute x8 -> x9, starting transfers between devices: 7.37 us -> 7.95 us  [swap(): return lax.ppermute(value, 'page', pairs)]
    ppermute x8 -> x9, waiting for transfers between devices: 3.63 us -> 3.21 us  [swap(): return lax.ppermute(value, 'page', pairs)]
  transfers between devices with their start and end apart: 13 -> 14, of which waited for: 6 -> 7; matrix products, arithmetic and copies ran while one was open for 4% -> 2% of each run, Pallas kernels for 4% -> 4%
where the time goes in v3:
time: 105 us; the launch traced here: 103 us
  starting transfers between devices  36.7 us (35%)
  waiting for transfers between devices  32.8 us (31%)
  Pallas kernels  18.6 us (18%)
  blocking collectives  12.6 us (12%)
  other arithmetic  1.34 us (1%)
  local copies, waits for them, and re-layouts  1.16 us (1%)
    all_to_all x1, blocking collectives, per_device(): lax.all_to_all(partials, 'page', 0, 0, axis_index_groups=groups, tiled=True)  12.6 us
    all_to_all x1, starting transfers between devices, per_device(): lax.all_to_all(projected.reshape(head_size, own, model), 'head', 0, 0, ti...  8.58 us
    all_to_all x1, waiting for transfers between devices, per_device(): lax.all_to_all(projected.reshape(head_size, own, model), 'head', 0, 0, ti...  8.53 us
    ppermute x9, starting transfers between devices, swap(): return lax.ppermute(value, 'page', pairs)  7.95 us
    all_to_all x1, waiting for transfers between devices, per_device(): lax.all_to_all(spread, 'head', 0, 0, tiled=True).reshape(tok_dev, model)  7.7 us
    all_to_all x1, waiting for transfers between devices, per_device(): arrived = lax.all_to_all(doc_sums, 'page', 0, 0, tiled=True)  7.33 us
    all_to_all x1, waiting for transfers between devices, per_device(): lax.all_to_all(pooled, 'head', 0, 0, tiled=True)  6.05 us
    all_to_all x1, starting transfers between devices, per_device(): lax.all_to_all(copies, 'page', 0, 0, axis_index_groups=groups, tiled=True)  5.4 us
  transfers between devices with their start and end apart: 14, of which 7 were waited for; matrix products, arithmetic and copies ran while one was open for 2% of the time, Pallas kernels for 4%

profile of v3, /device:TPU:32, one launch (start us, length us, event | category | flops | bytes accessed | tf_op | source)
XLA Modules:
  0.0 103.5 jit_solution(13086279536235599645)
XLA Ops:
  0.0 2.4 %project.1 = bf16[8,64,256]{2,1,0:T(8,128)(2,1)} custom-call(bf16[64,2048]{1,0:T(8,128)(2,1)} %states.1, f32[1,2048]{1,0:T(1,128)} %bitcast.16, bf16[2048,256]{1,0:T(8,128)(2,1)} %weight.1), custom_call_target="tpu_custom_call" | custom-call | tf_op jit(solution)/shard_map/project/pallas_call | solution.py:341
  2.4 3.1 %collective-permute-start.3 = (bf16[2,128,256]{2,1,0:T(8,128)(2,1)}, bf16[2,128,256]{2,1,0:T(8,128)(2,1)S(1)}, u32[]{:S(2)}, u32[]{:S(2)}) collective-permute-start(bf16[2,128,256]{2,1,0:T(8,128)(2,1)} %k0.1), channel_id=1, source_target_pairs={{0,4},{1,5},{2,6},{3,7},{4,0},{5,1},{6,2},{7,3},{8,12},{9,13},{10,... | collective-permute-start | bytes 393224 | tf_op jit(solution)/shard_map/ppermute | solution.py:338
  5.5 0.5 collective-permute-start.5
  6.0 5.4 %all-to-all-start = ((bf16[8,64,256]{2,1,0:T(8,128)(2,1)}), bf16[8,64,256]{2,1,0:T(8,128)(2,1)S(1)}, u32[]{:S(2)}, u32[]{:S(2)}) async-start(bf16[8,64,256]{2,1,0:T(8,128)(2,1)} %project.1), calls=%async_computation | async-start | bytes 524288 | tf_op jit(solution)/shard_map/all_to_all | solution.py:360
  11.4 0.0 collective-permute-start
  11.4 0.5 collective-permute-start.1
  11.9 0.0 collective-permute-done.3.k0
  11.9 0.1 collective-permute-start.4
  12.0 0.2 collective-permute-done.5.v0
  12.2 0.2 collective-permute-start.6
  12.4 0.3 collective-permute-start.2
  12.7 1.0 %collective-permute-done.2.b1 = s32[2,128]{1,0:T(2,128)S(1)} collective-permute-done((s32[2,128]{1,0:T(2,128)}, s32[2,128]{1,0:T(2,128)S(1)}, u32[]{:S(2)}, u32[]{:S(2)}) %collective-permute-start.2) | collective-permute-done | bytes 1056 | tf_op jit(solution)/shard_map/ppermute | solution.py:338
  13.8 3.2 %collective-permute-start.7 = (s32[2,128]{1,0:T(2,128)}, s32[2,128]{1,0:T(2,128)S(1)}, u32[]{:S(2)}, u32[]{:S(2)}) collective-permute-start(s32[2,128]{1,0:T(2,128)} %b0.1), channel_id=1, source_target_pairs={{0,4},{1,5},{2,6},{3,7},{4,0},{5,1},{6,2},{7,3},{8,12},{9,13},{10,... | collective-permute-start | bytes 3080 | tf_op jit(solution)/shard_map/ppermute | solution.py:338
  17.0 0.0 collective-permute-done.k1
  17.0 0.0 collective-permute-start.8
  17.0 1.1 %columns.1.extra = bf16[512,128]{1,0:T(8,128)(2,1)S(1)} custom-call(s32[1]{0:T(128)} %bitcast.1.rank, s32[1,256]{1,0:T(1,128)} %bitcast.19, s32[16,128]{1,0:T(8,128)} %bitcast.15), custom_call_target="tpu_custom_call" | custom-call | tf_op jit(solution)/shard_map/columns/pallas_call | solution.py:364
  18.1 0.0 collective-permute-done.1.v1
  18.1 1.7 %prepare.2 = (bf16[4,512,128]{2,1,0:T(8,128)(2,1)S(1)}, bf16[256,512]{1,0:T(8,128)(2,1)S(1)}) custom-call(s32[1]{0:T(128)} %bitcast.1.rank, bf16[2,128,256]{2,1,0:T(8,128)(2,1)} %k0.1, bf16[2,128,256]{2,1,0:T(8,128)(2,1)S(1)} %collective-permute-done.k1, bf16[2,128,256]{2,1,0:T(8,128)(2,1)} %v0.1, bf16[2,128,256]{2,1,0:T(8,128)(2,1)S(1)} %collective-permute-done.1.v1, ...), custom_call_target="tpu_custom_call" | custom-call | tf_op jit(solution)/shard_map/prepare/pallas_call | solution.py:375
  19.7 0.0 collective-permute-done.7.b0
  19.8 1.9 %collective-permute-done.8.b1 = s32[2,128]{1,0:T(2,128)S(1)} collective-permute-done((s32[2,128]{1,0:T(2,128)}, s32[2,128]{1,0:T(2,128)S(1)}, u32[]{:S(2)}, u32[]{:S(2)}) %collective-permute-start.8) | collective-permute-done | bytes 1056 | tf_op jit(solution)/shard_map/ppermute | solution.py:338
  21.7 0.0 collective-permute-done.4.k1
  21.7 1.7 %prepare.3 = (bf16[4,512,128]{2,1,0:T(8,128)(2,1)S(1)}, bf16[256,512]{1,0:T(8,128)(2,1)S(1)}) custom-call(s32[1]{0:T(128)} %bitcast.1.rank, bf16[2,128,256]{2,1,0:T(8,128)(2,1)S(1)} %collective-permute-done.3.k0, bf16[2,128,256]{2,1,0:T(8,128)(2,1)S(1)} %collective-permute-done.4.k1, bf16[2,128,256]{2,1,0:T(8,128)(2,1)S(1)} %collective-permute-done.5.v0, ...), custom_call_target="tpu_custom_call" | custom-call | tf_op jit(solution)/shard_map/prepare/pallas_call | solution.py:375
  23.4 0.0 copy-start
  23.4 0.0 copy-start.1
  23.4 0.0 all-to-all-done.queries
  23.4 3.9 %attention.1 = bf16[8,136,128]{2,1,0:T(8,128)(2,1)S(1)} custom-call(bf16[8,64,256]{2,1,0:T(8,128)(2,1)S(1)} %all-to-all-done.queries, bf16[4,512,128]{2,1,0:T(8,128)(2,1)S(1)} %get-tuple-element.15.keys_near, bf16[4,512,128]{2,1,0:T(8,128)(2,1)S(1)} %get-tuple-element.18.keys_far, bf16[256,512]{1,0:T(8,128)(2,1)S(1)} %get-tuple-element.19.values_near, ...), custom_call_target="tpu_custom_call" | custom-call | tf_op jit(solution)/shard_map/attention/pallas_call | solution.py:394
  27.3 0.0 copy-start.2
  27.3 12.6 %all_to_all.30.parts = bf16[8,136,128]{2,1,0:T(8,128)(2,1)S(1)} all-to-all(bf16[8,136,128]{2,1,0:T(8,128)(2,1)S(1)} %attention.1), channel_id=1, replica_groups={{0,2,8,10,16,18,24,26},{1,3,9,11,17,19,25,27},{4,6,12,14,20,22,28,30},{..., dimensions={0} | all-to-all | bytes 557056 | tf_op jit(solution)/shard_map/all_to_all | solution.py:401
  40.0 2.3 %combine.1 = bf16[64,2048]{1,0:T(8,128)(2,1)} custom-call(bf16[8,136,128]{2,1,0:T(8,128)(2,1)S(1)} %all_to_all.30.parts, bf16[256,2048]{1,0:T(8,128)(2,1)} %out_weight.1), custom_call_target="tpu_custom_call" | custom-call | tf_op jit(solution)/shard_map/combine/pallas_call | solution.py:402
  42.3 8.6 %all-to-all-start.2 = ((bf16[8,8,2048]{2,1,0:T(8,128)(2,1)}), bf16[8,8,2048]{2,1,0:T(8,128)(2,1)S(1)}, u32[]{:S(2)}, u32[]{:S(2)}) async-start(bf16[8,8,2048]{2,1,0:T(8,128)(2,1)} %bitcast.5), calls=%async_computation.2 | async-start | bytes 524288 | tf_op jit(solution)/shard_map/all_to_all | solution.py:408
  50.9 0.8 constant_dynamic-slice_fusion.states
  51.6 8.5 %all-to-all-done.2.terms = bf16[8,8,2048]{2,1,0:T(8,128)(2,1)S(1)} async-done(((bf16[8,8,2048]{2,1,0:T(8,128)(2,1)}), bf16[8,8,2048]{2,1,0:T(8,128)(2,1)S(1)}, u32[]{:S(2)}, u32[]{:S(2)}) %all-to-all-start.2) | async-done | bytes 262176 | tf_op jit(solution)/shard_map/all_to_all | solution.py:408
  60.2 0.9 norm.1
  61.0 4.8 %all-to-all-start.3 = ((bf16[8,8,2048]{2,1,0:T(8,128)(2,1)}), bf16[8,8,2048]{2,1,0:T(8,128)(2,1)S(1)}, u32[]{:S(2)}, u32[]{:S(2)}) async-start(bf16[8,8,2048]{2,1,0:T(8,128)(2,1)} %get-tuple-element.21), calls=%async_computation.3 | async-start | bytes 524288 | tf_op jit(solution)/shard_map/all_to_all | solution.py:416
  65.8 0.6 multiply_reduce_fusion
  66.4 0.1 dynamic-slice_bitcast_fusion
  66.5 0.1 copy.23.own_docs
  66.6 0.1 slice_reduce_fusion
  66.7 0.1 tile.14
  66.8 7.7 %all-to-all-done.3 = bf16[8,8,2048]{2,1,0:T(8,128)(2,1)S(1)} async-done(((bf16[8,8,2048]{2,1,0:T(8,128)(2,1)}), bf16[8,8,2048]{2,1,0:T(8,128)(2,1)S(1)}, u32[]{:S(2)}, u32[]{:S(2)}) %all-to-all-start.3) | async-done | bytes 262176 | tf_op jit(solution)/shard_map/all_to_all | solution.py:416
  74.5 4.2 %feed.1 = f32[32,128]{1,0:T(8,128)} custom-call(bf16[64,2048]{1,0:T(8,128)(2,1)S(1)} %bitcast.12, bf16[2048,640]{1,0:T(8,128)(2,1)} %gate_weight.1, bf16[2048,640]{1,0:T(8,128)(2,1)} %up_weight.1, f32[1,640]{1,0:T(1,128)S(1)} %reshape.124.down_score, f32[64,1]{1,0:T(8,128)S(1)} %fusion.4.own_score, s32[64,1]{1,0:T(8,128)S(1)} %copy.23.own_docs), custom_call_target="tpu_custom_call" | custom-call | tf_op jit(solution)/shard_map/feed/pallas_call | solution.py:424
  78.7 5.4 %all-to-all-start.4 = ((f32[32,1,128]{2,1,0:T(1,128)}), f32[32,1,128]{2,1,0:T(1,128)S(1)}, u32[]{:S(2)}, u32[]{:S(2)}) async-start(f32[32,1,128]{2,1,0:T(1,128)} %bitcast.10), calls=%async_computation.4 | async-start | bytes 32768 | tf_op jit(solution)/shard_map/all_to_all | solution.py:429
  84.1 7.3 %all-to-all-done.4.terms = f32[32,1,128]{2,1,0:T(1,128)S(1)} async-done(((f32[32,1,128]{2,1,0:T(1,128)}), f32[32,1,128]{2,1,0:T(1,128)S(1)}, u32[]{:S(2)}, u32[]{:S(2)}) %all-to-all-start.4) | async-done | bytes 16416 | tf_op jit(solution)/shard_map/all_to_all | solution.py:429
  91.4 0.6 fold.1
  92.0 4.6 %all-to-all-start.5 = ((f32[8,1,128]{2,1,0:T(1,128)}), f32[8,1,128]{2,1,0:T(1,128)S(1)}, u32[]{:S(2)}, u32[]{:S(2)}) async-start(f32[8,1,128]{2,1,0:T(1,128)} %fold.1), calls=%async_computation.5 | async-start | bytes 8192 | tf_op jit(solution)/shard_map/all_to_all | solution.py:431
  96.7 0.2 convert_reduce_fusion
  96.9 6.1 %all-to-all-done.5 = f32[8,1,128]{2,1,0:T(1,128)S(1)} async-done(((f32[8,1,128]{2,1,0:T(1,128)}), f32[8,1,128]{2,1,0:T(1,128)S(1)}, u32[]{:S(2)}, u32[]{:S(2)}) %all-to-all-start.5) | async-done | bytes 4128 | tf_op jit(solution)/shard_map/all_to_all | solution.py:431
  103.0 0.5 slice_divide_fusion
  (11 shorter events, 0.1 us)
Async XLA Ops:
  2.4 9.5 %collective-permute-start.3 = (bf16[2,128,256]{2,1,0:T(8,128)(2,1)}, bf16[2,128,256]{2,1,0:T(8,128)(2,1)S(1)}, u32[]{:S(2)}, u32[]{:S(2)}) collective-permute-start(bf16[2,128,256]{2,1,0:T(8,128)(2,1)} %k0.1), channel_id=1, source_target_pairs={{0,4},{1,5},{2,6},{3,7},{4,0},{5,1},{6,2},{7,3},{8,12},{9,13},{10,... | collective-permute-start | bytes 393224 | tf_op jit(solution)/shard_map/ppermute | solution.py:338
  5.5 6.7 %collective-permute-start.5 = (bf16[2,128,256]{2,1,0:T(8,128)(2,1)}, bf16[2,128,256]{2,1,0:T(8,128)(2,1)S(1)}, u32[]{:S(2)}, u32[]{:S(2)}) collective-permute-start(bf16[2,128,256]{2,1,0:T(8,128)(2,1)} %v0.1), channel_id=1, source_target_pairs={{0,4},{1,5},{2,6},{3,7},{4,0},{5,1},{6,2},{7,3},{8,12},{9,13},{10,... | collective-permute-start | bytes 393224 | tf_op jit(solution)/shard_map/ppermute | solution.py:338
  6.0 17.4 %all-to-all-start = ((bf16[8,64,256]{2,1,0:T(8,128)(2,1)}), bf16[8,64,256]{2,1,0:T(8,128)(2,1)S(1)}, u32[]{:S(2)}, u32[]{:S(2)}) async-start(bf16[8,64,256]{2,1,0:T(8,128)(2,1)} %project.1), calls=%async_computation | async-start | bytes 524288 | tf_op jit(solution)/shard_map/all_to_all | solution.py:360
  11.4 5.6 %collective-permute-start = (bf16[2,128,256]{2,1,0:T(8,128)(2,1)}, bf16[2,128,256]{2,1,0:T(8,128)(2,1)S(1)}, u32[]{:S(2)}, u32[]{:S(2)}) collective-permute-start(bf16[2,128,256]{2,1,0:T(8,128)(2,1)} %k0.1), channel_id=1, source_target_pairs={{0,1},{1,0},{2,3},{3,2},{4,5},{5,4},{6,7},{7,6},{8,9},{9,8},{10,11... | collective-permute-start | bytes 393224 | tf_op jit(solution)/shard_map/ppermute | solution.py:338
  11.4 6.7 %collective-permute-start.1 = (bf16[2,128,256]{2,1,0:T(8,128)(2,1)}, bf16[2,128,256]{2,1,0:T(8,128)(2,1)S(1)}, u32[]{:S(2)}, u32[]{:S(2)}) collective-permute-start(bf16[2,128,256]{2,1,0:T(8,128)(2,1)} %v0.1), channel_id=1, source_target_pairs={{0,1},{1,0},{2,3},{3,2},{4,5},{5,4},{6,7},{7,6},{8,9},{9,8},{10,11... | collective-permute-start | bytes 393224 | tf_op jit(solution)/shard_map/ppermute | solution.py:338
  11.9 9.8 %collective-permute-start.4 = (bf16[2,128,256]{2,1,0:T(8,128)(2,1)S(1)}, bf16[2,128,256]{2,1,0:T(8,128)(2,1)S(1)}, u32[]{:S(2)}, u32[]{:S(2)}) collective-permute-start(bf16[2,128,256]{2,1,0:T(8,128)(2,1)S(1)} %collective-permute-done.3.k0), channel_id=1, source_target_pairs={{0,1},{1,0},{2,3},{3,2},{4,5},{5,4},{6,7},{7,6},{8,9},{9,8},{10,11... | collective-permute-start | bytes 393224 | tf_op jit(solution)/shard_map/ppermute | solution.py:338
  12.2 9.5 %collective-permute-start.6 = (bf16[2,128,256]{2,1,0:T(8,128)(2,1)S(1)}, bf16[2,128,256]{2,1,0:T(8,128)(2,1)S(1)}, u32[]{:S(2)}, u32[]{:S(2)}) collective-permute-start(bf16[2,128,256]{2,1,0:T(8,128)(2,1)S(1)} %collective-permute-done.5.v0), channel_id=1, source_target_pairs={{0,1},{1,0},{2,3},{3,2},{4,5},{5,4},{6,7},{7,6},{8,9},{9,8},{10,11... | collective-permute-start | bytes 393224 | tf_op jit(solution)/shard_map/ppermute | solution.py:338
  12.4 1.4 %collective-permute-start.2 = (s32[2,128]{1,0:T(2,128)}, s32[2,128]{1,0:T(2,128)S(1)}, u32[]{:S(2)}, u32[]{:S(2)}) collective-permute-start(s32[2,128]{1,0:T(2,128)} %b0.1), channel_id=1, source_target_pairs={{0,1},{1,0},{2,3},{3,2},{4,5},{5,4},{6,7},{7,6},{8,9},{9,8},{10,11... | collective-permute-start | bytes 3080 | tf_op jit(solution)/shard_map/ppermute | solution.py:338
  13.8 6.0 %collective-permute-start.7 = (s32[2,128]{1,0:T(2,128)}, s32[2,128]{1,0:T(2,128)S(1)}, u32[]{:S(2)}, u32[]{:S(2)}) collective-permute-start(s32[2,128]{1,0:T(2,128)} %b0.1), channel_id=1, source_target_pairs={{0,4},{1,5},{2,6},{3,7},{4,0},{5,1},{6,2},{7,3},{8,12},{9,13},{10,... | collective-permute-start | bytes 3080 | tf_op jit(solution)/shard_map/ppermute | solution.py:338
  17.0 4.7 %collective-permute-start.8 = (s32[2,128]{1,0:T(2,128)}, s32[2,128]{1,0:T(2,128)S(1)}, u32[]{:S(2)}, u32[]{:S(2)}) collective-permute-start(s32[2,128]{1,0:T(2,128)} %b0.1), channel_id=1, source_target_pairs={{0,5},{1,4},{2,7},{3,6},{4,1},{5,0},{6,3},{7,2},{8,13},{9,12},{10,... | collective-permute-start | bytes 3080 | tf_op jit(solution)/shard_map/ppermute | solution.py:338
  23.4 36.8 %copy-start = (f32[2048]{0:T(1024)S(1)}, f32[2048]{0:T(1024)}, u32[]{:S(2)}) copy-start(f32[2048]{0:T(1024)} %param.29) | copy-start | bytes 24580
  23.4 36.8 %copy-start.1 = (f32[2048]{0:T(1024)S(1)}, f32[2048]{0:T(1024)}, u32[]{:S(2)}) copy-start(f32[2048]{0:T(1024)} %param.25) | copy-start | bytes 24580
  27.3 38.5 %copy-start.2 = (bf16[640,2048]{1,0:T(8,128)(2,1)S(1)}, bf16[640,2048]{1,0:T(8,128)(2,1)}, u32[]{:S(2)}) copy-start(bf16[640,2048]{1,0:T(8,128)(2,1)} %param.28) | copy-start | bytes 7864324
  40.0 26.4 %copy-start.3 = (s32[2048]{0:T(1024)S(1)}, s32[2048]{0:T(1024)}, u32[]{:S(2)}) copy-start(s32[2048]{0:T(1024)} %param.32) | copy-start | bytes 24580
  42.3 17.9 %all-to-all-start.2 = ((bf16[8,8,2048]{2,1,0:T(8,128)(2,1)}), bf16[8,8,2048]{2,1,0:T(8,128)(2,1)S(1)}, u32[]{:S(2)}, u32[]{:S(2)}) async-start(bf16[8,8,2048]{2,1,0:T(8,128)(2,1)} %bitcast.5), calls=%async_computation.2 | async-start | bytes 524288 | tf_op jit(solution)/shard_map/all_to_all | solution.py:408
  61.0 13.5 %all-to-all-start.3 = ((bf16[8,8,2048]{2,1,0:T(8,128)(2,1)}), bf16[8,8,2048]{2,1,0:T(8,128)(2,1)S(1)}, u32[]{:S(2)}, u32[]{:S(2)}) async-start(bf16[8,8,2048]{2,1,0:T(8,128)(2,1)} %get-tuple-element.21), calls=%async_computation.3 | async-start | bytes 524288 | tf_op jit(solution)/shard_map/all_to_all | solution.py:416
  78.7 12.7 %all-to-all-start.4 = ((f32[32,1,128]{2,1,0:T(1,128)}), f32[32,1,128]{2,1,0:T(1,128)S(1)}, u32[]{:S(2)}, u32[]{:S(2)}) async-start(f32[32,1,128]{2,1,0:T(1,128)} %bitcast.10), calls=%async_computation.4 | async-start | bytes 32768 | tf_op jit(solution)/shard_map/all_to_all | solution.py:429
  92.0 10.9 %all-to-all-start.5 = ((f32[8,1,128]{2,1,0:T(1,128)}), f32[8,1,128]{2,1,0:T(1,128)S(1)}, u32[]{:S(2)}, u32[]{:S(2)}) async-start(f32[8,1,128]{2,1,0:T(1,128)} %fold.1), calls=%async_computation.5 | async-start | bytes 8192 | tf_op jit(solution)/shard_map/all_to_all | solution.py:431

commit v4 on v3

--- a/solution.py
+++ b/solution.py
@@ -27,18 +27,30 @@
     return first, second, third
 
 
-def project_kernel(states, gain, weight, out, states_here, gain_here, weight_here, arrivals):
-    pairs = ((states, states_here), (gain, gain_here), (weight, weight_here))
+def project_kernel(states, gain, weight, keys, buckets, out, payload, states_here, gain_here, weight_here, buckets_here,
+                   arrivals):
+    count = keys.shape[0]
+    pairs = (
+        (states, states_here),
+        (gain, gain_here),
+        (weight, weight_here),
+        (buckets, buckets_here),
+        (keys, payload.at[pl.ds(0, count)]),
+    )
     copies = [pltpu.make_async_copy(there, here, arrivals.at[i]) for i, (there, here) in enumerate(pairs)]
     for copy in copies:
         copy.start()
     copies[0].wait()
     copies[1].wait()
     normed = rms_scale(states_here[...], gain_here[...]).astype(BF)
+    copies[3].wait()
+    both = jnp.concatenate([buckets_here[0:1, :], buckets_here[1:2, :]], axis=1).astype(F32)
+    payload[count : count + 8, :] = jnp.broadcast_to(both, (8, both.shape[1])).astype(BF)
     copies[2].wait()
     queries = jnp.dot(normed, weight_here[...], preferred_element_type=F32).astype(BF)
     for chip in range(out.shape[0]):
         out[chip] = queries
+    copies[4].wait()
 
 
 def columns_kernel(rank, doc_query, doc_rows, extra, query_here, rows_here, arrivals):
@@ -81,17 +93,18 @@
     extra[...] = columns.T.astype(BF)
 
 
-def prepare_kernel(rank, k0, k1, v0, v1, b0, b1, bias_table, page_table, query_lengths, keys_aug, values_t,
-                   held, bucket_here, table_here, slots_here, lengths_here, info, arrivals, *, side):
-    pages, page_len, width = k0.shape
+def prepare_kernel(rank, k0, k1, v0, v1, bias_table, page_table, query_lengths, keys_aug, values_t, held, held_values,
+                   table_here, slots_here, lengths_here, info, arrivals, *, side, pages):
+    width, total = values_t.shape
+    page_len = total // (2 * pages)
+    keys = pages * page_len
     heads, bucket_count = bias_table.shape
     depth = width // heads
     slot_count = page_table.shape[0]
     max_pages = slot_count // NQ
     row_chips = 4
     pairs = [(page_table, slots_here), (query_lengths, lengths_here), (bias_table, table_here)]
-    pairs += [(b0, bucket_here.at[0]), (b1, bucket_here.at[1])]
-    pairs += [(cache, held.at[i]) for i, cache in enumerate((k0, k1, v0, v1))]
+    pairs += [(k0, held.at[0]), (k1, held.at[1]), (v0, held_values.at[0]), (v1, held_values.at[1])]
     copies = [pltpu.make_async_copy(there, here, arrivals.at[i]) for i, (there, here) in enumerate(pairs)]
     for copy in copies:
         copy.start()
@@ -120,7 +133,7 @@
             jnp.where(col == NQ + 1, a.astype(F32), jnp.where(col == NQ + 2, b.astype(F32), third)).astype(BF)
         )
     spread = jnp.concatenate(spreads, axis=1)
-    bucket_row = lax.broadcasted_iota(jnp.int32, (bucket_count, page_len), 0)
+    bucket_row = lax.broadcasted_iota(jnp.int32, (bucket_count, page_len), 0).astype(F32)
     slot = lax.broadcasted_iota(jnp.int32, (page_len, 128), 0)
     key_col = lax.broadcasted_iota(jnp.int32, (page_len, 128), 1) % 64
     mine = ((chip % row_chips // 2) * 2 + core) * pages
@@ -130,17 +143,18 @@
         for page in range(pages):
             place = (mine ^ ((2 * side + part) * pages)) + page
             span = pl.ds((part * pages + page) * page_len, page_len)
-            bucket = bucket_here[part, page : page + 1, :]
+            bucket = held[part, keys : keys + 8, page * page_len : (page + 1) * page_len].astype(F32)[0:1]
             onehot = (jnp.broadcast_to(bucket, bucket_row.shape) == bucket_row).astype(F32).astype(BF)
             bias = lax.dot_general(onehot, spread, (((0,), (0,)), ((), ())), preferred_element_type=F32)
             holder = jnp.where(slot < info[1, place], info[0, place], NQ)
             marks = (key_col == holder).astype(F32)
-            key = held[part, page].astype(F32)
+            key = held[part, page * page_len : (page + 1) * page_len, :].astype(F32)
             for h in range(heads):
                 keep = low if h % 2 == 0 else jnp.logical_not(low)
                 half = key[:, (h // 2) * 128 : (h // 2 + 1) * 128]
                 keys_aug[h, span, :] = jnp.where(keep, half, bias[:, h * 128 : (h + 1) * 128] + marks).astype(BF)
-            values_t[:, span] = held[2 + part, page].astype(F32).T.astype(BF)
+            value = held_values[part, page * page_len : (page + 1) * page_len, :]
+            values_t[:, span] = value.astype(F32).T.astype(BF)
 
 
 def attention_kernel(queries, keys_near, keys_far, values_near, values_far, extra, out, rows_aug):
@@ -195,9 +209,7 @@
             out[duo * 2 + which, 128:136, :] = jnp.concatenate(packed, axis=0).astype(BF)
 
 
-def combine_kernel(parts, out_weight, out, weight_here, arrival):
-    copy = pltpu.make_async_copy(out_weight, weight_here, arrival)
-    copy.start()
+def combine_kernel(parts, out_weight, out):
     chips = parts.shape[0]
     logs = []
     for chip in range(chips):
@@ -217,8 +229,7 @@
             sums[r] = sums[r] + share[r : r + 1] * parts[chip, r * 64 : (r + 1) * 64, :].astype(F32)
     joined = jnp.concatenate(sums, axis=0).T
     context = jnp.concatenate([joined[0:64], joined[64:128]], axis=1).astype(BF)
-    copy.wait()
-    out[...] = jnp.dot(context, weight_here[...], preferred_element_type=F32).astype(BF)
+    out[...] = jnp.dot(context, out_weight[...], preferred_element_type=F32).astype(BF)
 
 
 def norm_kernel(terms, states, gain, score_vector, out, score):
@@ -231,36 +242,49 @@
     score[...] = jnp.broadcast_to(jnp.sum(hidden * score_vector[...], axis=-1, keepdims=True), score.shape)
 
 
-def feed_kernel(rows, gate_weight, up_weight, down_score, own_score, own_docs, out, gate_here, up_here, arrivals):
-    steps = gate_here.shape[0]
+def down_kernel(weight, score_vector, out_weight, out, fetched, weight_here, arrivals):
+    copy = pltpu.make_async_copy(weight, weight_here, arrivals.at[0])
+    fetch = pltpu.make_async_copy(out_weight, fetched, arrivals.at[1])
+    fetch.start()
+    copy.start()
+    pieces = [piece.astype(F32) for piece in split_three(score_vector[...])]
+    rows = jnp.concatenate(pieces + [jnp.zeros((5, score_vector.shape[1]), F32)], axis=0).astype(BF)
+    copy.wait()
+    terms = lax.dot_general(rows, weight_here[...], (((1,), (1,)), ((), ())), preferred_element_type=F32)
+    out[...] = terms[0:1] + terms[1:2] + terms[2:3]
+    fetch.wait()
+
+
+def fetch_kernel(weight, out, arrival):
+    copy = pltpu.make_async_copy(weight, out, arrival)
+    copy.start()
+    copy.wait()
+
+
+def feed_kernel(rows, gate_weight, up_weight, down_score, own_score, own_docs, out, up_here, arrivals):
+    steps = up_here.shape[0]
     size = rows.shape[1] // steps
-    copies = []
-    for i in range(steps):
-        for j, (there, here) in enumerate(((gate_weight, gate_here), (up_weight, up_here))):
-            copies.append(
-                pltpu.make_async_copy(there.at[pl.ds(i * size, size)], here.at[i], arrivals.at[2 * i + j])
-            )
+    copies = [
+        pltpu.make_async_copy(up_weight.at[pl.ds(i * size, size)], up_here.at[i], arrivals.at[i]) for i in range(steps)
+    ]
     for copy in copies:
         copy.start()
-    gate = jnp.zeros((rows.shape[0], gate_weight.shape[1]), F32)
-    upper = gate
+    gate = jnp.dot(rows[...], gate_weight[...], preferred_element_type=F32)
+    gate = jax.nn.gelu(gate, approximate=True)
+    upper = jnp.zeros_like(gate)
     for i in range(steps):
-        part = rows[:, i * size : (i + 1) * size]
-        copies[2 * i].wait()
-        gate += jnp.dot(part, gate_here[i], preferred_element_type=F32)
-        copies[2 * i + 1].wait()
-        upper += jnp.dot(part, up_here[i], preferred_element_type=F32)
-    middle = (jax.nn.gelu(gate, approximate=True) * upper).astype(BF).astype(F32)
+        copies[i].wait()
+        upper += jnp.dot(rows[:, i * size : (i + 1) * size], up_here[i], preferred_element_type=F32)
+    middle = (gate * upper).astype(BF).astype(F32)
     tok_score = jnp.sum(middle * down_score[...], axis=-1, keepdims=True) + own_score[...]
     docs = own_docs[...]
     doc_dev = DOCS // out.shape[0]
     lane = lax.broadcasted_iota(jnp.int32, (docs.shape[0], 128), 1)
     holder = (docs // doc_dev == lane).astype(F32).astype(BF)
     placed = jnp.where(docs % doc_dev == lane, tok_score, 0.0)
-    sums = jnp.zeros((128, 128), F32)
-    for piece in split_three(placed):
-        sums += lax.dot_general(holder, piece, (((0,), (0,)), ((), ())), preferred_element_type=F32)
-    out[...] = sums[0 : out.shape[0]]
+    pieces = jnp.concatenate([piece.astype(F32) for piece in split_three(placed)], axis=1).astype(BF)
+    sums = lax.dot_general(holder, pieces, (((0,), (0,)), ((), ())), preferred_element_type=F32)[0 : out.shape[0]]
+    out[...] = sums[:, 0:128] + sums[:, 128:256] + sums[:, 256:384]
 
 
 def fold_kernel(terms, out):
@@ -337,25 +361,33 @@
     def swap(value, pairs):
         return lax.ppermute(value, "page", pairs)
 
-    far_swap = [(i, i ^ 5) for i in range(page_size)]
-    copies = call(
-        project_kernel, "project", shape((group, tok_dev, local_width), BF), [hbm()] * 3,
+    keys_held = local_pages * page_len
+    copies, payload = call(
+        project_kernel,
+        "project",
+        [shape((group, tok_dev, local_width), BF), shape((keys_held + 8, local_width), BF)],
+        [hbm()] * 5,
         [
             pltpu.VMEM((tok_dev, model), BF),
             pltpu.VMEM((1, model), F32),
             pltpu.VMEM((model, local_width), BF),
-            pltpu.SemaphoreType.DMA((3,)),
+            pltpu.VMEM((local_pages, page_len), jnp.int32),
+            pltpu.SemaphoreType.DMA((5,)),
         ],
-    )(in_hbm(doc_states), in_hbm(gain_attn.reshape(1, model)), in_hbm(query_weight))
-    sent_keys, sent_values, copies = lax.optimization_barrier((cache_keys, cache_values, copies))
-    keys_side = swap(sent_keys, side_swap)
-    values_side = swap(sent_values, side_swap)
-    keys_core = swap(cache_keys, core_swap)
-    values_core = swap(cache_values, core_swap)
-    bucket_core = swap(rel_bucket, core_swap)
-    bucket_side = swap(rel_bucket, side_swap)
-    bucket_far = swap(rel_bucket, far_swap)
-    keys_far = swap(keys_side, core_swap)
+    )(
+        in_hbm(doc_states),
+        in_hbm(gain_attn.reshape(1, model)),
+        in_hbm(query_weight),
+        in_hbm(cache_keys.reshape(keys_held, local_width)),
+        in_hbm(rel_bucket),
+    )
+    values_own = cache_values.reshape(keys_held, local_width)
+    values_sent, copies = lax.optimization_barrier((values_own, copies))
+    payload_side = swap(payload, side_swap)
+    values_side = swap(values_sent, side_swap)
+    payload_core = swap(payload, core_swap)
+    values_core = swap(values_own, core_swap)
+    payload_far = swap(payload_side, core_swap)
     values_far = swap(values_side, core_swap)
     gathered = lax.all_to_all(copies, "page", 0, 0, axis_index_groups=groups, tiled=True)
 
@@ -371,26 +403,25 @@
     )(rank, in_hbm(doc_query.reshape(1, -1)), in_hbm(doc_rows))
     key_count = 2 * local_pages * page_len
 
-    def prepared(side, caches, buckets):
+    def prepared(side, caches):
         return call(
-            functools.partial(prepare_kernel, side=side),
+            functools.partial(prepare_kernel, side=side, pages=local_pages),
             "prepare",
             [shape((local_heads, key_count, 128), BF), shape((local_width, key_count), BF)],
-            [smem()] + [anywhere()] * 6 + [hbm()] * 3,
+            [smem()] + [anywhere()] * 4 + [hbm()] * 3,
             [
-                pltpu.VMEM((4, local_pages, page_len, local_width), BF),
-                pltpu.VMEM((2, local_pages, page_len), jnp.int32),
+                pltpu.VMEM((2,) + payload.shape, BF),
+                pltpu.VMEM((2,) + values_own.shape, BF),
                 pltpu.VMEM(bias_table.T.shape, F32),
                 pltpu.SMEM(page_table.shape, jnp.int32),
                 pltpu.SMEM(query_lengths.shape, jnp.int32),
                 pltpu.SMEM((2, 4 * local_pages + 1), jnp.int32),
-                pltpu.SemaphoreType.DMA((9,)),
+                pltpu.SemaphoreType.DMA((7,)),
             ],
-        )(rank, *caches, *buckets, in_hbm(bias_table.T), in_hbm(page_table), in_hbm(query_lengths))
-
-    near = (in_hbm(cache_keys), keys_core, in_hbm(cache_values), values_core)
-    keys_near, values_near = prepared(0, near, (in_hbm(rel_bucket), bucket_core))
-    keys_away, values_away = prepared(1, (keys_side, keys_far, values_side, values_far), (bucket_side, bucket_far))
+        )(rank, *caches, in_hbm(bias_table.T), in_hbm(page_table), in_hbm(query_lengths))
+
+    keys_near, values_near = prepared(0, (payload, payload_core, in_hbm(values_own), values_core))
+    keys_away, values_away = prepared(1, (payload_side, payload_far, values_side, values_far))
     partials = call(
         attention_kernel,
         "attention",
@@ -398,11 +429,17 @@
         [vmem()] * 6,
         [pltpu.VMEM((local_heads, group * tok_dev, 128), BF)],
     )(gathered, keys_near, keys_away, values_near, values_away, extra)
+    partials, down_weight, late_weight = lax.optimization_barrier((partials, wo_ffn, out_weight))
+    hidden_units = wi_gate.shape[1]
+    down_score, fetched = call(
+        down_kernel,
+        "down",
+        [shape((1, hidden_units), F32), shape(out_weight.shape, BF)],
+        [hbm(), vmem(), hbm()],
+        [pltpu.VMEM(wo_ffn.shape, BF), pltpu.SemaphoreType.DMA((2,))],
+    )(in_hbm(down_weight), score_vector.reshape(1, model), in_hbm(late_weight))
     returned = lax.all_to_all(partials, "page", 0, 0, axis_index_groups=groups, tiled=True)
-    projected = call(
-        combine_kernel, "combine", shape((tok_dev, model), BF), [vmem(), hbm()],
-        [pltpu.VMEM((local_width, model), BF), pltpu.SemaphoreType.DMA(())],
-    )(returned, in_hbm(out_weight))
+    projected = call(combine_kernel, "combine", shape((tok_dev, model), BF), [vmem()] * 2)(returned, fetched)
 
     own = tok_dev // head_size
     terms = lax.all_to_all(projected.reshape(head_size, own, model), "head", 0, 0, tiled=True)
@@ -413,18 +450,20 @@
         [shape((head_size, own, model), BF), shape((own, 128), F32)],
         [vmem()] * 4,
     )(terms, own_states, gain_ffn.reshape(1, model), score_vector.reshape(1, model))
+    spread, late_gate = lax.optimization_barrier((spread, wi_gate))
+    gate_here = call(
+        fetch_kernel, "fetch", shape(wi_gate.shape, BF), [hbm()], [pltpu.SemaphoreType.DMA(())]
+    )(in_hbm(late_gate))
     rows = lax.all_to_all(spread, "head", 0, 0, tiled=True).reshape(tok_dev, model)
-    down_score = jnp.sum(wo_ffn.astype(F32) * score_vector, axis=-1)
     token = jnp.arange(tok_dev, dtype=jnp.int32)[:, None]
     own_score = jnp.where(token // own == head_rank, jnp.tile(hidden_score[:, :1], (head_size, 1)), 0.0)
     own_docs = lax.dynamic_slice_in_dim(doc_of_token, page_rank * tok_dev, tok_dev, 0)[:, None]
     doc_dev = doc_query.shape[0] // page_size
     steps = 4
-    weight_slices = pltpu.VMEM((steps, model // steps, wi_gate.shape[1]), BF)
     doc_sums = call(
-        feed_kernel, "feed", shape((page_size, 128), F32), [vmem(), hbm(), hbm(), vmem(), vmem(), vmem()],
-        [weight_slices, weight_slices, pltpu.SemaphoreType.DMA((2 * steps,))],
-    )(rows, in_hbm(wi_gate), in_hbm(wi_up), down_score.reshape(1, -1), own_score, own_docs)
+        feed_kernel, "feed", shape((page_size, 128), F32), [vmem(), vmem(), hbm(), vmem(), vmem(), vmem()],
+        [pltpu.VMEM((steps, model // steps, hidden_units), BF), pltpu.SemaphoreType.DMA((steps,))],
+    )(rows, gate_here, in_hbm(wi_up), down_score, own_score, own_docs)
     doc_sums = doc_sums.reshape(page_size, 1, 128)
     arrived = lax.all_to_all(doc_sums, "page", 0, 0, tiled=True)
     pooled = call(fold_kernel, "fold", shape((head_size, 1, 128), F32), [vmem()])(arrived)

time: 105 us -> 98.3 us (0.936)
  blocking collectives: 12.6 us -> 0 us
  Pallas kernels: 18.6 us -> 22.1 us
  waiting for transfers between devices: 32.8 us -> 35.4 us
    all_to_all x1 -> x0, blocking collectives: 12.6 us -> none  [per_device(): lax.all_to_all(partials, 'page', 0, 0, axis_index_groups=groups, tiled=True)]
    all_to_all x0 -> x1, waiting for transfers between devices: none -> 4.81 us  [per_device(): lax.all_to_all(partials, 'page', 0, 0, axis_index_groups=groups, tiled=True)]
    all_to_all x0 -> x1, starting transfers between devices: none -> 3.96 us  [per_device(): lax.all_to_all(partials, 'page', 0, 0, axis_index_groups=groups, tiled=True)]
    ppermute x9 -> x6, starting transfers between devices: 7.95 us -> 4.47 us  [swap(): return lax.ppermute(value, 'page', pairs)]
    ppermute x9 -> x6, waiting for transfers between devices: 3.21 us -> 0.17 us  [swap(): return lax.ppermute(value, 'page', pairs)]
    pallas_call x5 -> x7, Pallas kernels: 12.2 us -> 15 us  [the longest x1 3.51 us: per_device(): call(feed_kernel, 'feed', shape((page_size, 128), F32), [vmem(), vmem(),...]
    all_to_all x1, waiting for transfers between devices: 0.01 us -> 1.75 us  [per_device(): lax.all_to_all(copies, 'page', 0, 0, axis_index_groups=groups, tiled=True)]
    all_to_all x1, waiting for transfers between devices: 7.7 us -> 6.51 us  [per_device(): lax.all_to_all(spread, 'head', 0, 0, tiled=True).reshape(tok_dev, model)]
  transfers between devices with their start and end apart: 14 -> 12, of which waited for: 7 -> 7; matrix products, arithmetic and copies ran while one was open for 2% -> 1% of each run, Pallas kernels for 4% -> 9%
where the time goes in v4:
time: 98.3 us; the launch traced here: 96.4 us
  starting transfers between devices  36.9 us (38%)
  waiting for transfers between devices  35.4 us (36%)
  Pallas kernels  22.1 us (22%)
  local copies, waits for them, and re-layouts  1.15 us (1%)
    all_to_all x1, waiting for transfers between devices, per_device(): lax.all_to_all(projected.reshape(head_size, own, model), 'head', 0, 0, ti...  8.78 us
    all_to_all x1, starting transfers between devices, per_device(): lax.all_to_all(projected.reshape(head_size, own, model), 'head', 0, 0, ti...  8.58 us
    all_to_all x1, waiting for transfers between devices, per_device(): arrived = lax.all_to_all(doc_sums, 'page', 0, 0, tiled=True)  7.34 us
    all_to_all x1, waiting for transfers between devices, per_device(): lax.all_to_all(spread, 'head', 0, 0, tiled=True).reshape(tok_dev, model)  6.51 us
    all_to_all x1, waiting for transfers between devices, per_device(): lax.all_to_all(pooled, 'head', 0, 0, tiled=True)  6.04 us
    all_to_all x1, starting transfers between devices, per_device(): lax.all_to_all(copies, 'page', 0, 0, axis_index_groups=groups, tiled=True)  5.4 us
    all_to_all x1, starting transfers between devices, per_device(): arrived = lax.all_to_all(doc_sums, 'page', 0, 0, tiled=True)  5.12 us
    all_to_all x1, waiting for transfers between devices, per_device(): lax.all_to_all(partials, 'page', 0, 0, axis_index_groups=groups, tiled=True)  4.81 us
  transfers between devices with their start and end apart: 12, of which 7 were waited for; matrix products, arithmetic and copies ran while one was open for 1% of the time, Pallas kernels for 9%

profile of v4, /device:TPU:32, one launch (start us, length us, event | category | flops | bytes accessed | tf_op | source)
XLA Modules:
  0.0 96.4 jit_solution(4019347667630960637)
XLA Ops:
  0.0 2.4 %project.1 = (bf16[8,64,256]{2,1,0:T(8,128)(2,1)}, bf16[264,256]{1,0:T(8,128)(2,1)S(1)}) custom-call(bf16[64,2048]{1,0:T(8,128)(2,1)} %states.1, f32[1,2048]{1,0:T(1,128)} %bitcast.23, bf16[2048,256]{1,0:T(8,128)(2,1)} %weight.1, bf16[256,256]{1,0:T(8,128)(2,1)} %bitcast.18, s32[2,128]{1,0:T(2,128)} %buckets.1), custom_call_target="tpu_custom_call" | custom-call | tf_op jit(solution)/shard_map/project/pallas_call | solution.py:365
  2.4 0.0 copy-start
  2.4 3.1 %collective-permute-start.2 = (bf16[264,256]{1,0:T(8,128)(2,1)S(1)}, bf16[264,256]{1,0:T(8,128)(2,1)S(1)}, u32[]{:S(2)}, u32[]{:S(2)}) collective-permute-start(bf16[264,256]{1,0:T(8,128)(2,1)S(1)} %get-tuple-element.24.k0), channel_id=1, source_target_pairs={{0,4},{1,5},{2,6},{3,7},{4,0},{5,1},{6,2},{7,3},{8,12},{9,13},{10,... | collective-permute-start | bytes 405512 | tf_op jit(solution)/shard_map/ppermute | solution.py:362
  5.5 0.5 collective-permute-start.4
  6.0 5.4 %all-to-all-start = ((bf16[8,64,256]{2,1,0:T(8,128)(2,1)}), bf16[8,64,256]{2,1,0:T(8,128)(2,1)S(1)}, u32[]{:S(2)}, u32[]{:S(2)}) async-start(bf16[8,64,256]{2,1,0:T(8,128)(2,1)} %get-tuple-element.23), calls=%async_computation | async-start | bytes 524288 | tf_op jit(solution)/shard_map/all_to_all | solution.py:392
  11.4 0.0 collective-permute-start
  11.4 0.0 collective-permute-done.2.k0
  11.4 0.5 collective-permute-start.3
  11.9 0.1 collective-permute-start.1
  12.0 0.2 collective-permute-done.4.v0
  12.2 0.3 collective-permute-start.5
  12.4 1.1 %columns.1.extra = bf16[512,128]{1,0:T(8,128)(2,1)S(1)} custom-call(s32[1]{0:T(128)} %bitcast.3.rank, s32[1,256]{1,0:T(1,128)} %bitcast.26, s32[16,128]{1,0:T(8,128)} %bitcast.22), custom_call_target="tpu_custom_call" | custom-call | tf_op jit(solution)/shard_map/columns/pallas_call | solution.py:396
  13.5 0.0 collective-permute-done.1.v1
  13.5 0.0 collective-permute-done.k1
  13.5 1.7 %prepare.2 = (bf16[4,512,128]{2,1,0:T(8,128)(2,1)S(1)}, bf16[256,512]{1,0:T(8,128)(2,1)S(1)}) custom-call(s32[1]{0:T(128)} %bitcast.3.rank, bf16[264,256]{1,0:T(8,128)(2,1)S(1)} %get-tuple-element.24.k0, bf16[264,256]{1,0:T(8,128)(2,1)S(1)} %collective-permute-done.k1, bf16[256,256]{1,0:T(8,128)(2,1)} %bitcast.21, ...), custom_call_target="tpu_custom_call" | custom-call | tf_op jit(solution)/shard_map/prepare/pallas_call | solution.py:407
  15.2 0.0 collective-permute-done.5.v1
  15.2 0.0 collective-permute-done.3.k1
  15.3 1.7 %prepare.3 = (bf16[4,512,128]{2,1,0:T(8,128)(2,1)S(1)}, bf16[256,512]{1,0:T(8,128)(2,1)S(1)}) custom-call(s32[1]{0:T(128)} %bitcast.3.rank, bf16[264,256]{1,0:T(8,128)(2,1)S(1)} %collective-permute-done.2.k0, bf16[264,256]{1,0:T(8,128)(2,1)S(1)} %collective-permute-done.3.k1, bf16[256,256]{1,0:T(8,128)(2,1)S(1)} %collective-permute-done.4.v0, ...), custom_call_target="tpu_custom_call" | custom-call | tf_op jit(solution)/shard_map/prepare/pallas_call | solution.py:407
  16.9 1.7 %all-to-all-done.queries = bf16[8,64,256]{2,1,0:T(8,128)(2,1)S(1)} async-done(((bf16[8,64,256]{2,1,0:T(8,128)(2,1)}), bf16[8,64,256]{2,1,0:T(8,128)(2,1)S(1)}, u32[]{:S(2)}, u32[]{:S(2)}) %all-to-all-start) | async-done | bytes 262176 | tf_op jit(solution)/shard_map/all_to_all | solution.py:392
  18.7 4.5 %attention.1 = bf16[8,136,128]{2,1,0:T(8,128)(2,1)} custom-call(bf16[8,64,256]{2,1,0:T(8,128)(2,1)S(1)} %all-to-all-done.queries, bf16[4,512,128]{2,1,0:T(8,128)(2,1)S(1)} %get-tuple-element.25.keys_near, bf16[4,512,128]{2,1,0:T(8,128)(2,1)S(1)} %get-tuple-element.27.keys_far, bf16[256,512]{1,0:T(8,128)(2,1)S(1)} %get-tuple-element.28.values_near, ...), custom_call_target="tpu_custom_call" | custom-call | tf_op jit(solution)/shard_map/attention/pallas_call | solution.py:425
  23.2 4.0 %all-to-all-start.1 = ((bf16[8,136,128]{2,1,0:T(8,128)(2,1)}), bf16[8,136,128]{2,1,0:T(8,128)(2,1)S(1)}, u32[]{:S(2)}, u32[]{:S(2)}) async-start(bf16[8,136,128]{2,1,0:T(8,128)(2,1)} %attention.1), calls=%async_computation.1 | async-start | bytes 557056 | tf_op jit(solution)/shard_map/all_to_all | solution.py:441
  27.2 0.0 copy-done
  27.2 0.0 copy-start.1
  27.2 0.0 copy-start.2
  27.2 2.9 %down.1 = (f32[1,640]{1,0:T(1,128)S(1)}, bf16[256,2048]{1,0:T(8,128)(2,1)S(1)}) custom-call(bf16[640,2048]{1,0:T(8,128)(2,1)} %weight.2, f32[1,2048]{1,0:T(1,128)S(1)} %bitcast.15, bf16[256,2048]{1,0:T(8,128)(2,1)} %out_weight), custom_call_target="tpu_custom_call" | custom-call | tf_op jit(solution)/shard_map/down/pallas_call | solution.py:434
  30.1 4.8 %all-to-all-done.1.parts = bf16[8,136,128]{2,1,0:T(8,128)(2,1)S(1)} async-done(((bf16[8,136,128]{2,1,0:T(8,128)(2,1)}), bf16[8,136,128]{2,1,0:T(8,128)(2,1)S(1)}, u32[]{:S(2)}, u32[]{:S(2)}) %all-to-all-start.1) | async-done | bytes 278560 | tf_op jit(solution)/shard_map/all_to_all | solution.py:441
  34.9 1.1 %combine.1 = bf16[64,2048]{1,0:T(8,128)(2,1)} custom-call(bf16[8,136,128]{2,1,0:T(8,128)(2,1)S(1)} %all-to-all-done.1.parts, bf16[256,2048]{1,0:T(8,128)(2,1)S(1)} %get-tuple-element.33.out_weight), custom_call_target="tpu_custom_call" | custom-call | tf_op jit(solution)/shard_map/combine/pallas_call | solution.py:442
  36.0 8.6 %all-to-all-start.2 = ((bf16[8,8,2048]{2,1,0:T(8,128)(2,1)}), bf16[8,8,2048]{2,1,0:T(8,128)(2,1)S(1)}, u32[]{:S(2)}, u32[]{:S(2)}) async-start(bf16[8,8,2048]{2,1,0:T(8,128)(2,1)} %bitcast.8), calls=%async_computation.2 | async-start | bytes 524288 | tf_op jit(solution)/shard_map/all_to_all | solution.py:445
  44.6 0.8 constant_dynamic-slice_fusion.states
  45.4 8.8 %all-to-all-done.2.terms = bf16[8,8,2048]{2,1,0:T(8,128)(2,1)S(1)} async-done(((bf16[8,8,2048]{2,1,0:T(8,128)(2,1)}), bf16[8,8,2048]{2,1,0:T(8,128)(2,1)S(1)}, u32[]{:S(2)}, u32[]{:S(2)}) %all-to-all-start.2) | async-done | bytes 262176 | tf_op jit(solution)/shard_map/all_to_all | solution.py:445
  54.2 0.0 copy-done.1
  54.2 0.8 norm.1
  55.0 4.8 %all-to-all-start.3 = ((bf16[8,8,2048]{2,1,0:T(8,128)(2,1)}), bf16[8,8,2048]{2,1,0:T(8,128)(2,1)S(1)}, u32[]{:S(2)}, u32[]{:S(2)}) async-start(bf16[8,8,2048]{2,1,0:T(8,128)(2,1)} %get-tuple-element.35), calls=%async_computation.3 | async-start | bytes 524288 | tf_op jit(solution)/shard_map/all_to_all | solution.py:457
  59.8 0.0 copy-done.2
  59.8 0.1 dynamic-slice_bitcast_fusion
  59.8 0.1 copy.23.own_docs
  59.9 0.1 slice_reduce_fusion
  60.1 0.1 tile.14
  60.1 1.8 %fetch.1.gate_weight = bf16[2048,640]{1,0:T(8,128)(2,1)S(1)} custom-call(bf16[2048,640]{1,0:T(8,128)(2,1)} %weight.3), custom_call_target="tpu_custom_call" | custom-call | tf_op jit(solution)/shard_map/fetch/pallas_call | solution.py:454
  61.9 6.5 %all-to-all-done.3 = bf16[8,8,2048]{2,1,0:T(8,128)(2,1)S(1)} async-done(((bf16[8,8,2048]{2,1,0:T(8,128)(2,1)}), bf16[8,8,2048]{2,1,0:T(8,128)(2,1)S(1)}, u32[]{:S(2)}, u32[]{:S(2)}) %all-to-all-start.3) | async-done | bytes 262176 | tf_op jit(solution)/shard_map/all_to_all | solution.py:457
  68.4 3.5 %feed.1 = f32[32,128]{1,0:T(8,128)} custom-call(bf16[64,2048]{1,0:T(8,128)(2,1)S(1)} %bitcast.14, bf16[2048,640]{1,0:T(8,128)(2,1)S(1)} %fetch.1.gate_weight, bf16[2048,640]{1,0:T(8,128)(2,1)} %up_weight.1, f32[1,640]{1,0:T(1,128)S(1)} %get-tuple-element.37.down_score, f32[64,1]{1,0:T(8,128)S(1)} %fusion.4.own_score, s32[64,1]{1,0:T(8,128)S(1)} %copy.23.own_docs), custom_call_target="tpu_custom_call" | custom-call | tf_op jit(solution)/shard_map/feed/pallas_call | solution.py:463
  71.9 5.1 %all-to-all-start.4 = ((f32[32,1,128]{2,1,0:T(1,128)}), f32[32,1,128]{2,1,0:T(1,128)S(1)}, u32[]{:S(2)}, u32[]{:S(2)}) async-start(f32[32,1,128]{2,1,0:T(1,128)} %bitcast.12), calls=%async_computation.4 | async-start | bytes 32768 | tf_op jit(solution)/shard_map/all_to_all | solution.py:468
  77.1 7.3 %all-to-all-done.4.terms = f32[32,1,128]{2,1,0:T(1,128)S(1)} async-done(((f32[32,1,128]{2,1,0:T(1,128)}), f32[32,1,128]{2,1,0:T(1,128)S(1)}, u32[]{:S(2)}, u32[]{:S(2)}) %all-to-all-start.4) | async-done | bytes 16416 | tf_op jit(solution)/shard_map/all_to_all | solution.py:468
  84.4 0.6 fold.1
  85.1 4.6 %all-to-all-start.5 = ((f32[8,1,128]{2,1,0:T(1,128)}), f32[8,1,128]{2,1,0:T(1,128)S(1)}, u32[]{:S(2)}, u32[]{:S(2)}) async-start(f32[8,1,128]{2,1,0:T(1,128)} %fold.1), calls=%async_computation.5 | async-start | bytes 8192 | tf_op jit(solution)/shard_map/all_to_all | solution.py:470
  89.6 0.2 convert_reduce_fusion
  89.8 6.0 %all-to-all-done.5 = f32[8,1,128]{2,1,0:T(1,128)S(1)} async-done(((f32[8,1,128]{2,1,0:T(1,128)}), f32[8,1,128]{2,1,0:T(1,128)S(1)}, u32[]{:S(2)}, u32[]{:S(2)}) %all-to-all-start.5) | async-done | bytes 4128 | tf_op jit(solution)/shard_map/all_to_all | solution.py:470
  95.9 0.5 slice_divide_fusion
  (4 shorter events, 0.0 us)
Async XLA Ops:
  2.4 24.8 %copy-start = (f32[2048]{0:T(1024)S(1)}, f32[2048]{0:T(1024)}, u32[]{:S(2)}) copy-start(f32[2048]{0:T(1024)} %param.29) | copy-start | bytes 24580
  2.4 9.0 %collective-permute-start.2 = (bf16[264,256]{1,0:T(8,128)(2,1)S(1)}, bf16[264,256]{1,0:T(8,128)(2,1)S(1)}, u32[]{:S(2)}, u32[]{:S(2)}) collective-permute-start(bf16[264,256]{1,0:T(8,128)(2,1)S(1)} %get-tuple-element.24.k0), channel_id=1, source_target_pairs={{0,4},{1,5},{2,6},{3,7},{4,0},{5,1},{6,2},{7,3},{8,12},{9,13},{10,... | collective-permute-start | bytes 405512 | tf_op jit(solution)/shard_map/ppermute | solution.py:362
  5.5 6.7 %collective-permute-start.4 = (bf16[256,256]{1,0:T(8,128)(2,1)}, bf16[256,256]{1,0:T(8,128)(2,1)S(1)}, u32[]{:S(2)}, u32[]{:S(2)}) collective-permute-start(bf16[256,256]{1,0:T(8,128)(2,1)} %bitcast.19), channel_id=1, source_target_pairs={{0,4},{1,5},{2,6},{3,7},{4,0},{5,1},{6,2},{7,3},{8,12},{9,13},{10,... | collective-permute-start | bytes 393224 | tf_op jit(solution)/shard_map/ppermute | solution.py:362
  6.0 12.7 %all-to-all-start = ((bf16[8,64,256]{2,1,0:T(8,128)(2,1)}), bf16[8,64,256]{2,1,0:T(8,128)(2,1)S(1)}, u32[]{:S(2)}, u32[]{:S(2)}) async-start(bf16[8,64,256]{2,1,0:T(8,128)(2,1)} %get-tuple-element.23), calls=%async_computation | async-start | bytes 524288 | tf_op jit(solution)/shard_map/all_to_all | solution.py:392
  11.4 2.1 %collective-permute-start = (bf16[264,256]{1,0:T(8,128)(2,1)S(1)}, bf16[264,256]{1,0:T(8,128)(2,1)S(1)}, u32[]{:S(2)}, u32[]{:S(2)}) collective-permute-start(bf16[264,256]{1,0:T(8,128)(2,1)S(1)} %get-tuple-element.24.k0), channel_id=1, source_target_pairs={{0,1},{1,0},{2,3},{3,2},{4,5},{5,4},{6,7},{7,6},{8,9},{9,8},{10,11... | collective-permute-start | bytes 405512 | tf_op jit(solution)/shard_map/ppermute | solution.py:362
  11.4 3.8 %collective-permute-start.3 = (bf16[264,256]{1,0:T(8,128)(2,1)S(1)}, bf16[264,256]{1,0:T(8,128)(2,1)S(1)}, u32[]{:S(2)}, u32[]{:S(2)}) collective-permute-start(bf16[264,256]{1,0:T(8,128)(2,1)S(1)} %collective-permute-done.2.k0), channel_id=1, source_target_pairs={{0,1},{1,0},{2,3},{3,2},{4,5},{5,4},{6,7},{7,6},{8,9},{9,8},{10,11... | collective-permute-start | bytes 405512 | tf_op jit(solution)/shard_map/ppermute | solution.py:362
  11.9 1.6 %collective-permute-start.1 = (bf16[256,256]{1,0:T(8,128)(2,1)}, bf16[256,256]{1,0:T(8,128)(2,1)S(1)}, u32[]{:S(2)}, u32[]{:S(2)}) collective-permute-start(bf16[256,256]{1,0:T(8,128)(2,1)} %bitcast.20), channel_id=1, source_target_pairs={{0,1},{1,0},{2,3},{3,2},{4,5},{5,4},{6,7},{7,6},{8,9},{9,8},{10,11... | collective-permute-start | bytes 393224 | tf_op jit(solution)/shard_map/ppermute | solution.py:362
  12.2 3.1 %collective-permute-start.5 = (bf16[256,256]{1,0:T(8,128)(2,1)S(1)}, bf16[256,256]{1,0:T(8,128)(2,1)S(1)}, u32[]{:S(2)}, u32[]{:S(2)}) collective-permute-start(bf16[256,256]{1,0:T(8,128)(2,1)S(1)} %collective-permute-done.4.v0), channel_id=1, source_target_pairs={{0,1},{1,0},{2,3},{3,2},{4,5},{5,4},{6,7},{7,6},{8,9},{9,8},{10,11... | collective-permute-start | bytes 393224 | tf_op jit(solution)/shard_map/ppermute | solution.py:362
  23.2 11.7 %all-to-all-start.1 = ((bf16[8,136,128]{2,1,0:T(8,128)(2,1)}), bf16[8,136,128]{2,1,0:T(8,128)(2,1)S(1)}, u32[]{:S(2)}, u32[]{:S(2)}) async-start(bf16[8,136,128]{2,1,0:T(8,128)(2,1)} %attention.1), calls=%async_computation.1 | async-start | bytes 557056 | tf_op jit(solution)/shard_map/all_to_all | solution.py:441
  27.2 27.0 %copy-start.1 = (f32[2048]{0:T(1024)S(1)}, f32[2048]{0:T(1024)}, u32[]{:S(2)}) copy-start(f32[2048]{0:T(1024)} %param.25) | copy-start | bytes 24580
  27.2 32.6 %copy-start.2 = (s32[2048]{0:T(1024)S(1)}, s32[2048]{0:T(1024)}, u32[]{:S(2)}) copy-start(s32[2048]{0:T(1024)} %param.32) | copy-start | bytes 24580
  36.0 18.1 %all-to-all-start.2 = ((bf16[8,8,2048]{2,1,0:T(8,128)(2,1)}), bf16[8,8,2048]{2,1,0:T(8,128)(2,1)S(1)}, u32[]{:S(2)}, u32[]{:S(2)}) async-start(bf16[8,8,2048]{2,1,0:T(8,128)(2,1)} %bitcast.8), calls=%async_computation.2 | async-start | bytes 524288 | tf_op jit(solution)/shard_map/all_to_all | solution.py:445
  55.0 13.4 %all-to-all-start.3 = ((bf16[8,8,2048]{2,1,0:T(8,128)(2,1)}), bf16[8,8,2048]{2,1,0:T(8,128)(2,1)S(1)}, u32[]{:S(2)}, u32[]{:S(2)}) async-start(bf16[8,8,2048]{2,1,0:T(8,128)(2,1)} %get-tuple-element.35), calls=%async_computation.3 | async-start | bytes 524288 | tf_op jit(solution)/shard_map/all_to_all | solution.py:457
  71.9 12.5 %all-to-all-start.4 = ((f32[32,1,128]{2,1,0:T(1,128)}), f32[32,1,128]{2,1,0:T(1,128)S(1)}, u32[]{:S(2)}, u32[]{:S(2)}) async-start(f32[32,1,128]{2,1,0:T(1,128)} %bitcast.12), calls=%async_computation.4 | async-start | bytes 32768 | tf_op jit(solution)/shard_map/all_to_all | solution.py:468
  85.1 10.8 %all-to-all-start.5 = ((f32[8,1,128]{2,1,0:T(1,128)}), f32[8,1,128]{2,1,0:T(1,128)S(1)}, u32[]{:S(2)}, u32[]{:S(2)}) async-start(f32[8,1,128]{2,1,0:T(1,128)} %fold.1), calls=%async_computation.5 | async-start | bytes 8192 | tf_op jit(solution)/shard_map/all_to_all | solution.py:470

commit v5 on v4

--- a/solution.py
+++ b/solution.py
@@ -27,8 +27,8 @@
     return first, second, third
 
 
-def project_kernel(states, gain, weight, keys, buckets, out, payload, states_here, gain_here, weight_here, buckets_here,
-                   arrivals):
+def project_kernel(states, gain, weight, keys, values, buckets, out, payload, states_here, gain_here, weight_here,
+                   buckets_here, arrivals):
     count = keys.shape[0]
     pairs = (
         (states, states_here),
@@ -36,6 +36,7 @@
         (weight, weight_here),
         (buckets, buckets_here),
         (keys, payload.at[pl.ds(0, count)]),
+        (values, payload.at[pl.ds(count + 8, count)]),
     )
     copies = [pltpu.make_async_copy(there, here, arrivals.at[i]) for i, (there, here) in enumerate(pairs)]
     for copy in copies:
@@ -51,15 +52,30 @@
     for chip in range(out.shape[0]):
         out[chip] = queries
     copies[4].wait()
-
-
-def columns_kernel(rank, doc_query, doc_rows, extra, query_here, rows_here, arrivals):
+    copies[5].wait()
+
+
+def near_kernel(rank, first, second, third, bias_table, page_table, query_lengths, doc_query, doc_rows, keys_aug, values_t,
+                extra, table_here, slots_here, lengths_here, info, arrivals, query_here, rows_here, doc_arrivals, *, pages):
     copies = [
-        pltpu.make_async_copy(doc_query, query_here, arrivals.at[0]),
-        pltpu.make_async_copy(doc_rows, rows_here, arrivals.at[1]),
+        pltpu.make_async_copy(doc_query, query_here, doc_arrivals.at[0]),
+        pltpu.make_async_copy(doc_rows, rows_here, doc_arrivals.at[1]),
     ]
     for copy in copies:
         copy.start()
+
+    def columns():
+        for copy in copies:
+            copy.wait()
+        query_columns(rank, query_here, rows_here, extra)
+
+    prepare_kernel(
+        rank, first, second, third, bias_table, page_table, query_lengths, keys_aug, values_t, table_here, slots_here,
+        lengths_here, info, arrivals, side=0, pages=pages, meanwhile=columns,
+    )
+
+
+def query_columns(rank, doc_query, doc_rows, extra):
     tokens = extra.shape[0]
     tok_dev = doc_rows.shape[1] // 2
     row_chips = 4
@@ -69,11 +85,9 @@
     doc_count = doc_query.shape[1]
     left = lax.broadcasted_iota(jnp.int32, (1, 128), 1) < tok_dev
     doc_id = lax.broadcasted_iota(jnp.int32, (doc_count, 128), 0)
-    for copy in copies:
-        copy.wait()
     blocks = []
     for y in range(tokens // (2 * tok_dev)):
-        two = rows_here[pl.ds(y * row_chips + pair % row_chips, 2), :]
+        two = doc_rows[pl.ds(y * row_chips + pair % row_chips, 2), :]
         turned = pltpu.roll(two, tok_dev, 1)
         row = jnp.where(
             left,
@@ -82,7 +96,7 @@
         )
         blocks.append((doc_id == row).astype(F32).astype(BF))
     member = jnp.concatenate(blocks, axis=1)
-    asked = jnp.broadcast_to(query_here[...].astype(F32), (128, doc_count)).astype(BF)
+    asked = jnp.broadcast_to(doc_query[...].astype(F32), (128, doc_count)).astype(BF)
     tok_query = jnp.dot(asked, member, preferred_element_type=F32)
     mark = lax.broadcasted_iota(jnp.int32, (128, tokens), 0) % 64
     columns = jnp.where(
@@ -93,8 +107,8 @@
     extra[...] = columns.T.astype(BF)
 
 
-def prepare_kernel(rank, k0, k1, v0, v1, bias_table, page_table, query_lengths, keys_aug, values_t, held, held_values,
-                   table_here, slots_here, lengths_here, info, arrivals, *, side, pages):
+def prepare_kernel(rank, first, second, third, bias_table, page_table, query_lengths, keys_aug, values_t, table_here,
+                   slots_here, lengths_here, info, arrivals, *, side, pages, meanwhile=None):
     width, total = values_t.shape
     page_len = total // (2 * pages)
     keys = pages * page_len
@@ -104,10 +118,11 @@
     max_pages = slot_count // NQ
     row_chips = 4
     pairs = [(page_table, slots_here), (query_lengths, lengths_here), (bias_table, table_here)]
-    pairs += [(k0, held.at[0]), (k1, held.at[1]), (v0, held_values.at[0]), (v1, held_values.at[1])]
     copies = [pltpu.make_async_copy(there, here, arrivals.at[i]) for i, (there, here) in enumerate(pairs)]
     for copy in copies:
         copy.start()
+    if meanwhile is not None:
+        meanwhile()
     core = rank[0] % 2
     chip = rank[0] // 2
     base = (chip // row_chips * row_chips + chip % 2) * 2 * pages
@@ -128,32 +143,31 @@
     spreads = []
     for h in range(heads):
         a, b, c = split_three(jnp.broadcast_to(table[:, h : h + 1], (bucket_count, 128)))
-        third = jnp.where(col == NQ + 3, c.astype(F32), 0.0)
+        last = jnp.where(col == NQ + 3, c.astype(F32), 0.0)
         spreads.append(
-            jnp.where(col == NQ + 1, a.astype(F32), jnp.where(col == NQ + 2, b.astype(F32), third)).astype(BF)
+            jnp.where(col == NQ + 1, a.astype(F32), jnp.where(col == NQ + 2, b.astype(F32), last)).astype(BF)
         )
     spread = jnp.concatenate(spreads, axis=1)
     bucket_row = lax.broadcasted_iota(jnp.int32, (bucket_count, page_len), 0).astype(F32)
     slot = lax.broadcasted_iota(jnp.int32, (page_len, 128), 0)
     key_col = lax.broadcasted_iota(jnp.int32, (page_len, 128), 1) % 64
     mine = ((chip % row_chips // 2) * 2 + core) * pages
-    for copy in copies[3:]:
-        copy.wait()
-    for part in range(2):
+    sources = ((first, first, keys + 8), (second, third, 0))
+    for part, (key_rows, value_rows, offset) in enumerate(sources):
         for page in range(pages):
             place = (mine ^ ((2 * side + part) * pages)) + page
             span = pl.ds((part * pages + page) * page_len, page_len)
-            bucket = held[part, keys : keys + 8, page * page_len : (page + 1) * page_len].astype(F32)[0:1]
+            bucket = key_rows[keys : keys + 8, page * page_len : (page + 1) * page_len].astype(F32)[0:1]
             onehot = (jnp.broadcast_to(bucket, bucket_row.shape) == bucket_row).astype(F32).astype(BF)
             bias = lax.dot_general(onehot, spread, (((0,), (0,)), ((), ())), preferred_element_type=F32)
             holder = jnp.where(slot < info[1, place], info[0, place], NQ)
             marks = (key_col == holder).astype(F32)
-            key = held[part, page * page_len : (page + 1) * page_len, :].astype(F32)
+            key = key_rows[page * page_len : (page + 1) * page_len, :].astype(F32)
             for h in range(heads):
                 keep = low if h % 2 == 0 else jnp.logical_not(low)
                 half = key[:, (h // 2) * 128 : (h // 2 + 1) * 128]
                 keys_aug[h, span, :] = jnp.where(keep, half, bias[:, h * 128 : (h + 1) * 128] + marks).astype(BF)
-            value = held_values[part, page * page_len : (page + 1) * page_len, :]
+            value = value_rows[offset + page * page_len : offset + (page + 1) * page_len, :]
             values_t[:, span] = value.astype(F32).T.astype(BF)
 
 
@@ -170,12 +184,19 @@
         rows_aug[h] = jnp.where(keep, half, extra[...].astype(F32)).astype(BF)
     sums = []
     logs = []
-    for h in range(heads):
-        span = slice(h * depth, (h + 1) * depth)
-        scores = [
+
+    def score(h):
+        return [
             lax.dot_general(keys[h], rows_aug[h], (((1,), (1,)), ((), ())), preferred_element_type=F32)
             for keys in (keys_near, keys_far)
         ]
+
+    ready = score(0)
+    for h in range(heads):
+        span = slice(h * depth, (h + 1) * depth)
+        scores = ready
+        if h + 1 < heads:
+            ready = score(h + 1)
         top = jnp.maximum(
             jnp.max(scores[0], axis=0, keepdims=True), jnp.max(scores[1], axis=0, keepdims=True)
         )
@@ -269,6 +290,10 @@
     ]
     for copy in copies:
         copy.start()
+    docs = own_docs[...]
+    doc_dev = DOCS // out.shape[0]
+    lane = lax.broadcasted_iota(jnp.int32, (docs.shape[0], 128), 1)
+    holder = (docs // doc_dev == lane).astype(F32).astype(BF)
     gate = jnp.dot(rows[...], gate_weight[...], preferred_element_type=F32)
     gate = jax.nn.gelu(gate, approximate=True)
     upper = jnp.zeros_like(gate)
@@ -277,10 +302,6 @@
         upper += jnp.dot(rows[:, i * size : (i + 1) * size], up_here[i], preferred_element_type=F32)
     middle = (gate * upper).astype(BF).astype(F32)
     tok_score = jnp.sum(middle * down_score[...], axis=-1, keepdims=True) + own_score[...]
-    docs = own_docs[...]
-    doc_dev = DOCS // out.shape[0]
-    lane = lax.broadcasted_iota(jnp.int32, (docs.shape[0], 128), 1)
-    holder = (docs // doc_dev == lane).astype(F32).astype(BF)
     placed = jnp.where(docs % doc_dev == lane, tok_score, 0.0)
     pieces = jnp.concatenate([piece.astype(F32) for piece in split_three(placed)], axis=1).astype(BF)
     sums = lax.dot_general(holder, pieces, (((0,), (0,)), ((), ())), preferred_element_type=F32)[0 : out.shape[0]]
@@ -365,63 +386,63 @@
     copies, payload = call(
         project_kernel,
         "project",
-        [shape((group, tok_dev, local_width), BF), shape((keys_held + 8, local_width), BF)],
-        [hbm()] * 5,
+        [shape((group, tok_dev, local_width), BF), shape((2 * keys_held + 8, local_width), BF)],
+        [hbm()] * 6,
         [
             pltpu.VMEM((tok_dev, model), BF),
             pltpu.VMEM((1, model), F32),
             pltpu.VMEM((model, local_width), BF),
             pltpu.VMEM((local_pages, page_len), jnp.int32),
-            pltpu.SemaphoreType.DMA((5,)),
+            pltpu.SemaphoreType.DMA((6,)),
         ],
     )(
         in_hbm(doc_states),
         in_hbm(gain_attn.reshape(1, model)),
         in_hbm(query_weight),
         in_hbm(cache_keys.reshape(keys_held, local_width)),
+        in_hbm(cache_values.reshape(keys_held, local_width)),
         in_hbm(rel_bucket),
     )
     values_own = cache_values.reshape(keys_held, local_width)
-    values_sent, copies = lax.optimization_barrier((values_own, copies))
     payload_side = swap(payload, side_swap)
-    values_side = swap(values_sent, side_swap)
-    payload_core = swap(payload, core_swap)
+    keys_core = swap(payload[0 : keys_held + 8], core_swap)
     values_core = swap(values_own, core_swap)
-    payload_far = swap(payload_side, core_swap)
-    values_far = swap(values_side, core_swap)
+    keys_far = swap(payload_side[0 : keys_held + 8], core_swap)
+    values_far = swap(payload_side[keys_held + 8 :], core_swap)
     gathered = lax.all_to_all(copies, "page", 0, 0, axis_index_groups=groups, tiled=True)
 
     rank = page_rank.reshape(1)
     doc_rows = doc_of_token.reshape(-1, 2 * tok_dev)
-    extra = call(
-        columns_kernel, "columns", shape((group * tok_dev, 128), BF), [smem()] + [hbm()] * 2,
-        [
+    key_count = 2 * local_pages * page_len
+
+    shapes = [shape((local_heads, key_count, 128), BF), shape((local_width, key_count), BF)]
+    scratch = [
+        pltpu.VMEM(bias_table.T.shape, F32),
+        pltpu.SMEM(page_table.shape, jnp.int32),
+        pltpu.SMEM(query_lengths.shape, jnp.int32),
+        pltpu.SMEM((2, 4 * local_pages + 1), jnp.int32),
+        pltpu.SemaphoreType.DMA((3,)),
+    ]
+    tables = (in_hbm(bias_table.T), in_hbm(page_table), in_hbm(query_lengths))
+    keys_near, values_near, extra = call(
+        functools.partial(near_kernel, pages=local_pages),
+        "near",
+        shapes + [shape((group * tok_dev, 128), BF)],
+        [smem()] + [vmem()] * 3 + [hbm()] * 5,
+        scratch
+        + [
             pltpu.VMEM((1, doc_query.shape[0]), jnp.int32),
             pltpu.VMEM(doc_rows.shape, jnp.int32),
             pltpu.SemaphoreType.DMA((2,)),
         ],
-    )(rank, in_hbm(doc_query.reshape(1, -1)), in_hbm(doc_rows))
-    key_count = 2 * local_pages * page_len
-
-    def prepared(side, caches):
-        return call(
-            functools.partial(prepare_kernel, side=side, pages=local_pages),
-            "prepare",
-            [shape((local_heads, key_count, 128), BF), shape((local_width, key_count), BF)],
-            [smem()] + [anywhere()] * 4 + [hbm()] * 3,
-            [
-                pltpu.VMEM((2,) + payload.shape, BF),
-                pltpu.VMEM((2,) + values_own.shape, BF),
-                pltpu.VMEM(bias_table.T.shape, F32),
-                pltpu.SMEM(page_table.shape, jnp.int32),
-                pltpu.SMEM(query_lengths.shape, jnp.int32),
-                pltpu.SMEM((2, 4 * local_pages + 1), jnp.int32),
-                pltpu.SemaphoreType.DMA((7,)),
-            ],
-        )(rank, *caches, in_hbm(bias_table.T), in_hbm(page_table), in_hbm(query_lengths))
-
-    keys_near, values_near = prepared(0, (payload, payload_core, in_hbm(values_own), values_core))
-    keys_away, values_away = prepared(1, (payload_side, payload_far, values_side, values_far))
+    )(rank, payload, keys_core, values_core, *tables, in_hbm(doc_query.reshape(1, -1)), in_hbm(doc_rows))
+    keys_away, values_away = call(
+        functools.partial(prepare_kernel, side=1, pages=local_pages),
+        "away",
+        shapes,
+        [smem()] + [vmem()] * 3 + [hbm()] * 3,
+        scratch,
+    )(rank, payload_side, keys_far, values_far, *tables)
     partials = call(
         attention_kernel,
         "attention",

time: 98.3 us -> 98.7 us (level)
  waiting for transfers between devices: 35.4 us -> 37.3 us
  Pallas kernels: 22.1 us -> 20.6 us
    ppermute x6 -> x5, waiting for transfers between devices: 0.17 us -> 3.02 us  [swap(): return lax.ppermute(value, 'page', pairs)]
    all_to_all x1, waiting for transfers between devices: 1.75 us -> 0.01 us  [per_device(): lax.all_to_all(copies, 'page', 0, 0, axis_index_groups=groups, tiled=True)]
    all_to_all x1, starting transfers between devices: 3.96 us -> 5.5 us  [per_device(): lax.all_to_all(partials, 'page', 0, 0, axis_index_groups=groups, tiled=True)]
    pallas_call x3 -> x2, Pallas kernels: 4.44 us -> 3.5 us  [the longest x1 1.95 us: per_device(): call(functools.partial(near_kernel, pages=local_pages), 'near', shapes +...]
    ppermute x6 -> x5, starting transfers between devices: 4.47 us -> 3.98 us  [swap(): return lax.ppermute(value, 'page', pairs)]
  transfers between devices with their start and end apart: 12 -> 11, of which waited for: 7 -> 7; matrix products, arithmetic and copies ran while one was open for 1% -> 1% of each run, Pallas kernels for 9% -> 8%
where the time goes in v5:
time: 98.7 us; the launch traced here: 96.8 us
  waiting for transfers between devices  37.3 us (38%)
  starting transfers between devices  36.8 us (37%)
  Pallas kernels  20.6 us (21%)
  local copies, waits for them, and re-layouts  1.18 us (1%)
    all_to_all x1, waiting for transfers between devices, per_device(): lax.all_to_all(projected.reshape(head_size, own, model), 'head', 0, 0, ti...  9.01 us
    all_to_all x1, starting transfers between devices, per_device(): lax.all_to_all(projected.reshape(head_size, own, model), 'head', 0, 0, ti...  8.57 us
    all_to_all x1, waiting for transfers between devices, per_device(): arrived = lax.all_to_all(doc_sums, 'page', 0, 0, tiled=True)  7.34 us
    all_to_all x1, waiting for transfers between devices, per_device(): lax.all_to_all(spread, 'head', 0, 0, tiled=True).reshape(tok_dev, model)  6.9 us
    all_to_all x1, waiting for transfers between devices, per_device(): lax.all_to_all(pooled, 'head', 0, 0, tiled=True)  6.04 us
    all_to_all x1, starting transfers between devices, per_device(): lax.all_to_all(partials, 'page', 0, 0, axis_index_groups=groups, tiled=True)  5.5 us
    all_to_all x1, waiting for transfers between devices, per_device(): lax.all_to_all(partials, 'page', 0, 0, axis_index_groups=groups, tiled=True)  5 us
    all_to_all x1, starting transfers between devices, per_device(): arrived = lax.all_to_all(doc_sums, 'page', 0, 0, tiled=True)  4.94 us
  transfers between devices with their start and end apart: 11, of which 7 were waited for; matrix products, arithmetic and copies ran while one was open for 1% of the time, Pallas kernels for 8%

profile of v5, /device:TPU:32, one launch (start us, length us, event | category | flops | bytes accessed | tf_op | source)
XLA Modules:
  0.0 96.8 jit_solution(5518336486148106435)
XLA Ops:
  0.0 0.0 copy-start.2
  0.0 2.4 %project.1 = (bf16[8,64,256]{2,1,0:T(8,128)(2,1)}, bf16[520,256]{1,0:T(8,128)(2,1)S(1)}) custom-call(bf16[64,2048]{1,0:T(8,128)(2,1)} %states.1, f32[1,2048]{1,0:T(1,128)} %bitcast.22, bf16[2048,256]{1,0:T(8,128)(2,1)} %weight.1, bf16[256,256]{1,0:T(8,128)(2,1)} %bitcast.18, bf16[256,256]{1,0:T(8,128)(2,1)} %bitcast.19, s32[2,128]{1,0:T(2,128)} %buckets.1), custom_call_target="tpu_custom_call" | custom-call | tf_op jit(solution)/shard_map/project/pallas_call | solution.py:386
  2.4 0.0 copy-start
  2.4 3.1 %collective-permute-start.2 = (bf16[520,256]{1,0:T(8,128)(2,1)S(1)}, bf16[520,256]{1,0:T(8,128)(2,1)S(1)}, u32[]{:S(2)}, u32[]{:S(2)}) collective-permute-start(bf16[520,256]{1,0:T(8,128)(2,1)S(1)} %get-tuple-element.22.first), channel_id=1, source_target_pairs={{0,4},{1,5},{2,6},{3,7},{4,0},{5,1},{6,2},{7,3},{8,12},{9,13},{10,... | collective-permute-start | bytes 798728 | tf_op jit(solution)/shard_map/ppermute | solution.py:383
  5.5 4.5 %all-to-all-start = ((bf16[8,64,256]{2,1,0:T(8,128)(2,1)}), bf16[8,64,256]{2,1,0:T(8,128)(2,1)S(1)}, u32[]{:S(2)}, u32[]{:S(2)}) async-start(bf16[8,64,256]{2,1,0:T(8,128)(2,1)} %get-tuple-element.21), calls=%async_computation | async-start | bytes 524288 | tf_op jit(solution)/shard_map/all_to_all | solution.py:412
  10.1 0.1 collective-permute-start
  10.2 2.2 %collective-permute-done.2.first = bf16[520,256]{1,0:T(8,128)(2,1)S(1)} collective-permute-done((bf16[520,256]{1,0:T(8,128)(2,1)S(1)}, bf16[520,256]{1,0:T(8,128)(2,1)S(1)}, u32[]{:S(2)}, u32[]{:S(2)}) %collective-permute-start.2) | collective-permute-done | bytes 266272 | tf_op jit(solution)/shard_map/ppermute | solution.py:383
  12.4 0.1 collective-permute-start.3
  12.5 0.0 copy-done.2
  12.5 0.5 collective-permute-start.1
  13.0 0.2 collective-permute-start.4
  13.2 0.8 collective-permute-done.1.third
  14.0 0.0 collective-permute-done.second
  14.0 2.0 %near.1 = (bf16[4,512,128]{2,1,0:T(8,128)(2,1)S(1)}, bf16[256,512]{1,0:T(8,128)(2,1)S(1)}, bf16[512,128]{1,0:T(8,128)(2,1)S(1)}) custom-call(s32[1]{0:T(128)} %bitcast.3.rank, bf16[520,256]{1,0:T(8,128)(2,1)S(1)} %get-tuple-element.22.first, bf16[264,256]{1,0:T(8,128)(2,1)S(1)} %collective-permute-done.second, ...), custom_call_target="tpu_custom_call" | custom-call | tf_op jit(solution)/shard_map/near/pallas_call | solution.py:427
  15.9 0.0 collective-permute-done.4.third
  16.0 0.0 collective-permute-done.3.second
  16.0 1.5 %away.1 = (bf16[4,512,128]{2,1,0:T(8,128)(2,1)S(1)}, bf16[256,512]{1,0:T(8,128)(2,1)S(1)}) custom-call(s32[1]{0:T(128)} %bitcast.3.rank, bf16[520,256]{1,0:T(8,128)(2,1)S(1)} %collective-permute-done.2.first, bf16[264,256]{1,0:T(8,128)(2,1)S(1)} %collective-permute-done.3.second, bf16[256,256]{1,0:T(8,128)(2,1)S(1)} %collective-permute-done.4.third, ...), custom_call_target="tpu_custom_call" | custom-call | tf_op jit(solution)/shard_map/away/pallas_call | solution.py:439
  17.5 0.0 all-to-all-done.queries
  17.5 3.9 %attention.1 = bf16[8,136,128]{2,1,0:T(8,128)(2,1)} custom-call(bf16[8,64,256]{2,1,0:T(8,128)(2,1)S(1)} %all-to-all-done.queries, bf16[4,512,128]{2,1,0:T(8,128)(2,1)S(1)} %get-tuple-element.23.keys_near, bf16[4,512,128]{2,1,0:T(8,128)(2,1)S(1)} %get-tuple-element.24.keys_far, bf16[256,512]{1,0:T(8,128)(2,1)S(1)} %get-tuple-element.25.values_near, ...), custom_call_target="tpu_custom_call" | custom-call | tf_op jit(solution)/shard_map/attention/pallas_call | solution.py:446
  21.5 5.5 %all-to-all-start.1 = ((bf16[8,136,128]{2,1,0:T(8,128)(2,1)}), bf16[8,136,128]{2,1,0:T(8,128)(2,1)S(1)}, u32[]{:S(2)}, u32[]{:S(2)}) async-start(bf16[8,136,128]{2,1,0:T(8,128)(2,1)} %attention.1), calls=%async_computation.1 | async-start | bytes 557056 | tf_op jit(solution)/shard_map/all_to_all | solution.py:462
  27.0 0.0 copy-done
  27.0 0.0 copy-start.1
  27.0 0.0 copy-start.3
  27.0 2.9 %down.1 = (f32[1,640]{1,0:T(1,128)S(1)}, bf16[256,2048]{1,0:T(8,128)(2,1)S(1)}) custom-call(bf16[640,2048]{1,0:T(8,128)(2,1)} %weight.2, f32[1,2048]{1,0:T(1,128)S(1)} %bitcast.15, bf16[256,2048]{1,0:T(8,128)(2,1)} %out_weight), custom_call_target="tpu_custom_call" | custom-call | tf_op jit(solution)/shard_map/down/pallas_call | solution.py:455
  29.9 5.0 %all-to-all-done.1.parts = bf16[8,136,128]{2,1,0:T(8,128)(2,1)S(1)} async-done(((bf16[8,136,128]{2,1,0:T(8,128)(2,1)}), bf16[8,136,128]{2,1,0:T(8,128)(2,1)S(1)}, u32[]{:S(2)}, u32[]{:S(2)}) %all-to-all-start.1) | async-done | bytes 278560 | tf_op jit(solution)/shard_map/all_to_all | solution.py:462
  34.9 1.1 %combine.1 = bf16[64,2048]{1,0:T(8,128)(2,1)} custom-call(bf16[8,136,128]{2,1,0:T(8,128)(2,1)S(1)} %all-to-all-done.1.parts, bf16[256,2048]{1,0:T(8,128)(2,1)S(1)} %get-tuple-element.31.out_weight), custom_call_target="tpu_custom_call" | custom-call | tf_op jit(solution)/shard_map/combine/pallas_call | solution.py:463
  36.0 8.6 %all-to-all-start.2 = ((bf16[8,8,2048]{2,1,0:T(8,128)(2,1)}), bf16[8,8,2048]{2,1,0:T(8,128)(2,1)S(1)}, u32[]{:S(2)}, u32[]{:S(2)}) async-start(bf16[8,8,2048]{2,1,0:T(8,128)(2,1)} %bitcast.8), calls=%async_computation.2 | async-start | bytes 524288 | tf_op jit(solution)/shard_map/all_to_all | solution.py:466
  44.6 0.8 constant_dynamic-slice_fusion.states
  45.3 9.0 %all-to-all-done.2.terms = bf16[8,8,2048]{2,1,0:T(8,128)(2,1)S(1)} async-done(((bf16[8,8,2048]{2,1,0:T(8,128)(2,1)}), bf16[8,8,2048]{2,1,0:T(8,128)(2,1)S(1)}, u32[]{:S(2)}, u32[]{:S(2)}) %all-to-all-start.2) | async-done | bytes 262176 | tf_op jit(solution)/shard_map/all_to_all | solution.py:466
  54.3 0.0 copy-done.1
  54.3 0.8 norm.1
  55.2 4.8 %all-to-all-start.3 = ((bf16[8,8,2048]{2,1,0:T(8,128)(2,1)}), bf16[8,8,2048]{2,1,0:T(8,128)(2,1)S(1)}, u32[]{:S(2)}, u32[]{:S(2)}) async-start(bf16[8,8,2048]{2,1,0:T(8,128)(2,1)} %get-tuple-element.33), calls=%async_computation.3 | async-start | bytes 524288 | tf_op jit(solution)/shard_map/all_to_all | solution.py:478
  60.0 0.0 copy-done.3
  60.0 0.1 dynamic-slice_bitcast_fusion
  60.0 0.1 copy.23.own_docs
  60.1 0.1 slice_reduce_fusion
  60.3 0.1 tile.14
  60.3 1.8 %fetch.1.gate_weight = bf16[2048,640]{1,0:T(8,128)(2,1)S(1)} custom-call(bf16[2048,640]{1,0:T(8,128)(2,1)} %weight.3), custom_call_target="tpu_custom_call" | custom-call | tf_op jit(solution)/shard_map/fetch/pallas_call | solution.py:475
  62.1 6.9 %all-to-all-done.3 = bf16[8,8,2048]{2,1,0:T(8,128)(2,1)S(1)} async-done(((bf16[8,8,2048]{2,1,0:T(8,128)(2,1)}), bf16[8,8,2048]{2,1,0:T(8,128)(2,1)S(1)}, u32[]{:S(2)}, u32[]{:S(2)}) %all-to-all-start.3) | async-done | bytes 262176 | tf_op jit(solution)/shard_map/all_to_all | solution.py:478
  69.0 3.5 %feed.1 = f32[32,128]{1,0:T(8,128)} custom-call(bf16[64,2048]{1,0:T(8,128)(2,1)S(1)} %bitcast.14, bf16[2048,640]{1,0:T(8,128)(2,1)S(1)} %fetch.1.gate_weight, bf16[2048,640]{1,0:T(8,128)(2,1)} %up_weight.1, f32[1,640]{1,0:T(1,128)S(1)} %get-tuple-element.35.down_score, f32[64,1]{1,0:T(8,128)S(1)} %fusion.4.own_score, s32[64,1]{1,0:T(8,128)S(1)} %copy.23.own_docs), custom_call_target="tpu_custom_call" | custom-call | tf_op jit(solution)/shard_map/feed/pallas_call | solution.py:484
  72.5 4.9 %all-to-all-start.4 = ((f32[32,1,128]{2,1,0:T(1,128)}), f32[32,1,128]{2,1,0:T(1,128)S(1)}, u32[]{:S(2)}, u32[]{:S(2)}) async-start(f32[32,1,128]{2,1,0:T(1,128)} %bitcast.12), calls=%async_computation.4 | async-start | bytes 32768 | tf_op jit(solution)/shard_map/all_to_all | solution.py:489
  77.5 7.3 %all-to-all-done.4.terms = f32[32,1,128]{2,1,0:T(1,128)S(1)} async-done(((f32[32,1,128]{2,1,0:T(1,128)}), f32[32,1,128]{2,1,0:T(1,128)S(1)}, u32[]{:S(2)}, u32[]{:S(2)}) %all-to-all-start.4) | async-done | bytes 16416 | tf_op jit(solution)/shard_map/all_to_all | solution.py:489
  84.8 0.6 fold.1
  85.5 4.6 %all-to-all-start.5 = ((f32[8,1,128]{2,1,0:T(1,128)}), f32[8,1,128]{2,1,0:T(1,128)S(1)}, u32[]{:S(2)}, u32[]{:S(2)}) async-start(f32[8,1,128]{2,1,0:T(1,128)} %fold.1), calls=%async_computation.5 | async-start | bytes 8192 | tf_op jit(solution)/shard_map/all_to_all | solution.py:491
  90.0 0.2 convert_reduce_fusion
  90.2 6.0 %all-to-all-done.5 = f32[8,1,128]{2,1,0:T(1,128)S(1)} async-done(((f32[8,1,128]{2,1,0:T(1,128)}), f32[8,1,128]{2,1,0:T(1,128)S(1)}, u32[]{:S(2)}, u32[]{:S(2)}) %all-to-all-start.5) | async-done | bytes 4128 | tf_op jit(solution)/shard_map/all_to_all | solution.py:491
  96.3 0.5 slice_divide_fusion
  (7 shorter events, 0.1 us)
Async XLA Ops:
  0.0 12.5 %copy-start.2 = (bf16[2,128,256]{2,1,0:T(8,128)(2,1)S(1)}, bf16[2,128,256]{2,1,0:T(8,128)(2,1)}, u32[]{:S(2)}) copy-start(bf16[2,128,256]{2,1,0:T(8,128)(2,1)} %param.21) | copy-start | bytes 393220
  2.4 24.6 %copy-start = (f32[2048]{0:T(1024)S(1)}, f32[2048]{0:T(1024)}, u32[]{:S(2)}) copy-start(f32[2048]{0:T(1024)} %param.29) | copy-start | bytes 24580
  2.4 9.9 %collective-permute-start.2 = (bf16[520,256]{1,0:T(8,128)(2,1)S(1)}, bf16[520,256]{1,0:T(8,128)(2,1)S(1)}, u32[]{:S(2)}, u32[]{:S(2)}) collective-permute-start(bf16[520,256]{1,0:T(8,128)(2,1)S(1)} %get-tuple-element.22.first), channel_id=1, source_target_pairs={{0,4},{1,5},{2,6},{3,7},{4,0},{5,1},{6,2},{7,3},{8,12},{9,13},{10,... | collective-permute-start | bytes 798728 | tf_op jit(solution)/shard_map/ppermute | solution.py:383
  5.5 12.0 %all-to-all-start = ((bf16[8,64,256]{2,1,0:T(8,128)(2,1)}), bf16[8,64,256]{2,1,0:T(8,128)(2,1)S(1)}, u32[]{:S(2)}, u32[]{:S(2)}) async-start(bf16[8,64,256]{2,1,0:T(8,128)(2,1)} %get-tuple-element.21), calls=%async_computation | async-start | bytes 524288 | tf_op jit(solution)/shard_map/all_to_all | solution.py:412
  10.1 3.9 %collective-permute-start = (bf16[264,256]{1,0:T(8,128)(2,1)S(1)}, bf16[264,256]{1,0:T(8,128)(2,1)S(1)}, u32[]{:S(2)}, u32[]{:S(2)}) collective-permute-start(bf16[264,256]{1,0:T(8,128)(2,1)S(1)} %slice.15), channel_id=1, source_target_pairs={{0,1},{1,0},{2,3},{3,2},{4,5},{5,4},{6,7},{7,6},{8,9},{9,8},{10,11... | collective-permute-start | bytes 405512 | tf_op jit(solution)/shard_map/ppermute | solution.py:383
  12.4 3.6 %collective-permute-start.3 = (bf16[264,256]{1,0:T(8,128)(2,1)S(1)}, bf16[264,256]{1,0:T(8,128)(2,1)S(1)}, u32[]{:S(2)}, u32[]{:S(2)}) collective-permute-start(bf16[264,256]{1,0:T(8,128)(2,1)S(1)} %slice.20), channel_id=1, source_target_pairs={{0,1},{1,0},{2,3},{3,2},{4,5},{5,4},{6,7},{7,6},{8,9},{9,8},{10,11... | collective-permute-start | bytes 405512 | tf_op jit(solution)/shard_map/ppermute | solution.py:383
  12.5 1.5 %collective-permute-start.1 = (bf16[256,256]{1,0:T(8,128)(2,1)S(1)}, bf16[256,256]{1,0:T(8,128)(2,1)S(1)}, u32[]{:S(2)}, u32[]{:S(2)}) collective-permute-start(bf16[256,256]{1,0:T(8,128)(2,1)S(1)} %bitcast.20), channel_id=1, source_target_pairs={{0,1},{1,0},{2,3},{3,2},{4,5},{5,4},{6,7},{7,6},{8,9},{9,8},{10,11... | collective-permute-start | bytes 393224 | tf_op jit(solution)/shard_map/ppermute | solution.py:383
  13.0 3.0 %collective-permute-start.4 = (bf16[256,256]{1,0:T(8,128)(2,1)S(1)}, bf16[256,256]{1,0:T(8,128)(2,1)S(1)}, u32[]{:S(2)}, u32[]{:S(2)}) collective-permute-start(bf16[256,256]{1,0:T(8,128)(2,1)S(1)} %slice.21), channel_id=1, source_target_pairs={{0,1},{1,0},{2,3},{3,2},{4,5},{5,4},{6,7},{7,6},{8,9},{9,8},{10,11... | collective-permute-start | bytes 393224 | tf_op jit(solution)/shard_map/ppermute | solution.py:383
  21.5 13.4 %all-to-all-start.1 = ((bf16[8,136,128]{2,1,0:T(8,128)(2,1)}), bf16[8,136,128]{2,1,0:T(8,128)(2,1)S(1)}, u32[]{:S(2)}, u32[]{:S(2)}) async-start(bf16[8,136,128]{2,1,0:T(8,128)(2,1)} %attention.1), calls=%async_computation.1 | async-start | bytes 557056 | tf_op jit(solution)/shard_map/all_to_all | solution.py:462
  27.0 27.4 %copy-start.1 = (f32[2048]{0:T(1024)S(1)}, f32[2048]{0:T(1024)}, u32[]{:S(2)}) copy-start(f32[2048]{0:T(1024)} %param.25) | copy-start | bytes 24580
  27.0 33.0 %copy-start.3 = (s32[2048]{0:T(1024)S(1)}, s32[2048]{0:T(1024)}, u32[]{:S(2)}) copy-start(s32[2048]{0:T(1024)} %param.32) | copy-start | bytes 24580
  36.0 18.3 %all-to-all-start.2 = ((bf16[8,8,2048]{2,1,0:T(8,128)(2,1)}), bf16[8,8,2048]{2,1,0:T(8,128)(2,1)S(1)}, u32[]{:S(2)}, u32[]{:S(2)}) async-start(bf16[8,8,2048]{2,1,0:T(8,128)(2,1)} %bitcast.8), calls=%async_computation.2 | async-start | bytes 524288 | tf_op jit(solution)/shard_map/all_to_all | solution.py:466
  55.2 13.8 %all-to-all-start.3 = ((bf16[8,8,2048]{2,1,0:T(8,128)(2,1)}), bf16[8,8,2048]{2,1,0:T(8,128)(2,1)S(1)}, u32[]{:S(2)}, u32[]{:S(2)}) async-start(bf16[8,8,2048]{2,1,0:T(8,128)(2,1)} %get-tuple-element.33), calls=%async_computation.3 | async-start | bytes 524288 | tf_op jit(solution)/shard_map/all_to_all | solution.py:478
  72.5 12.3 %all-to-all-start.4 = ((f32[32,1,128]{2,1,0:T(1,128)}), f32[32,1,128]{2,1,0:T(1,128)S(1)}, u32[]{:S(2)}, u32[]{:S(2)}) async-start(f32[32,1,128]{2,1,0:T(1,128)} %bitcast.12), calls=%async_computation.4 | async-start | bytes 32768 | tf_op jit(solution)/shard_map/all_to_all | solution.py:489
  85.5 10.8 %all-to-all-start.5 = ((f32[8,1,128]{2,1,0:T(1,128)}), f32[8,1,128]{2,1,0:T(1,128)S(1)}, u32[]{:S(2)}, u32[]{:S(2)}) async-start(f32[8,1,128]{2,1,0:T(1,128)} %fold.1), calls=%async_computation.5 | async-start | bytes 8192 | tf_op jit(solution)/shard_map/all_to_all | solution.py:491

commit v6 on v5

--- a/solution.py
+++ b/solution.py
@@ -27,50 +27,52 @@
     return first, second, third
 
 
-def project_kernel(states, gain, weight, keys, values, buckets, out, payload, states_here, gain_here, weight_here,
-                   buckets_here, arrivals):
+def project_kernel(states, gain, weight, keys, buckets, out, payload, states_here, gain_here, weight_here, buckets_here,
+                   arrivals):
     count = keys.shape[0]
-    pairs = (
-        (states, states_here),
-        (gain, gain_here),
-        (weight, weight_here),
-        (buckets, buckets_here),
-        (keys, payload.at[pl.ds(0, count)]),
-        (values, payload.at[pl.ds(count + 8, count)]),
-    )
+    steps = weight_here.shape[0]
+    size = weight.shape[0] // steps
+    pairs = [(states, states_here), (gain, gain_here)]
+    pairs += [(weight.at[pl.ds(i * size, size)], weight_here.at[i]) for i in range(steps)]
+    pairs += [(buckets, buckets_here), (keys, payload.at[pl.ds(0, count)])]
     copies = [pltpu.make_async_copy(there, here, arrivals.at[i]) for i, (there, here) in enumerate(pairs)]
     for copy in copies:
         copy.start()
     copies[0].wait()
     copies[1].wait()
     normed = rms_scale(states_here[...], gain_here[...]).astype(BF)
-    copies[3].wait()
+    queries = jnp.zeros((normed.shape[0], weight.shape[1]), F32)
+    for i in range(steps):
+        copies[2 + i].wait()
+        queries += jnp.dot(normed[:, i * size : (i + 1) * size], weight_here[i], preferred_element_type=F32)
+    queries = queries.astype(BF)
+    for chip in range(out.shape[0]):
+        out[chip] = queries
+    copies[2 + steps].wait()
     both = jnp.concatenate([buckets_here[0:1, :], buckets_here[1:2, :]], axis=1).astype(F32)
     payload[count : count + 8, :] = jnp.broadcast_to(both, (8, both.shape[1])).astype(BF)
-    copies[2].wait()
-    queries = jnp.dot(normed, weight_here[...], preferred_element_type=F32).astype(BF)
-    for chip in range(out.shape[0]):
-        out[chip] = queries
-    copies[4].wait()
-    copies[5].wait()
-
-
-def near_kernel(rank, first, second, third, bias_table, page_table, query_lengths, doc_query, doc_rows, keys_aug, values_t,
-                extra, table_here, slots_here, lengths_here, info, arrivals, query_here, rows_here, doc_arrivals, *, pages):
+    copies[3 + steps].wait()
+
+
+def near_kernel(rank, k0, k1, v0, v1, bias_table, page_table, query_lengths, doc_query, doc_rows, keys_aug, values_t,
+                extra, table_here, slots_here, lengths_here, info, arrivals, query_here, rows_here, values_here,
+                doc_arrivals, *, pages):
     copies = [
         pltpu.make_async_copy(doc_query, query_here, doc_arrivals.at[0]),
         pltpu.make_async_copy(doc_rows, rows_here, doc_arrivals.at[1]),
+        pltpu.make_async_copy(v0, values_here, doc_arrivals.at[2]),
     ]
     for copy in copies:
         copy.start()
 
     def columns():
-        for copy in copies:
-            copy.wait()
+        copies[0].wait()
+        copies[1].wait()
         query_columns(rank, query_here, rows_here, extra)
+        copies[2].wait()
 
     prepare_kernel(
-        rank, first, second, third, bias_table, page_table, query_lengths, keys_aug, values_t, table_here, slots_here,
+        rank, k0, k1, values_here, v1, bias_table, page_table, query_lengths, keys_aug, values_t, table_here, slots_here,
         lengths_here, info, arrivals, side=0, pages=pages, meanwhile=columns,
     )
 
@@ -107,7 +109,7 @@
     extra[...] = columns.T.astype(BF)
 
 
-def prepare_kernel(rank, first, second, third, bias_table, page_table, query_lengths, keys_aug, values_t, table_here,
+def prepare_kernel(rank, k0, k1, v0, v1, bias_table, page_table, query_lengths, keys_aug, values_t, table_here,
                    slots_here, lengths_here, info, arrivals, *, side, pages, meanwhile=None):
     width, total = values_t.shape
     page_len = total // (2 * pages)
@@ -152,8 +154,7 @@
     slot = lax.broadcasted_iota(jnp.int32, (page_len, 128), 0)
     key_col = lax.broadcasted_iota(jnp.int32, (page_len, 128), 1) % 64
     mine = ((chip % row_chips // 2) * 2 + core) * pages
-    sources = ((first, first, keys + 8), (second, third, 0))
-    for part, (key_rows, value_rows, offset) in enumerate(sources):
+    for part, (key_rows, value_rows) in enumerate(((k0, v0), (k1, v1))):
         for page in range(pages):
             place = (mine ^ ((2 * side + part) * pages)) + page
             span = pl.ds((part * pages + page) * page_len, page_len)
@@ -167,7 +168,7 @@
                 keep = low if h % 2 == 0 else jnp.logical_not(low)
                 half = key[:, (h // 2) * 128 : (h // 2 + 1) * 128]
                 keys_aug[h, span, :] = jnp.where(keep, half, bias[:, h * 128 : (h + 1) * 128] + marks).astype(BF)
-            value = value_rows[offset + page * page_len : offset + (page + 1) * page_len, :]
+            value = value_rows[page * page_len : (page + 1) * page_len, :]
             values_t[:, span] = value.astype(F32).T.astype(BF)
 
 
@@ -383,32 +384,34 @@
         return lax.ppermute(value, "page", pairs)
 
     keys_held = local_pages * page_len
+    steps = 4
     copies, payload = call(
         project_kernel,
         "project",
-        [shape((group, tok_dev, local_width), BF), shape((2 * keys_held + 8, local_width), BF)],
-        [hbm()] * 6,
+        [shape((group, tok_dev, local_width), BF), shape((keys_held + 8, local_width), BF)],
+        [hbm()] * 5,
         [
             pltpu.VMEM((tok_dev, model), BF),
             pltpu.VMEM((1, model), F32),
-            pltpu.VMEM((model, local_width), BF),
+            pltpu.VMEM((steps, model // steps, local_width), BF),
             pltpu.VMEM((local_pages, page_len), jnp.int32),
-            pltpu.SemaphoreType.DMA((6,)),
+            pltpu.SemaphoreType.DMA((steps + 4,)),
         ],
     )(
         in_hbm(doc_states),
         in_hbm(gain_attn.reshape(1, model)),
         in_hbm(query_weight),
         in_hbm(cache_keys.reshape(keys_held, local_width)),
-        in_hbm(cache_values.reshape(keys_held, local_width)),
         in_hbm(rel_bucket),
     )
     values_own = cache_values.reshape(keys_held, local_width)
+    values_sent, copies = lax.optimization_barrier((values_own, copies))
     payload_side = swap(payload, side_swap)
-    keys_core = swap(payload[0 : keys_held + 8], core_swap)
+    values_side = swap(values_sent, side_swap)
+    payload_core = swap(payload, core_swap)
     values_core = swap(values_own, core_swap)
-    keys_far = swap(payload_side[0 : keys_held + 8], core_swap)
-    values_far = swap(payload_side[keys_held + 8 :], core_swap)
+    payload_far = swap(payload_side, core_swap)
+    values_far = swap(values_side, core_swap)
     gathered = lax.all_to_all(copies, "page", 0, 0, axis_index_groups=groups, tiled=True)
 
     rank = page_rank.reshape(1)
@@ -428,21 +431,22 @@
         functools.partial(near_kernel, pages=local_pages),
         "near",
         shapes + [shape((group * tok_dev, 128), BF)],
-        [smem()] + [vmem()] * 3 + [hbm()] * 5,
+        [smem()] + [vmem()] * 2 + [hbm(), vmem()] + [hbm()] * 5,
         scratch
         + [
             pltpu.VMEM((1, doc_query.shape[0]), jnp.int32),
             pltpu.VMEM(doc_rows.shape, jnp.int32),
-            pltpu.SemaphoreType.DMA((2,)),
+            pltpu.VMEM(values_own.shape, BF),
+            pltpu.SemaphoreType.DMA((3,)),
         ],
-    )(rank, payload, keys_core, values_core, *tables, in_hbm(doc_query.reshape(1, -1)), in_hbm(doc_rows))
+    )(rank, payload, payload_core, in_hbm(values_own), values_core, *tables, in_hbm(doc_query.reshape(1, -1)), in_hbm(doc_rows))
     keys_away, values_away = call(
         functools.partial(prepare_kernel, side=1, pages=local_pages),
         "away",
         shapes,
-        [smem()] + [vmem()] * 3 + [hbm()] * 3,
+        [smem()] + [vmem()] * 4 + [hbm()] * 3,
         scratch,
-    )(rank, payload_side, keys_far, values_far, *tables)
+    )(rank, payload_side, payload_far, values_side, values_far, *tables)
     partials = call(
         attention_kernel,
         "attention",
@@ -480,7 +484,7 @@
     own_score = jnp.where(token // own == head_rank, jnp.tile(hidden_score[:, :1], (head_size, 1)), 0.0)
     own_docs = lax.dynamic_slice_in_dim(doc_of_token, page_rank * tok_dev, tok_dev, 0)[:, None]
     doc_dev = doc_query.shape[0] // page_size
-    steps = 4
+    steps = 8
     doc_sums = call(
         feed_kernel, "feed", shape((page_size, 128), F32), [vmem(), vmem(), hbm(), vmem(), vmem(), vmem()],
         [pltpu.VMEM((steps, model // steps, hidden_units), BF), pltpu.SemaphoreType.DMA((steps,))],

time: 98.7 us -> 98.3 us (level)
  waiting for transfers between devices: 37.3 us -> 36.3 us
    ppermute x5 -> x6, waiting for transfers between devices: 3.02 us -> 1.21 us  [swap(): return lax.ppermute(value, 'page', pairs)]
    all_to_all x1, waiting for transfers between devices: 0.01 us -> 1.66 us  [per_device(): lax.all_to_all(copies, 'page', 0, 0, axis_index_groups=groups, tiled=True)]
    all_to_all x1, starting transfers between devices: 5.5 us -> 4.05 us  [per_device(): lax.all_to_all(partials, 'page', 0, 0, axis_index_groups=groups, tiled=True)]
    ppermute x5 -> x6, starting transfers between devices: 3.98 us -> 4.47 us  [swap(): return lax.ppermute(value, 'page', pairs)]
  transfers between devices with their start and end apart: 11 -> 12, of which waited for: 7 -> 8; matrix products, arithmetic and copies ran while one was open for 1% -> 1% of each run, Pallas kernels for 8% -> 8%
where the time goes in v6:
time: 98.3 us; the launch traced here: 96.5 us
  starting transfers between devices  37.1 us (38%)
  waiting for transfers between devices  36.3 us (37%)
  Pallas kernels  21 us (21%)
  local copies, waits for them, and re-layouts  1.14 us (1%)
    all_to_all x1, waiting for transfers between devices, per_device(): lax.all_to_all(projected.reshape(head_size, own, model), 'head', 0, 0, ti...  8.64 us
    all_to_all x1, starting transfers between devices, per_device(): lax.all_to_all(projected.reshape(head_size, own, model), 'head', 0, 0, ti...  8.57 us
    all_to_all x1, waiting for transfers between devices, per_device(): arrived = lax.all_to_all(doc_sums, 'page', 0, 0, tiled=True)  7.34 us
    all_to_all x1, waiting for transfers between devices, per_device(): lax.all_to_all(spread, 'head', 0, 0, tiled=True).reshape(tok_dev, model)  6.54 us
    all_to_all x1, waiting for transfers between devices, per_device(): lax.all_to_all(pooled, 'head', 0, 0, tiled=True)  6.04 us
    all_to_all x1, starting transfers between devices, per_device(): lax.all_to_all(copies, 'page', 0, 0, axis_index_groups=groups, tiled=True)  5.4 us
    all_to_all x1, starting transfers between devices, per_device(): arrived = lax.all_to_all(doc_sums, 'page', 0, 0, tiled=True)  5.29 us
    all_to_all x1, waiting for transfers between devices, per_device(): lax.all_to_all(partials, 'page', 0, 0, axis_index_groups=groups, tiled=True)  4.88 us
  transfers between devices with their start and end apart: 12, of which 8 were waited for; matrix products, arithmetic and copies ran while one was open for 1% of the time, Pallas kernels for 8%

profile of v6, /device:TPU:32, one launch (start us, length us, event | category | flops | bytes accessed | tf_op | source)
XLA Modules:
  0.0 96.5 jit_solution(7323091716471725201)
XLA Ops:
  0.0 0.0 copy-start
  0.0 2.5 %project.1 = (bf16[8,64,256]{2,1,0:T(8,128)(2,1)}, bf16[264,256]{1,0:T(8,128)(2,1)S(1)}) custom-call(bf16[64,2048]{1,0:T(8,128)(2,1)} %states.1, f32[1,2048]{1,0:T(1,128)} %bitcast.23, bf16[2048,256]{1,0:T(8,128)(2,1)} %weight.1, bf16[256,256]{1,0:T(8,128)(2,1)} %bitcast.18, s32[2,128]{1,0:T(2,128)} %buckets.1), custom_call_target="tpu_custom_call" | custom-call | tf_op jit(solution)/shard_map/project/pallas_call | solution.py:388
  2.5 3.1 %collective-permute-start.2 = (bf16[264,256]{1,0:T(8,128)(2,1)S(1)}, bf16[264,256]{1,0:T(8,128)(2,1)S(1)}, u32[]{:S(2)}, u32[]{:S(2)}) collective-permute-start(bf16[264,256]{1,0:T(8,128)(2,1)S(1)} %get-tuple-element.25.k0), channel_id=1, source_target_pairs={{0,4},{1,5},{2,6},{3,7},{4,0},{5,1},{6,2},{7,3},{8,12},{9,13},{10,... | collective-permute-start | bytes 405512 | tf_op jit(solution)/shard_map/ppermute | solution.py:384
  5.6 0.5 collective-permute-start.4
  6.1 5.4 %all-to-all-start = ((bf16[8,64,256]{2,1,0:T(8,128)(2,1)}), bf16[8,64,256]{2,1,0:T(8,128)(2,1)S(1)}, u32[]{:S(2)}, u32[]{:S(2)}) async-start(bf16[8,64,256]{2,1,0:T(8,128)(2,1)} %get-tuple-element.24), calls=%async_computation | async-start | bytes 524288 | tf_op jit(solution)/shard_map/all_to_all | solution.py:415
  11.5 0.0 collective-permute-start
  11.5 0.0 collective-permute-done.2.k0
  11.5 0.5 collective-permute-start.3
  12.0 0.1 collective-permute-start.1
  12.1 0.2 collective-permute-done.4.v0
  12.3 0.3 collective-permute-start.5
  12.5 1.0 %collective-permute-done.1.v1 = bf16[256,256]{1,0:T(8,128)(2,1)S(1)} collective-permute-done((bf16[256,256]{1,0:T(8,128)(2,1)}, bf16[256,256]{1,0:T(8,128)(2,1)S(1)}, u32[]{:S(2)}, u32[]{:S(2)}) %collective-permute-start.1) | collective-permute-done | bytes 131104 | tf_op jit(solution)/shard_map/ppermute | solution.py:384
  13.6 0.0 collective-permute-done.k1
  13.6 2.0 %near.1 = (bf16[4,512,128]{2,1,0:T(8,128)(2,1)S(1)}, bf16[256,512]{1,0:T(8,128)(2,1)S(1)}, bf16[512,128]{1,0:T(8,128)(2,1)S(1)}) custom-call(s32[1]{0:T(128)} %bitcast.3.rank, bf16[264,256]{1,0:T(8,128)(2,1)S(1)} %get-tuple-element.25.k0, bf16[264,256]{1,0:T(8,128)(2,1)S(1)} %collective-permute-done.k1, bf16[256,256]{1,0:T(8,128)(2,1)} %bitcast.21, ...), custom_call_target="tpu_custom_call" | custom-call | tf_op jit(solution)/shard_map/near/pallas_call | solution.py:430
  15.6 0.0 collective-permute-done.5.v1
  15.6 0.0 collective-permute-done.3.k1
  15.6 1.5 %away.1 = (bf16[4,512,128]{2,1,0:T(8,128)(2,1)S(1)}, bf16[256,512]{1,0:T(8,128)(2,1)S(1)}) custom-call(s32[1]{0:T(128)} %bitcast.3.rank, bf16[264,256]{1,0:T(8,128)(2,1)S(1)} %collective-permute-done.2.k0, bf16[264,256]{1,0:T(8,128)(2,1)S(1)} %collective-permute-done.3.k1, bf16[256,256]{1,0:T(8,128)(2,1)S(1)} %collective-permute-done.4.v0, ...), custom_call_target="tpu_custom_call" | custom-call | tf_op jit(solution)/shard_map/away/pallas_call | solution.py:443
  17.1 1.7 %all-to-all-done.queries = bf16[8,64,256]{2,1,0:T(8,128)(2,1)S(1)} async-done(((bf16[8,64,256]{2,1,0:T(8,128)(2,1)}), bf16[8,64,256]{2,1,0:T(8,128)(2,1)S(1)}, u32[]{:S(2)}, u32[]{:S(2)}) %all-to-all-start) | async-done | bytes 262176 | tf_op jit(solution)/shard_map/all_to_all | solution.py:415
  18.8 3.9 %attention.1 = bf16[8,136,128]{2,1,0:T(8,128)(2,1)} custom-call(bf16[8,64,256]{2,1,0:T(8,128)(2,1)S(1)} %all-to-all-done.queries, bf16[4,512,128]{2,1,0:T(8,128)(2,1)S(1)} %get-tuple-element.26.keys_near, bf16[4,512,128]{2,1,0:T(8,128)(2,1)S(1)} %get-tuple-element.28.keys_far, bf16[256,512]{1,0:T(8,128)(2,1)S(1)} %get-tuple-element.29.values_near, ...), custom_call_target="tpu_custom_call" | custom-call | tf_op jit(solution)/shard_map/attention/pallas_call | solution.py:450
  22.7 4.1 %all-to-all-start.1 = ((bf16[8,136,128]{2,1,0:T(8,128)(2,1)}), bf16[8,136,128]{2,1,0:T(8,128)(2,1)S(1)}, u32[]{:S(2)}, u32[]{:S(2)}) async-start(bf16[8,136,128]{2,1,0:T(8,128)(2,1)} %attention.1), calls=%async_computation.1 | async-start | bytes 557056 | tf_op jit(solution)/shard_map/all_to_all | solution.py:466
  26.7 0.0 copy-done
  26.7 0.0 copy-start.1
  26.8 0.0 copy-start.2
  26.8 2.9 %down.1 = (f32[1,640]{1,0:T(1,128)S(1)}, bf16[256,2048]{1,0:T(8,128)(2,1)S(1)}) custom-call(bf16[640,2048]{1,0:T(8,128)(2,1)} %weight.2, f32[1,2048]{1,0:T(1,128)S(1)} %bitcast.15, bf16[256,2048]{1,0:T(8,128)(2,1)} %out_weight), custom_call_target="tpu_custom_call" | custom-call | tf_op jit(solution)/shard_map/down/pallas_call | solution.py:459
  29.7 4.9 %all-to-all-done.1.parts = bf16[8,136,128]{2,1,0:T(8,128)(2,1)S(1)} async-done(((bf16[8,136,128]{2,1,0:T(8,128)(2,1)}), bf16[8,136,128]{2,1,0:T(8,128)(2,1)S(1)}, u32[]{:S(2)}, u32[]{:S(2)}) %all-to-all-start.1) | async-done | bytes 278560 | tf_op jit(solution)/shard_map/all_to_all | solution.py:466
  34.6 1.1 %combine.1 = bf16[64,2048]{1,0:T(8,128)(2,1)} custom-call(bf16[8,136,128]{2,1,0:T(8,128)(2,1)S(1)} %all-to-all-done.1.parts, bf16[256,2048]{1,0:T(8,128)(2,1)S(1)} %get-tuple-element.35.out_weight), custom_call_target="tpu_custom_call" | custom-call | tf_op jit(solution)/shard_map/combine/pallas_call | solution.py:467
  35.7 8.6 %all-to-all-start.2 = ((bf16[8,8,2048]{2,1,0:T(8,128)(2,1)}), bf16[8,8,2048]{2,1,0:T(8,128)(2,1)S(1)}, u32[]{:S(2)}, u32[]{:S(2)}) async-start(bf16[8,8,2048]{2,1,0:T(8,128)(2,1)} %bitcast.8), calls=%async_computation.2 | async-start | bytes 524288 | tf_op jit(solution)/shard_map/all_to_all | solution.py:470
  44.2 0.8 constant_dynamic-slice_fusion.states
  45.0 8.6 %all-to-all-done.2.terms = bf16[8,8,2048]{2,1,0:T(8,128)(2,1)S(1)} async-done(((bf16[8,8,2048]{2,1,0:T(8,128)(2,1)}), bf16[8,8,2048]{2,1,0:T(8,128)(2,1)S(1)}, u32[]{:S(2)}, u32[]{:S(2)}) %all-to-all-start.2) | async-done | bytes 262176 | tf_op jit(solution)/shard_map/all_to_all | solution.py:470
  53.6 0.0 copy-done.1
  53.6 0.8 norm.1
  54.5 4.8 %all-to-all-start.3 = ((bf16[8,8,2048]{2,1,0:T(8,128)(2,1)}), bf16[8,8,2048]{2,1,0:T(8,128)(2,1)S(1)}, u32[]{:S(2)}, u32[]{:S(2)}) async-start(bf16[8,8,2048]{2,1,0:T(8,128)(2,1)} %get-tuple-element.37), calls=%async_computation.3 | async-start | bytes 524288 | tf_op jit(solution)/shard_map/all_to_all | solution.py:482
  59.2 0.0 copy-done.2
  59.2 0.1 dynamic-slice_bitcast_fusion
  59.3 0.1 copy.23.own_docs
  59.4 0.1 slice_reduce_fusion
  59.5 0.1 tile.14
  59.6 1.8 %fetch.1.gate_weight = bf16[2048,640]{1,0:T(8,128)(2,1)S(1)} custom-call(bf16[2048,640]{1,0:T(8,128)(2,1)} %weight.3), custom_call_target="tpu_custom_call" | custom-call | tf_op jit(solution)/shard_map/fetch/pallas_call | solution.py:479
  61.4 6.5 %all-to-all-done.3 = bf16[8,8,2048]{2,1,0:T(8,128)(2,1)S(1)} async-done(((bf16[8,8,2048]{2,1,0:T(8,128)(2,1)}), bf16[8,8,2048]{2,1,0:T(8,128)(2,1)S(1)}, u32[]{:S(2)}, u32[]{:S(2)}) %all-to-all-start.3) | async-done | bytes 262176 | tf_op jit(solution)/shard_map/all_to_all | solution.py:482
  67.9 3.9 %feed.1 = f32[32,128]{1,0:T(8,128)} custom-call(bf16[64,2048]{1,0:T(8,128)(2,1)S(1)} %bitcast.14, bf16[2048,640]{1,0:T(8,128)(2,1)S(1)} %fetch.1.gate_weight, bf16[2048,640]{1,0:T(8,128)(2,1)} %up_weight.1, f32[1,640]{1,0:T(1,128)S(1)} %get-tuple-element.39.down_score, f32[64,1]{1,0:T(8,128)S(1)} %fusion.4.own_score, s32[64,1]{1,0:T(8,128)S(1)} %copy.23.own_docs), custom_call_target="tpu_custom_call" | custom-call | tf_op jit(solution)/shard_map/feed/pallas_call | solution.py:488
  71.8 5.3 %all-to-all-start.4 = ((f32[32,1,128]{2,1,0:T(1,128)}), f32[32,1,128]{2,1,0:T(1,128)S(1)}, u32[]{:S(2)}, u32[]{:S(2)}) async-start(f32[32,1,128]{2,1,0:T(1,128)} %bitcast.12), calls=%async_computation.4 | async-start | bytes 32768 | tf_op jit(solution)/shard_map/all_to_all | solution.py:493
  77.1 7.3 %all-to-all-done.4.terms = f32[32,1,128]{2,1,0:T(1,128)S(1)} async-done(((f32[32,1,128]{2,1,0:T(1,128)}), f32[32,1,128]{2,1,0:T(1,128)S(1)}, u32[]{:S(2)}, u32[]{:S(2)}) %all-to-all-start.4) | async-done | bytes 16416 | tf_op jit(solution)/shard_map/all_to_all | solution.py:493
  84.5 0.6 fold.1
  85.1 4.6 %all-to-all-start.5 = ((f32[8,1,128]{2,1,0:T(1,128)}), f32[8,1,128]{2,1,0:T(1,128)S(1)}, u32[]{:S(2)}, u32[]{:S(2)}) async-start(f32[8,1,128]{2,1,0:T(1,128)} %fold.1), calls=%async_computation.5 | async-start | bytes 8192 | tf_op jit(solution)/shard_map/all_to_all | solution.py:495
  89.7 0.2 convert_reduce_fusion
  89.9 6.0 %all-to-all-done.5 = f32[8,1,128]{2,1,0:T(1,128)S(1)} async-done(((f32[8,1,128]{2,1,0:T(1,128)}), f32[8,1,128]{2,1,0:T(1,128)S(1)}, u32[]{:S(2)}, u32[]{:S(2)}) %all-to-all-start.5) | async-done | bytes 4128 | tf_op jit(solution)/shard_map/all_to_all | solution.py:495
  96.0 0.5 slice_divide_fusion
  (4 shorter events, 0.0 us)
Async XLA Ops:
  0.0 26.7 %copy-start = (f32[2048]{0:T(1024)S(1)}, f32[2048]{0:T(1024)}, u32[]{:S(2)}) copy-start(f32[2048]{0:T(1024)} %param.29) | copy-start | bytes 24580
  2.5 9.0 %collective-permute-start.2 = (bf16[264,256]{1,0:T(8,128)(2,1)S(1)}, bf16[264,256]{1,0:T(8,128)(2,1)S(1)}, u32[]{:S(2)}, u32[]{:S(2)}) collective-permute-start(bf16[264,256]{1,0:T(8,128)(2,1)S(1)} %get-tuple-element.25.k0), channel_id=1, source_target_pairs={{0,4},{1,5},{2,6},{3,7},{4,0},{5,1},{6,2},{7,3},{8,12},{9,13},{10,... | collective-permute-start | bytes 405512 | tf_op jit(solution)/shard_map/ppermute | solution.py:384
  5.6 6.7 %collective-permute-start.4 = (bf16[256,256]{1,0:T(8,128)(2,1)}, bf16[256,256]{1,0:T(8,128)(2,1)S(1)}, u32[]{:S(2)}, u32[]{:S(2)}) collective-permute-start(bf16[256,256]{1,0:T(8,128)(2,1)} %bitcast.19), channel_id=1, source_target_pairs={{0,4},{1,5},{2,6},{3,7},{4,0},{5,1},{6,2},{7,3},{8,12},{9,13},{10,... | collective-permute-start | bytes 393224 | tf_op jit(solution)/shard_map/ppermute | solution.py:384
  6.1 12.7 %all-to-all-start = ((bf16[8,64,256]{2,1,0:T(8,128)(2,1)}), bf16[8,64,256]{2,1,0:T(8,128)(2,1)S(1)}, u32[]{:S(2)}, u32[]{:S(2)}) async-start(bf16[8,64,256]{2,1,0:T(8,128)(2,1)} %get-tuple-element.24), calls=%async_computation | async-start | bytes 524288 | tf_op jit(solution)/shard_map/all_to_all | solution.py:415
  11.5 2.1 %collective-permute-start = (bf16[264,256]{1,0:T(8,128)(2,1)S(1)}, bf16[264,256]{1,0:T(8,128)(2,1)S(1)}, u32[]{:S(2)}, u32[]{:S(2)}) collective-permute-start(bf16[264,256]{1,0:T(8,128)(2,1)S(1)} %get-tuple-element.25.k0), channel_id=1, source_target_pairs={{0,1},{1,0},{2,3},{3,2},{4,5},{5,4},{6,7},{7,6},{8,9},{9,8},{10,11... | collective-permute-start | bytes 405512 | tf_op jit(solution)/shard_map/ppermute | solution.py:384
  11.5 4.0 %collective-permute-start.3 = (bf16[264,256]{1,0:T(8,128)(2,1)S(1)}, bf16[264,256]{1,0:T(8,128)(2,1)S(1)}, u32[]{:S(2)}, u32[]{:S(2)}) collective-permute-start(bf16[264,256]{1,0:T(8,128)(2,1)S(1)} %collective-permute-done.2.k0), channel_id=1, source_target_pairs={{0,1},{1,0},{2,3},{3,2},{4,5},{5,4},{6,7},{7,6},{8,9},{9,8},{10,11... | collective-permute-start | bytes 405512 | tf_op jit(solution)/shard_map/ppermute | solution.py:384
  12.0 1.6 %collective-permute-start.1 = (bf16[256,256]{1,0:T(8,128)(2,1)}, bf16[256,256]{1,0:T(8,128)(2,1)S(1)}, u32[]{:S(2)}, u32[]{:S(2)}) collective-permute-start(bf16[256,256]{1,0:T(8,128)(2,1)} %bitcast.20), channel_id=1, source_target_pairs={{0,1},{1,0},{2,3},{3,2},{4,5},{5,4},{6,7},{7,6},{8,9},{9,8},{10,11... | collective-permute-start | bytes 393224 | tf_op jit(solution)/shard_map/ppermute | solution.py:384
  12.3 3.3 %collective-permute-start.5 = (bf16[256,256]{1,0:T(8,128)(2,1)S(1)}, bf16[256,256]{1,0:T(8,128)(2,1)S(1)}, u32[]{:S(2)}, u32[]{:S(2)}) collective-permute-start(bf16[256,256]{1,0:T(8,128)(2,1)S(1)} %collective-permute-done.4.v0), channel_id=1, source_target_pairs={{0,1},{1,0},{2,3},{3,2},{4,5},{5,4},{6,7},{7,6},{8,9},{9,8},{10,11... | collective-permute-start | bytes 393224 | tf_op jit(solution)/shard_map/ppermute | solution.py:384
  22.7 11.9 %all-to-all-start.1 = ((bf16[8,136,128]{2,1,0:T(8,128)(2,1)}), bf16[8,136,128]{2,1,0:T(8,128)(2,1)S(1)}, u32[]{:S(2)}, u32[]{:S(2)}) async-start(bf16[8,136,128]{2,1,0:T(8,128)(2,1)} %attention.1), calls=%async_computation.1 | async-start | bytes 557056 | tf_op jit(solution)/shard_map/all_to_all | solution.py:466
  26.7 26.9 %copy-start.1 = (f32[2048]{0:T(1024)S(1)}, f32[2048]{0:T(1024)}, u32[]{:S(2)}) copy-start(f32[2048]{0:T(1024)} %param.25) | copy-start | bytes 24580
  26.8 32.5 %copy-start.2 = (s32[2048]{0:T(1024)S(1)}, s32[2048]{0:T(1024)}, u32[]{:S(2)}) copy-start(s32[2048]{0:T(1024)} %param.32) | copy-start | bytes 24580
  35.7 18.0 %all-to-all-start.2 = ((bf16[8,8,2048]{2,1,0:T(8,128)(2,1)}), bf16[8,8,2048]{2,1,0:T(8,128)(2,1)S(1)}, u32[]{:S(2)}, u32[]{:S(2)}) async-start(bf16[8,8,2048]{2,1,0:T(8,128)(2,1)} %bitcast.8), calls=%async_computation.2 | async-start | bytes 524288 | tf_op jit(solution)/shard_map/all_to_all | solution.py:470
  54.5 13.5 %all-to-all-start.3 = ((bf16[8,8,2048]{2,1,0:T(8,128)(2,1)}), bf16[8,8,2048]{2,1,0:T(8,128)(2,1)S(1)}, u32[]{:S(2)}, u32[]{:S(2)}) async-start(bf16[8,8,2048]{2,1,0:T(8,128)(2,1)} %get-tuple-element.37), calls=%async_computation.3 | async-start | bytes 524288 | tf_op jit(solution)/shard_map/all_to_all | solution.py:482
  71.8 12.7 %all-to-all-start.4 = ((f32[32,1,128]{2,1,0:T(1,128)}), f32[32,1,128]{2,1,0:T(1,128)S(1)}, u32[]{:S(2)}, u32[]{:S(2)}) async-start(f32[32,1,128]{2,1,0:T(1,128)} %bitcast.12), calls=%async_computation.4 | async-start | bytes 32768 | tf_op jit(solution)/shard_map/all_to_all | solution.py:493
  85.1 10.8 %all-to-all-start.5 = ((f32[8,1,128]{2,1,0:T(1,128)}), f32[8,1,128]{2,1,0:T(1,128)S(1)}, u32[]{:S(2)}, u32[]{:S(2)}) async-start(f32[8,1,128]{2,1,0:T(1,128)} %fold.1), calls=%async_computation.5 | async-start | bytes 8192 | tf_op jit(solution)/shard_map/all_to_all | solution.py:495

commit v7 on v5

--- a/solution.py
+++ b/solution.py
@@ -55,7 +55,7 @@
     copies[5].wait()
 
 
-def near_kernel(rank, first, second, third, bias_table, page_table, query_lengths, doc_query, doc_rows, keys_aug, values_t,
+def near_kernel(rank, first, second, bias_table, page_table, query_lengths, doc_query, doc_rows, keys_aug, values_t,
                 extra, table_here, slots_here, lengths_here, info, arrivals, query_here, rows_here, doc_arrivals, *, pages):
     copies = [
         pltpu.make_async_copy(doc_query, query_here, doc_arrivals.at[0]),
@@ -70,7 +70,7 @@
         query_columns(rank, query_here, rows_here, extra)
 
     prepare_kernel(
-        rank, first, second, third, bias_table, page_table, query_lengths, keys_aug, values_t, table_here, slots_here,
+        rank, first, second, None, bias_table, page_table, query_lengths, keys_aug, values_t, table_here, slots_here,
         lengths_here, info, arrivals, side=0, pages=pages, meanwhile=columns,
     )
 
@@ -121,6 +121,11 @@
     copies = [pltpu.make_async_copy(there, here, arrivals.at[i]) for i, (there, here) in enumerate(pairs)]
     for copy in copies:
         copy.start()
+    sources = ((first, keys + 8), (second, keys + 8) if third is None else (third, 0))
+    for part, (value_rows, offset) in enumerate(sources):
+        for page in range(pages):
+            value = value_rows[offset + page * page_len : offset + (page + 1) * page_len, :]
+            values_t[:, pl.ds((part * pages + page) * page_len, page_len)] = value.astype(F32).T.astype(BF)
     if meanwhile is not None:
         meanwhile()
     core = rank[0] % 2
@@ -152,8 +157,7 @@
     slot = lax.broadcasted_iota(jnp.int32, (page_len, 128), 0)
     key_col = lax.broadcasted_iota(jnp.int32, (page_len, 128), 1) % 64
     mine = ((chip % row_chips // 2) * 2 + core) * pages
-    sources = ((first, first, keys + 8), (second, third, 0))
-    for part, (key_rows, value_rows, offset) in enumerate(sources):
+    for part, key_rows in enumerate((first, second)):
         for page in range(pages):
             place = (mine ^ ((2 * side + part) * pages)) + page
             span = pl.ds((part * pages + page) * page_len, page_len)
@@ -167,8 +171,6 @@
                 keep = low if h % 2 == 0 else jnp.logical_not(low)
                 half = key[:, (h // 2) * 128 : (h // 2 + 1) * 128]
                 keys_aug[h, span, :] = jnp.where(keep, half, bias[:, h * 128 : (h + 1) * 128] + marks).astype(BF)
-            value = value_rows[offset + page * page_len : offset + (page + 1) * page_len, :]
-            values_t[:, span] = value.astype(F32).T.astype(BF)
 
 
 def attention_kernel(queries, keys_near, keys_far, values_near, values_far, extra, out, rows_aug):
@@ -403,10 +405,8 @@
         in_hbm(cache_values.reshape(keys_held, local_width)),
         in_hbm(rel_bucket),
     )
-    values_own = cache_values.reshape(keys_held, local_width)
     payload_side = swap(payload, side_swap)
-    keys_core = swap(payload[0 : keys_held + 8], core_swap)
-    values_core = swap(values_own, core_swap)
+    payload_core = swap(payload, core_swap)
     keys_far = swap(payload_side[0 : keys_held + 8], core_swap)
     values_far = swap(payload_side[keys_held + 8 :], core_swap)
     gathered = lax.all_to_all(copies, "page", 0, 0, axis_index_groups=groups, tiled=True)
@@ -428,14 +428,14 @@
         functools.partial(near_kernel, pages=local_pages),
         "near",
         shapes + [shape((group * tok_dev, 128), BF)],
-        [smem()] + [vmem()] * 3 + [hbm()] * 5,
+        [smem()] + [vmem()] * 2 + [hbm()] * 5,
         scratch
         + [
             pltpu.VMEM((1, doc_query.shape[0]), jnp.int32),
             pltpu.VMEM(doc_rows.shape, jnp.int32),
             pltpu.SemaphoreType.DMA((2,)),
         ],
-    )(rank, payload, keys_core, values_core, *tables, in_hbm(doc_query.reshape(1, -1)), in_hbm(doc_rows))
+    )(rank, payload, payload_core, *tables, in_hbm(doc_query.reshape(1, -1)), in_hbm(doc_rows))
     keys_away, values_away = call(
         functools.partial(prepare_kernel, side=1, pages=local_pages),
         "away",

time: 98.7 us -> 96.7 us (0.980)
  starting transfers between devices: 36.8 us -> 35.1 us
    all_to_all x1, starting transfers between devices: 5.5 us -> 3.77 us  [per_device(): lax.all_to_all(partials, 'page', 0, 0, axis_index_groups=groups, tiled=True)]
    all_to_all x1, waiting for transfers between devices: 0.01 us -> 1.64 us  [per_device(): lax.all_to_all(copies, 'page', 0, 0, axis_index_groups=groups, tiled=True)]
    ppermute x5 -> x4, waiting for transfers between devices: 3.02 us -> 2.12 us  [swap(): return lax.ppermute(value, 'page', pairs)]
    ppermute x5 -> x4, starting transfers between devices: 3.98 us -> 3.78 us  [swap(): return lax.ppermute(value, 'page', pairs)]
  transfers between devices with their start and end apart: 11 -> 10, of which waited for: 7 -> 7; matrix products, arithmetic and copies ran while one was open for 1% -> 1% of each run, Pallas kernels for 8% -> 9%
where the time goes in v7:
time: 96.7 us; the launch traced here: 94.8 us
  waiting for transfers between devices  37.1 us (38%)
  starting transfers between devices  35.1 us (36%)
  Pallas kernels  20.5 us (21%)
  local copies, waits for them, and re-layouts  1.17 us (1%)
    all_to_all x1, waiting for transfers between devices, per_device(): lax.all_to_all(projected.reshape(head_size, own, model), 'head', 0, 0, ti...  8.69 us
    all_to_all x1, starting transfers between devices, per_device(): lax.all_to_all(projected.reshape(head_size, own, model), 'head', 0, 0, ti...  8.57 us
    all_to_all x1, waiting for transfers between devices, per_device(): arrived = lax.all_to_all(doc_sums, 'page', 0, 0, tiled=True)  7.33 us
    all_to_all x1, waiting for transfers between devices, per_device(): lax.all_to_all(spread, 'head', 0, 0, tiled=True).reshape(tok_dev, model)  6.54 us
    all_to_all x1, waiting for transfers between devices, per_device(): lax.all_to_all(pooled, 'head', 0, 0, tiled=True)  6.05 us
    all_to_all x1, starting transfers between devices, per_device(): arrived = lax.all_to_all(doc_sums, 'page', 0, 0, tiled=True)  4.91 us
    all_to_all x1, starting transfers between devices, per_device(): lax.all_to_all(pooled, 'head', 0, 0, tiled=True)  4.82 us
    all_to_all x1, starting transfers between devices, per_device(): lax.all_to_all(spread, 'head', 0, 0, tiled=True).reshape(tok_dev, model)  4.77 us
  transfers between devices with their start and end apart: 10, of which 7 were waited for; matrix products, arithmetic and copies ran while one was open for 1% of the time, Pallas kernels for 9%

profile of v7, /device:TPU:32, one launch (start us, length us, event | category | flops | bytes accessed | tf_op | source)
XLA Modules:
  0.0 94.8 jit_solution(10416410923483900797)
XLA Ops:
  0.0 2.4 %project.1 = (bf16[8,64,256]{2,1,0:T(8,128)(2,1)}, bf16[520,256]{1,0:T(8,128)(2,1)S(1)}) custom-call(bf16[64,2048]{1,0:T(8,128)(2,1)} %states.1, f32[1,2048]{1,0:T(1,128)} %bitcast.21, bf16[2048,256]{1,0:T(8,128)(2,1)} %weight.1, bf16[256,256]{1,0:T(8,128)(2,1)} %bitcast.18, bf16[256,256]{1,0:T(8,128)(2,1)} %bitcast.19, s32[2,128]{1,0:T(2,128)} %buckets.1), custom_call_target="tpu_custom_call" | custom-call | tf_op jit(solution)/shard_map/project/pallas_call | solution.py:388
  2.4 0.0 copy-start
  2.4 3.1 %collective-permute-start.1 = (bf16[520,256]{1,0:T(8,128)(2,1)S(1)}, bf16[520,256]{1,0:T(8,128)(2,1)S(1)}, u32[]{:S(2)}, u32[]{:S(2)}) collective-permute-start(bf16[520,256]{1,0:T(8,128)(2,1)S(1)} %get-tuple-element.22.first), channel_id=1, source_target_pairs={{0,4},{1,5},{2,6},{3,7},{4,0},{5,1},{6,2},{7,3},{8,12},{9,13},{10,... | collective-permute-start | bytes 798728 | tf_op jit(solution)/shard_map/ppermute | solution.py:385
  5.5 0.0 collective-permute-start
  5.5 4.5 %all-to-all-start = ((bf16[8,64,256]{2,1,0:T(8,128)(2,1)}), bf16[8,64,256]{2,1,0:T(8,128)(2,1)S(1)}, u32[]{:S(2)}, u32[]{:S(2)}) async-start(bf16[8,64,256]{2,1,0:T(8,128)(2,1)} %get-tuple-element.21), calls=%async_computation | async-start | bytes 524288 | tf_op jit(solution)/shard_map/all_to_all | solution.py:412
  10.0 2.1 %collective-permute-done.1.first = bf16[520,256]{1,0:T(8,128)(2,1)S(1)} collective-permute-done((bf16[520,256]{1,0:T(8,128)(2,1)S(1)}, bf16[520,256]{1,0:T(8,128)(2,1)S(1)}, u32[]{:S(2)}, u32[]{:S(2)}) %collective-permute-start.1) | collective-permute-done | bytes 266272 | tf_op jit(solution)/shard_map/ppermute | solution.py:385
  12.1 0.1 collective-permute-start.2
  12.3 0.6 collective-permute-start.3
  12.8 0.0 collective-permute-done.second
  12.8 1.9 %near.1 = (bf16[4,512,128]{2,1,0:T(8,128)(2,1)S(1)}, bf16[256,512]{1,0:T(8,128)(2,1)S(1)}, bf16[512,128]{1,0:T(8,128)(2,1)S(1)}) custom-call(s32[1]{0:T(128)} %bitcast.3.rank, bf16[520,256]{1,0:T(8,128)(2,1)S(1)} %get-tuple-element.22.first, bf16[520,256]{1,0:T(8,128)(2,1)S(1)} %collective-permute-done.second, f32[4,32]{1,0:T(4,128)} %bitcast.22, ...), custom_call_target="tpu_custom_call" | custom-call | tf_op jit(solution)/shard_map/near/pallas_call | solution.py:427
  14.8 0.0 collective-permute-done.3.third
  14.8 0.0 collective-permute-done.2.second
  14.8 1.5 %away.1 = (bf16[4,512,128]{2,1,0:T(8,128)(2,1)S(1)}, bf16[256,512]{1,0:T(8,128)(2,1)S(1)}) custom-call(s32[1]{0:T(128)} %bitcast.3.rank, bf16[520,256]{1,0:T(8,128)(2,1)S(1)} %collective-permute-done.1.first, bf16[264,256]{1,0:T(8,128)(2,1)S(1)} %collective-permute-done.2.second, bf16[256,256]{1,0:T(8,128)(2,1)S(1)} %collective-permute-done.3.third, ...), custom_call_target="tpu_custom_call" | custom-call | tf_op jit(solution)/shard_map/away/pallas_call | solution.py:439
  16.3 1.6 %all-to-all-done.queries = bf16[8,64,256]{2,1,0:T(8,128)(2,1)S(1)} async-done(((bf16[8,64,256]{2,1,0:T(8,128)(2,1)}), bf16[8,64,256]{2,1,0:T(8,128)(2,1)S(1)}, u32[]{:S(2)}, u32[]{:S(2)}) %all-to-all-start) | async-done | bytes 262176 | tf_op jit(solution)/shard_map/all_to_all | solution.py:412
  18.0 3.9 %attention.1 = bf16[8,136,128]{2,1,0:T(8,128)(2,1)} custom-call(bf16[8,64,256]{2,1,0:T(8,128)(2,1)S(1)} %all-to-all-done.queries, bf16[4,512,128]{2,1,0:T(8,128)(2,1)S(1)} %get-tuple-element.23.keys_near, bf16[4,512,128]{2,1,0:T(8,128)(2,1)S(1)} %get-tuple-element.24.keys_far, bf16[256,512]{1,0:T(8,128)(2,1)S(1)} %get-tuple-element.25.values_near, ...), custom_call_target="tpu_custom_call" | custom-call | tf_op jit(solution)/shard_map/attention/pallas_call | solution.py:446
  21.9 3.8 %all-to-all-start.1 = ((bf16[8,136,128]{2,1,0:T(8,128)(2,1)}), bf16[8,136,128]{2,1,0:T(8,128)(2,1)S(1)}, u32[]{:S(2)}, u32[]{:S(2)}) async-start(bf16[8,136,128]{2,1,0:T(8,128)(2,1)} %attention.1), calls=%async_computation.1 | async-start | bytes 557056 | tf_op jit(solution)/shard_map/all_to_all | solution.py:462
  25.7 0.0 copy-done
  25.7 0.0 copy-start.1
  25.7 0.0 copy-start.2
  25.7 2.9 %down.1 = (f32[1,640]{1,0:T(1,128)S(1)}, bf16[256,2048]{1,0:T(8,128)(2,1)S(1)}) custom-call(bf16[640,2048]{1,0:T(8,128)(2,1)} %weight.2, f32[1,2048]{1,0:T(1,128)S(1)} %bitcast.15, bf16[256,2048]{1,0:T(8,128)(2,1)} %out_weight), custom_call_target="tpu_custom_call" | custom-call | tf_op jit(solution)/shard_map/down/pallas_call | solution.py:455
  28.6 4.7 %all-to-all-done.1.parts = bf16[8,136,128]{2,1,0:T(8,128)(2,1)S(1)} async-done(((bf16[8,136,128]{2,1,0:T(8,128)(2,1)}), bf16[8,136,128]{2,1,0:T(8,128)(2,1)S(1)}, u32[]{:S(2)}, u32[]{:S(2)}) %all-to-all-start.1) | async-done | bytes 278560 | tf_op jit(solution)/shard_map/all_to_all | solution.py:462
  33.3 1.1 %combine.1 = bf16[64,2048]{1,0:T(8,128)(2,1)} custom-call(bf16[8,136,128]{2,1,0:T(8,128)(2,1)S(1)} %all-to-all-done.1.parts, bf16[256,2048]{1,0:T(8,128)(2,1)S(1)} %get-tuple-element.31.out_weight), custom_call_target="tpu_custom_call" | custom-call | tf_op jit(solution)/shard_map/combine/pallas_call | solution.py:463
  34.4 8.6 %all-to-all-start.2 = ((bf16[8,8,2048]{2,1,0:T(8,128)(2,1)}), bf16[8,8,2048]{2,1,0:T(8,128)(2,1)S(1)}, u32[]{:S(2)}, u32[]{:S(2)}) async-start(bf16[8,8,2048]{2,1,0:T(8,128)(2,1)} %bitcast.8), calls=%async_computation.2 | async-start | bytes 524288 | tf_op jit(solution)/shard_map/all_to_all | solution.py:466
  43.0 0.8 constant_dynamic-slice_fusion.states
  43.8 8.7 %all-to-all-done.2.terms = bf16[8,8,2048]{2,1,0:T(8,128)(2,1)S(1)} async-done(((bf16[8,8,2048]{2,1,0:T(8,128)(2,1)}), bf16[8,8,2048]{2,1,0:T(8,128)(2,1)S(1)}, u32[]{:S(2)}, u32[]{:S(2)}) %all-to-all-start.2) | async-done | bytes 262176 | tf_op jit(solution)/shard_map/all_to_all | solution.py:466
  52.4 0.0 copy-done.1
  52.4 0.9 norm.1
  53.3 4.8 %all-to-all-start.3 = ((bf16[8,8,2048]{2,1,0:T(8,128)(2,1)}), bf16[8,8,2048]{2,1,0:T(8,128)(2,1)S(1)}, u32[]{:S(2)}, u32[]{:S(2)}) async-start(bf16[8,8,2048]{2,1,0:T(8,128)(2,1)} %get-tuple-element.33), calls=%async_computation.3 | async-start | bytes 524288 | tf_op jit(solution)/shard_map/all_to_all | solution.py:478
  58.1 0.0 copy-done.2
  58.1 0.1 dynamic-slice_bitcast_fusion
  58.1 0.1 copy.23.own_docs
  58.2 0.1 slice_reduce_fusion
  58.4 0.1 tile.14
  58.4 1.8 %fetch.1.gate_weight = bf16[2048,640]{1,0:T(8,128)(2,1)S(1)} custom-call(bf16[2048,640]{1,0:T(8,128)(2,1)} %weight.3), custom_call_target="tpu_custom_call" | custom-call | tf_op jit(solution)/shard_map/fetch/pallas_call | solution.py:475
  60.2 6.5 %all-to-all-done.3 = bf16[8,8,2048]{2,1,0:T(8,128)(2,1)S(1)} async-done(((bf16[8,8,2048]{2,1,0:T(8,128)(2,1)}), bf16[8,8,2048]{2,1,0:T(8,128)(2,1)S(1)}, u32[]{:S(2)}, u32[]{:S(2)}) %all-to-all-start.3) | async-done | bytes 262176 | tf_op jit(solution)/shard_map/all_to_all | solution.py:478
  66.8 3.5 %feed.1 = f32[32,128]{1,0:T(8,128)} custom-call(bf16[64,2048]{1,0:T(8,128)(2,1)S(1)} %bitcast.14, bf16[2048,640]{1,0:T(8,128)(2,1)S(1)} %fetch.1.gate_weight, bf16[2048,640]{1,0:T(8,128)(2,1)} %up_weight.1, f32[1,640]{1,0:T(1,128)S(1)} %get-tuple-element.35.down_score, f32[64,1]{1,0:T(8,128)S(1)} %fusion.4.own_score, s32[64,1]{1,0:T(8,128)S(1)} %copy.23.own_docs), custom_call_target="tpu_custom_call" | custom-call | tf_op jit(solution)/shard_map/feed/pallas_call | solution.py:484
  70.3 4.9 %all-to-all-start.4 = ((f32[32,1,128]{2,1,0:T(1,128)}), f32[32,1,128]{2,1,0:T(1,128)S(1)}, u32[]{:S(2)}, u32[]{:S(2)}) async-start(f32[32,1,128]{2,1,0:T(1,128)} %bitcast.12), calls=%async_computation.4 | async-start | bytes 32768 | tf_op jit(solution)/shard_map/all_to_all | solution.py:489
  75.2 7.3 %all-to-all-done.4.terms = f32[32,1,128]{2,1,0:T(1,128)S(1)} async-done(((f32[32,1,128]{2,1,0:T(1,128)}), f32[32,1,128]{2,1,0:T(1,128)S(1)}, u32[]{:S(2)}, u32[]{:S(2)}) %all-to-all-start.4) | async-done | bytes 16416 | tf_op jit(solution)/shard_map/all_to_all | solution.py:489
  82.5 0.6 fold.1
  83.2 4.8 %all-to-all-start.5 = ((f32[8,1,128]{2,1,0:T(1,128)}), f32[8,1,128]{2,1,0:T(1,128)S(1)}, u32[]{:S(2)}, u32[]{:S(2)}) async-start(f32[8,1,128]{2,1,0:T(1,128)} %fold.1), calls=%async_computation.5 | async-start | bytes 8192 | tf_op jit(solution)/shard_map/all_to_all | solution.py:491
  88.0 0.2 convert_reduce_fusion
  88.2 6.1 %all-to-all-done.5 = f32[8,1,128]{2,1,0:T(1,128)S(1)} async-done(((f32[8,1,128]{2,1,0:T(1,128)}), f32[8,1,128]{2,1,0:T(1,128)S(1)}, u32[]{:S(2)}, u32[]{:S(2)}) %all-to-all-start.5) | async-done | bytes 4128 | tf_op jit(solution)/shard_map/all_to_all | solution.py:491
  94.3 0.5 slice_divide_fusion
  (6 shorter events, 0.1 us)
Async XLA Ops:
  2.4 23.3 %copy-start = (f32[2048]{0:T(1024)S(1)}, f32[2048]{0:T(1024)}, u32[]{:S(2)}) copy-start(f32[2048]{0:T(1024)} %param.29) | copy-start | bytes 24580
  2.4 9.7 %collective-permute-start.1 = (bf16[520,256]{1,0:T(8,128)(2,1)S(1)}, bf16[520,256]{1,0:T(8,128)(2,1)S(1)}, u32[]{:S(2)}, u32[]{:S(2)}) collective-permute-start(bf16[520,256]{1,0:T(8,128)(2,1)S(1)} %get-tuple-element.22.first), channel_id=1, source_target_pairs={{0,4},{1,5},{2,6},{3,7},{4,0},{5,1},{6,2},{7,3},{8,12},{9,13},{10,... | collective-permute-start | bytes 798728 | tf_op jit(solution)/shard_map/ppermute | solution.py:385
  5.5 7.3 %collective-permute-start = (bf16[520,256]{1,0:T(8,128)(2,1)S(1)}, bf16[520,256]{1,0:T(8,128)(2,1)S(1)}, u32[]{:S(2)}, u32[]{:S(2)}) collective-permute-start(bf16[520,256]{1,0:T(8,128)(2,1)S(1)} %get-tuple-element.22.first), channel_id=1, source_target_pairs={{0,1},{1,0},{2,3},{3,2},{4,5},{5,4},{6,7},{7,6},{8,9},{9,8},{10,11... | collective-permute-start | bytes 798728 | tf_op jit(solution)/shard_map/ppermute | solution.py:385
  5.5 12.4 %all-to-all-start = ((bf16[8,64,256]{2,1,0:T(8,128)(2,1)}), bf16[8,64,256]{2,1,0:T(8,128)(2,1)S(1)}, u32[]{:S(2)}, u32[]{:S(2)}) async-start(bf16[8,64,256]{2,1,0:T(8,128)(2,1)} %get-tuple-element.21), calls=%async_computation | async-start | bytes 524288 | tf_op jit(solution)/shard_map/all_to_all | solution.py:412
  12.1 2.6 %collective-permute-start.2 = (bf16[264,256]{1,0:T(8,128)(2,1)S(1)}, bf16[264,256]{1,0:T(8,128)(2,1)S(1)}, u32[]{:S(2)}, u32[]{:S(2)}) collective-permute-start(bf16[264,256]{1,0:T(8,128)(2,1)S(1)} %slice.16), channel_id=1, source_target_pairs={{0,1},{1,0},{2,3},{3,2},{4,5},{5,4},{6,7},{7,6},{8,9},{9,8},{10,11... | collective-permute-start | bytes 405512 | tf_op jit(solution)/shard_map/ppermute | solution.py:385
  12.3 2.5 %collective-permute-start.3 = (bf16[256,256]{1,0:T(8,128)(2,1)S(1)}, bf16[256,256]{1,0:T(8,128)(2,1)S(1)}, u32[]{:S(2)}, u32[]{:S(2)}) collective-permute-start(bf16[256,256]{1,0:T(8,128)(2,1)S(1)} %slice.17), channel_id=1, source_target_pairs={{0,1},{1,0},{2,3},{3,2},{4,5},{5,4},{6,7},{7,6},{8,9},{9,8},{10,11... | collective-permute-start | bytes 393224 | tf_op jit(solution)/shard_map/ppermute | solution.py:385
  21.9 11.4 %all-to-all-start.1 = ((bf16[8,136,128]{2,1,0:T(8,128)(2,1)}), bf16[8,136,128]{2,1,0:T(8,128)(2,1)S(1)}, u32[]{:S(2)}, u32[]{:S(2)}) async-start(bf16[8,136,128]{2,1,0:T(8,128)(2,1)} %attention.1), calls=%async_computation.1 | async-start | bytes 557056 | tf_op jit(solution)/shard_map/all_to_all | solution.py:462
  25.7 26.8 %copy-start.1 = (f32[2048]{0:T(1024)S(1)}, f32[2048]{0:T(1024)}, u32[]{:S(2)}) copy-start(f32[2048]{0:T(1024)} %param.25) | copy-start | bytes 24580
  25.7 32.4 %copy-start.2 = (s32[2048]{0:T(1024)S(1)}, s32[2048]{0:T(1024)}, u32[]{:S(2)}) copy-start(s32[2048]{0:T(1024)} %param.32) | copy-start | bytes 24580
  34.4 18.0 %all-to-all-start.2 = ((bf16[8,8,2048]{2,1,0:T(8,128)(2,1)}), bf16[8,8,2048]{2,1,0:T(8,128)(2,1)S(1)}, u32[]{:S(2)}, u32[]{:S(2)}) async-start(bf16[8,8,2048]{2,1,0:T(8,128)(2,1)} %bitcast.8), calls=%async_computation.2 | async-start | bytes 524288 | tf_op jit(solution)/shard_map/all_to_all | solution.py:466
  53.3 13.5 %all-to-all-start.3 = ((bf16[8,8,2048]{2,1,0:T(8,128)(2,1)}), bf16[8,8,2048]{2,1,0:T(8,128)(2,1)S(1)}, u32[]{:S(2)}, u32[]{:S(2)}) async-start(bf16[8,8,2048]{2,1,0:T(8,128)(2,1)} %get-tuple-element.33), calls=%async_computation.3 | async-start | bytes 524288 | tf_op jit(solution)/shard_map/all_to_all | solution.py:478
  70.3 12.3 %all-to-all-start.4 = ((f32[32,1,128]{2,1,0:T(1,128)}), f32[32,1,128]{2,1,0:T(1,128)S(1)}, u32[]{:S(2)}, u32[]{:S(2)}) async-start(f32[32,1,128]{2,1,0:T(1,128)} %bitcast.12), calls=%async_computation.4 | async-start | bytes 32768 | tf_op jit(solution)/shard_map/all_to_all | solution.py:489
  83.2 11.1 %all-to-all-start.5 = ((f32[8,1,128]{2,1,0:T(1,128)}), f32[8,1,128]{2,1,0:T(1,128)S(1)}, u32[]{:S(2)}, u32[]{:S(2)}) async-start(f32[8,1,128]{2,1,0:T(1,128)} %fold.1), calls=%async_computation.5 | async-start | bytes 8192 | tf_op jit(solution)/shard_map/all_to_all | solution.py:491

commit v8 on v7

--- a/solution.py
+++ b/solution.py
@@ -28,7 +28,7 @@
 
 
 def project_kernel(states, gain, weight, keys, values, buckets, out, payload, states_here, gain_here, weight_here,
-                   buckets_here, arrivals):
+                   buckets_here, queries_here, arrivals, sent):
     count = keys.shape[0]
     pairs = (
         (states, states_here),
@@ -49,10 +49,14 @@
     payload[count : count + 8, :] = jnp.broadcast_to(both, (8, both.shape[1])).astype(BF)
     copies[2].wait()
     queries = jnp.dot(normed, weight_here[...], preferred_element_type=F32).astype(BF)
-    for chip in range(out.shape[0]):
-        out[chip] = queries
+    queries_here[...] = queries
+    sends = [pltpu.make_async_copy(queries_here, out.at[i], sent.at[i]) for i in range(out.shape[0])]
+    for send in sends:
+        send.start()
     copies[4].wait()
     copies[5].wait()
+    for send in sends:
+        send.wait()
 
 
 def near_kernel(rank, first, second, bias_table, page_table, query_lengths, doc_query, doc_rows, keys_aug, values_t,
@@ -173,7 +177,7 @@
                 keys_aug[h, span, :] = jnp.where(keep, half, bias[:, h * 128 : (h + 1) * 128] + marks).astype(BF)
 
 
-def attention_kernel(queries, keys_near, keys_far, values_near, values_far, extra, out, rows_aug):
+def attention_kernel(queries, keys_near, keys_far, values_near, values_far, extra, out, rows_aug, parts, sent):
     chips, tok_dev, width = queries.shape
     heads = keys_near.shape[0]
     depth = width // heads
@@ -210,6 +214,7 @@
             summed += jnp.dot(values[span, :], weights.astype(BF), preferred_element_type=F32)
         sums.append(summed / total)
         logs.append(top + jnp.log(total))
+    sends = []
     for duo in range(chips // 2):
         lanes = slice(duo * 128, (duo + 1) * 128)
         pad = [jnp.zeros((6, 128), F32)]
@@ -228,11 +233,15 @@
         for which in range(2):
             a, b, c = split_three(stat[which])
             packed = [a[0:2].astype(F32), b[0:2].astype(F32), c[0:2].astype(F32), jnp.zeros((2, 128), F32)]
-            out[duo * 2 + which, 0:128, :] = block[which].astype(BF)
-            out[duo * 2 + which, 128:136, :] = jnp.concatenate(packed, axis=0).astype(BF)
-
-
-def combine_kernel(parts, out_weight, out):
+            parts[duo * 2 + which, 0:128, :] = block[which].astype(BF)
+            parts[duo * 2 + which, 128:136, :] = jnp.concatenate(packed, axis=0).astype(BF)
+        sends.append(pltpu.make_async_copy(parts.at[pl.ds(duo * 2, 2)], out.at[pl.ds(duo * 2, 2)], sent.at[duo]))
+        sends[duo].start()
+    for send in sends:
+        send.wait()
+
+
+def combine_kernel(parts, out_weight, out, product, sent):
     chips = parts.shape[0]
     logs = []
     for chip in range(chips):
@@ -252,17 +261,28 @@
             sums[r] = sums[r] + share[r : r + 1] * parts[chip, r * 64 : (r + 1) * 64, :].astype(F32)
     joined = jnp.concatenate(sums, axis=0).T
     context = jnp.concatenate([joined[0:64], joined[64:128]], axis=1).astype(BF)
-    out[...] = jnp.dot(context, out_weight[...], preferred_element_type=F32).astype(BF)
-
-
-def norm_kernel(terms, states, gain, score_vector, out, score):
+    sends = []
+    for i in range(product.shape[0]):
+        cols = slice(i * product.shape[2], (i + 1) * product.shape[2])
+        product[i] = jnp.dot(context, out_weight[:, cols], preferred_element_type=F32).astype(BF)
+        place = out.at[:, pl.ds(i * product.shape[2], product.shape[2])]
+        sends.append(pltpu.make_async_copy(product.at[i], place, sent.at[i]))
+        sends[i].start()
+    for send in sends:
+        send.wait()
+
+
+def norm_kernel(terms, states, gain, score_vector, out, score, normed, sent):
     hidden = states[...].astype(F32)
     for source in range(terms.shape[0]):
         hidden = hidden + terms[source].astype(F32)
-    normed = rms_scale(hidden, gain[...]).astype(BF)
-    for target in range(out.shape[0]):
-        out[target] = normed
+    normed[...] = rms_scale(hidden, gain[...]).astype(BF)
+    sends = [pltpu.make_async_copy(normed, out.at[i], sent.at[i]) for i in range(out.shape[0])]
+    for send in sends:
+        send.start()
     score[...] = jnp.broadcast_to(jnp.sum(hidden * score_vector[...], axis=-1, keepdims=True), score.shape)
+    for send in sends:
+        send.wait()
 
 
 def down_kernel(weight, score_vector, out_weight, out, fetched, weight_here, arrivals):
@@ -334,13 +354,13 @@
     return pl.BlockSpec(memory_space=pl.ANY)
 
 
-def call(kernel, name, shapes, specs, scratch=()):
+def call(kernel, name, shapes, specs, scratch=(), results=None):
     single = not isinstance(shapes, (list, tuple))
     return pl.pallas_call(
         kernel,
         out_shape=shapes,
         in_specs=specs,
-        out_specs=vmem() if single else [vmem()] * len(shapes),
+        out_specs=results or (vmem() if single else [vmem()] * len(shapes)),
         scratch_shapes=list(scratch),
         compiler_params=pltpu.CompilerParams(vmem_limit_bytes=40 << 20),
         name=name,
@@ -395,8 +415,11 @@
             pltpu.VMEM((1, model), F32),
             pltpu.VMEM((model, local_width), BF),
             pltpu.VMEM((local_pages, page_len), jnp.int32),
+            pltpu.VMEM((tok_dev, local_width), BF),
             pltpu.SemaphoreType.DMA((6,)),
+            pltpu.SemaphoreType.DMA((group,)),
         ],
+        [hbm(), vmem()],
     )(
         in_hbm(doc_states),
         in_hbm(gain_attn.reshape(1, model)),
@@ -448,7 +471,12 @@
         "attention",
         shape((group, 136, 128), BF),
         [vmem()] * 6,
-        [pltpu.VMEM((local_heads, group * tok_dev, 128), BF)],
+        [
+            pltpu.VMEM((local_heads, group * tok_dev, 128), BF),
+            pltpu.VMEM((group, 136, 128), BF),
+            pltpu.SemaphoreType.DMA((group // 2,)),
+        ],
+        hbm(),
     )(gathered, keys_near, keys_away, values_near, values_away, extra)
     partials, down_weight, late_weight = lax.optimization_barrier((partials, wo_ffn, out_weight))
     hidden_units = wi_gate.shape[1]
@@ -460,7 +488,11 @@
         [pltpu.VMEM(wo_ffn.shape, BF), pltpu.SemaphoreType.DMA((2,))],
     )(in_hbm(down_weight), score_vector.reshape(1, model), in_hbm(late_weight))
     returned = lax.all_to_all(partials, "page", 0, 0, axis_index_groups=groups, tiled=True)
-    projected = call(combine_kernel, "combine", shape((tok_dev, model), BF), [vmem()] * 2)(returned, fetched)
+    projected = call(
+        combine_kernel, "combine", shape((tok_dev, model), BF), [vmem()] * 2,
+        [pltpu.VMEM((4, tok_dev, model // 4), BF), pltpu.SemaphoreType.DMA((4,))],
+        hbm(),
+    )(returned, fetched)
 
     own = tok_dev // head_size
     terms = lax.all_to_all(projected.reshape(head_size, own, model), "head", 0, 0, tiled=True)
@@ -470,6 +502,8 @@
         "norm",
         [shape((head_size, own, model), BF), shape((own, 128), F32)],
         [vmem()] * 4,
+        [pltpu.VMEM((own, model), BF), pltpu.SemaphoreType.DMA((head_size,))],
+        [hbm(), vmem()],
     )(terms, own_states, gain_ffn.reshape(1, model), score_vector.reshape(1, model))
     spread, late_gate = lax.optimization_barrier((spread, wi_gate))
     gate_here = call(

time: 96.7 us -> 96.8 us (level)
  no operation moved by 1% of the time
where the time goes in v8:
time: 96.8 us; the launch traced here: 94.9 us
  waiting for transfers between devices  37.1 us (38%)
  starting transfers between devices  35.1 us (36%)
  Pallas kernels  20.6 us (21%)
  local copies, waits for them, and re-layouts  1.17 us (1%)
    all_to_all x1, waiting for transfers between devices, per_device(): lax.all_to_all(projected.reshape(head_size, own, model), 'head', 0, 0, ti...  8.69 us
    all_to_all x1, starting transfers between devices, per_device(): lax.all_to_all(projected.reshape(head_size, own, model), 'head', 0, 0, ti...  8.59 us
    all_to_all x1, waiting for transfers between devices, per_device(): arrived = lax.all_to_all(doc_sums, 'page', 0, 0, tiled=True)  7.33 us
    all_to_all x1, waiting for transfers between devices, per_device(): lax.all_to_all(spread, 'head', 0, 0, tiled=True).reshape(tok_dev, model)  6.54 us
    all_to_all x1, waiting for transfers between devices, per_device(): lax.all_to_all(pooled, 'head', 0, 0, tiled=True)  6.05 us
    all_to_all x1, starting transfers between devices, per_device(): arrived = lax.all_to_all(doc_sums, 'page', 0, 0, tiled=True)  4.88 us
    all_to_all x1, starting transfers between devices, per_device(): lax.all_to_all(pooled, 'head', 0, 0, tiled=True)  4.82 us
    all_to_all x1, starting transfers between devices, per_device(): lax.all_to_all(spread, 'head', 0, 0, tiled=True).reshape(tok_dev, model)  4.79 us
  transfers between devices with their start and end apart: 10, of which 7 were waited for; matrix products, arithmetic and copies ran while one was open for 1% of the time, Pallas kernels for 9%

profile of v8, /device:TPU:32, one launch (start us, length us, event | category | flops | bytes accessed | tf_op | source)
XLA Modules:
  0.0 94.9 jit_solution(13093695301827728427)
XLA Ops:
  0.0 2.5 %project.1 = (bf16[8,64,256]{2,1,0:T(8,128)(2,1)}, bf16[520,256]{1,0:T(8,128)(2,1)S(1)}) custom-call(bf16[64,2048]{1,0:T(8,128)(2,1)} %states.1, f32[1,2048]{1,0:T(1,128)} %bitcast.21, bf16[2048,256]{1,0:T(8,128)(2,1)} %weight.1, bf16[256,256]{1,0:T(8,128)(2,1)} %bitcast.18, bf16[256,256]{1,0:T(8,128)(2,1)} %bitcast.19, s32[2,128]{1,0:T(2,128)} %buckets.1), custom_call_target="tpu_custom_call" | custom-call | tf_op jit(solution)/shard_map/project/pallas_call | solution.py:408
  2.5 0.0 copy-start
  2.5 3.1 %collective-permute-start.1 = (bf16[520,256]{1,0:T(8,128)(2,1)S(1)}, bf16[520,256]{1,0:T(8,128)(2,1)S(1)}, u32[]{:S(2)}, u32[]{:S(2)}) collective-permute-start(bf16[520,256]{1,0:T(8,128)(2,1)S(1)} %get-tuple-element.22.first), channel_id=1, source_target_pairs={{0,4},{1,5},{2,6},{3,7},{4,0},{5,1},{6,2},{7,3},{8,12},{9,13},{10,... | collective-permute-start | bytes 798728 | tf_op jit(solution)/shard_map/ppermute | solution.py:405
  5.6 0.0 collective-permute-start
  5.6 4.5 %all-to-all-start = ((bf16[8,64,256]{2,1,0:T(8,128)(2,1)}), bf16[8,64,256]{2,1,0:T(8,128)(2,1)S(1)}, u32[]{:S(2)}, u32[]{:S(2)}) async-start(bf16[8,64,256]{2,1,0:T(8,128)(2,1)} %get-tuple-element.21), calls=%async_computation | async-start | bytes 524288 | tf_op jit(solution)/shard_map/all_to_all | solution.py:435
  10.1 2.1 %collective-permute-done.1.first = bf16[520,256]{1,0:T(8,128)(2,1)S(1)} collective-permute-done((bf16[520,256]{1,0:T(8,128)(2,1)S(1)}, bf16[520,256]{1,0:T(8,128)(2,1)S(1)}, u32[]{:S(2)}, u32[]{:S(2)}) %collective-permute-start.1) | collective-permute-done | bytes 266272 | tf_op jit(solution)/shard_map/ppermute | solution.py:405
  12.2 0.1 collective-permute-start.2
  12.3 0.6 collective-permute-start.3
  12.9 0.0 collective-permute-done.second
  12.9 1.9 %near.1 = (bf16[4,512,128]{2,1,0:T(8,128)(2,1)S(1)}, bf16[256,512]{1,0:T(8,128)(2,1)S(1)}, bf16[512,128]{1,0:T(8,128)(2,1)S(1)}) custom-call(s32[1]{0:T(128)} %bitcast.3.rank, bf16[520,256]{1,0:T(8,128)(2,1)S(1)} %get-tuple-element.22.first, bf16[520,256]{1,0:T(8,128)(2,1)S(1)} %collective-permute-done.second, f32[4,32]{1,0:T(4,128)} %bitcast.22, ...), custom_call_target="tpu_custom_call" | custom-call | tf_op jit(solution)/shard_map/near/pallas_call | solution.py:450
  14.8 0.0 collective-permute-done.3.third
  14.9 0.0 collective-permute-done.2.second
  14.9 1.5 %away.1 = (bf16[4,512,128]{2,1,0:T(8,128)(2,1)S(1)}, bf16[256,512]{1,0:T(8,128)(2,1)S(1)}) custom-call(s32[1]{0:T(128)} %bitcast.3.rank, bf16[520,256]{1,0:T(8,128)(2,1)S(1)} %collective-permute-done.1.first, bf16[264,256]{1,0:T(8,128)(2,1)S(1)} %collective-permute-done.2.second, bf16[256,256]{1,0:T(8,128)(2,1)S(1)} %collective-permute-done.3.third, ...), custom_call_target="tpu_custom_call" | custom-call | tf_op jit(solution)/shard_map/away/pallas_call | solution.py:462
  16.4 1.6 %all-to-all-done.queries = bf16[8,64,256]{2,1,0:T(8,128)(2,1)S(1)} async-done(((bf16[8,64,256]{2,1,0:T(8,128)(2,1)}), bf16[8,64,256]{2,1,0:T(8,128)(2,1)S(1)}, u32[]{:S(2)}, u32[]{:S(2)}) %all-to-all-start) | async-done | bytes 262176 | tf_op jit(solution)/shard_map/all_to_all | solution.py:435
  18.0 3.9 %attention.1 = bf16[8,136,128]{2,1,0:T(8,128)(2,1)} custom-call(bf16[8,64,256]{2,1,0:T(8,128)(2,1)S(1)} %all-to-all-done.queries, bf16[4,512,128]{2,1,0:T(8,128)(2,1)S(1)} %get-tuple-element.23.keys_near, bf16[4,512,128]{2,1,0:T(8,128)(2,1)S(1)} %get-tuple-element.24.keys_far, bf16[256,512]{1,0:T(8,128)(2,1)S(1)} %get-tuple-element.25.values_near, ...), custom_call_target="tpu_custom_call" | custom-call | tf_op jit(solution)/shard_map/attention/pallas_call | solution.py:469
  22.0 3.8 %all-to-all-start.1 = ((bf16[8,136,128]{2,1,0:T(8,128)(2,1)}), bf16[8,136,128]{2,1,0:T(8,128)(2,1)S(1)}, u32[]{:S(2)}, u32[]{:S(2)}) async-start(bf16[8,136,128]{2,1,0:T(8,128)(2,1)} %attention.1), calls=%async_computation.1 | async-start | bytes 557056 | tf_op jit(solution)/shard_map/all_to_all | solution.py:490
  25.8 0.0 copy-done
  25.8 0.0 copy-start.1
  25.8 0.0 copy-start.2
  25.8 2.9 %down.1 = (f32[1,640]{1,0:T(1,128)S(1)}, bf16[256,2048]{1,0:T(8,128)(2,1)S(1)}) custom-call(bf16[640,2048]{1,0:T(8,128)(2,1)} %weight.2, f32[1,2048]{1,0:T(1,128)S(1)} %bitcast.15, bf16[256,2048]{1,0:T(8,128)(2,1)} %out_weight), custom_call_target="tpu_custom_call" | custom-call | tf_op jit(solution)/shard_map/down/pallas_call | solution.py:483
  28.7 4.7 %all-to-all-done.1.parts = bf16[8,136,128]{2,1,0:T(8,128)(2,1)S(1)} async-done(((bf16[8,136,128]{2,1,0:T(8,128)(2,1)}), bf16[8,136,128]{2,1,0:T(8,128)(2,1)S(1)}, u32[]{:S(2)}, u32[]{:S(2)}) %all-to-all-start.1) | async-done | bytes 278560 | tf_op jit(solution)/shard_map/all_to_all | solution.py:490
  33.4 1.1 %combine.1 = bf16[64,2048]{1,0:T(8,128)(2,1)} custom-call(bf16[8,136,128]{2,1,0:T(8,128)(2,1)S(1)} %all-to-all-done.1.parts, bf16[256,2048]{1,0:T(8,128)(2,1)S(1)} %get-tuple-element.31.out_weight), custom_call_target="tpu_custom_call" | custom-call | tf_op jit(solution)/shard_map/combine/pallas_call | solution.py:491
  34.5 8.6 %all-to-all-start.2 = ((bf16[8,8,2048]{2,1,0:T(8,128)(2,1)}), bf16[8,8,2048]{2,1,0:T(8,128)(2,1)S(1)}, u32[]{:S(2)}, u32[]{:S(2)}) async-start(bf16[8,8,2048]{2,1,0:T(8,128)(2,1)} %bitcast.8), calls=%async_computation.2 | async-start | bytes 524288 | tf_op jit(solution)/shard_map/all_to_all | solution.py:498
  43.1 0.8 constant_dynamic-slice_fusion.states
  43.8 8.7 %all-to-all-done.2.terms = bf16[8,8,2048]{2,1,0:T(8,128)(2,1)S(1)} async-done(((bf16[8,8,2048]{2,1,0:T(8,128)(2,1)}), bf16[8,8,2048]{2,1,0:T(8,128)(2,1)S(1)}, u32[]{:S(2)}, u32[]{:S(2)}) %all-to-all-start.2) | async-done | bytes 262176 | tf_op jit(solution)/shard_map/all_to_all | solution.py:498
  52.5 0.0 copy-done.1
  52.5 0.9 norm.1
  53.5 4.8 %all-to-all-start.3 = ((bf16[8,8,2048]{2,1,0:T(8,128)(2,1)}), bf16[8,8,2048]{2,1,0:T(8,128)(2,1)S(1)}, u32[]{:S(2)}, u32[]{:S(2)}) async-start(bf16[8,8,2048]{2,1,0:T(8,128)(2,1)} %get-tuple-element.33), calls=%async_computation.3 | async-start | bytes 524288 | tf_op jit(solution)/shard_map/all_to_all | solution.py:512
  58.2 0.0 copy-done.2
  58.2 0.1 dynamic-slice_bitcast_fusion
  58.3 0.1 copy.23.own_docs
  58.4 0.1 slice_reduce_fusion
  58.5 0.1 tile.14
  58.6 1.8 %fetch.1.gate_weight = bf16[2048,640]{1,0:T(8,128)(2,1)S(1)} custom-call(bf16[2048,640]{1,0:T(8,128)(2,1)} %weight.3), custom_call_target="tpu_custom_call" | custom-call | tf_op jit(solution)/shard_map/fetch/pallas_call | solution.py:509
  60.4 6.5 %all-to-all-done.3 = bf16[8,8,2048]{2,1,0:T(8,128)(2,1)S(1)} async-done(((bf16[8,8,2048]{2,1,0:T(8,128)(2,1)}), bf16[8,8,2048]{2,1,0:T(8,128)(2,1)S(1)}, u32[]{:S(2)}, u32[]{:S(2)}) %all-to-all-start.3) | async-done | bytes 262176 | tf_op jit(solution)/shard_map/all_to_all | solution.py:512
  66.9 3.5 %feed.1 = f32[32,128]{1,0:T(8,128)} custom-call(bf16[64,2048]{1,0:T(8,128)(2,1)S(1)} %bitcast.14, bf16[2048,640]{1,0:T(8,128)(2,1)S(1)} %fetch.1.gate_weight, bf16[2048,640]{1,0:T(8,128)(2,1)} %up_weight.1, f32[1,640]{1,0:T(1,128)S(1)} %get-tuple-element.35.down_score, f32[64,1]{1,0:T(8,128)S(1)} %fusion.4.own_score, s32[64,1]{1,0:T(8,128)S(1)} %copy.23.own_docs), custom_call_target="tpu_custom_call" | custom-call | tf_op jit(solution)/shard_map/feed/pallas_call | solution.py:518
  70.4 4.9 %all-to-all-start.4 = ((f32[32,1,128]{2,1,0:T(1,128)}), f32[32,1,128]{2,1,0:T(1,128)S(1)}, u32[]{:S(2)}, u32[]{:S(2)}) async-start(f32[32,1,128]{2,1,0:T(1,128)} %bitcast.12), calls=%async_computation.4 | async-start | bytes 32768 | tf_op jit(solution)/shard_map/all_to_all | solution.py:523
  75.3 7.3 %all-to-all-done.4.terms = f32[32,1,128]{2,1,0:T(1,128)S(1)} async-done(((f32[32,1,128]{2,1,0:T(1,128)}), f32[32,1,128]{2,1,0:T(1,128)S(1)}, u32[]{:S(2)}, u32[]{:S(2)}) %all-to-all-start.4) | async-done | bytes 16416 | tf_op jit(solution)/shard_map/all_to_all | solution.py:523
  82.7 0.6 fold.1
  83.3 4.8 %all-to-all-start.5 = ((f32[8,1,128]{2,1,0:T(1,128)}), f32[8,1,128]{2,1,0:T(1,128)S(1)}, u32[]{:S(2)}, u32[]{:S(2)}) async-start(f32[8,1,128]{2,1,0:T(1,128)} %fold.1), calls=%async_computation.5 | async-start | bytes 8192 | tf_op jit(solution)/shard_map/all_to_all | solution.py:525
  88.1 0.2 convert_reduce_fusion
  88.3 6.1 %all-to-all-done.5 = f32[8,1,128]{2,1,0:T(1,128)S(1)} async-done(((f32[8,1,128]{2,1,0:T(1,128)}), f32[8,1,128]{2,1,0:T(1,128)S(1)}, u32[]{:S(2)}, u32[]{:S(2)}) %all-to-all-start.5) | async-done | bytes 4128 | tf_op jit(solution)/shard_map/all_to_all | solution.py:525
  94.4 0.5 slice_divide_fusion
  (6 shorter events, 0.1 us)
Async XLA Ops:
  2.5 23.3 %copy-start = (f32[2048]{0:T(1024)S(1)}, f32[2048]{0:T(1024)}, u32[]{:S(2)}) copy-start(f32[2048]{0:T(1024)} %param.29) | copy-start | bytes 24580
  2.5 9.7 %collective-permute-start.1 = (bf16[520,256]{1,0:T(8,128)(2,1)S(1)}, bf16[520,256]{1,0:T(8,128)(2,1)S(1)}, u32[]{:S(2)}, u32[]{:S(2)}) collective-permute-start(bf16[520,256]{1,0:T(8,128)(2,1)S(1)} %get-tuple-element.22.first), channel_id=1, source_target_pairs={{0,4},{1,5},{2,6},{3,7},{4,0},{5,1},{6,2},{7,3},{8,12},{9,13},{10,... | collective-permute-start | bytes 798728 | tf_op jit(solution)/shard_map/ppermute | solution.py:405
  5.6 7.3 %collective-permute-start = (bf16[520,256]{1,0:T(8,128)(2,1)S(1)}, bf16[520,256]{1,0:T(8,128)(2,1)S(1)}, u32[]{:S(2)}, u32[]{:S(2)}) collective-permute-start(bf16[520,256]{1,0:T(8,128)(2,1)S(1)} %get-tuple-element.22.first), channel_id=1, source_target_pairs={{0,1},{1,0},{2,3},{3,2},{4,5},{5,4},{6,7},{7,6},{8,9},{9,8},{10,11... | collective-permute-start | bytes 798728 | tf_op jit(solution)/shard_map/ppermute | solution.py:405
  5.6 12.4 %all-to-all-start = ((bf16[8,64,256]{2,1,0:T(8,128)(2,1)}), bf16[8,64,256]{2,1,0:T(8,128)(2,1)S(1)}, u32[]{:S(2)}, u32[]{:S(2)}) async-start(bf16[8,64,256]{2,1,0:T(8,128)(2,1)} %get-tuple-element.21), calls=%async_computation | async-start | bytes 524288 | tf_op jit(solution)/shard_map/all_to_all | solution.py:435
  12.2 2.6 %collective-permute-start.2 = (bf16[264,256]{1,0:T(8,128)(2,1)S(1)}, bf16[264,256]{1,0:T(8,128)(2,1)S(1)}, u32[]{:S(2)}, u32[]{:S(2)}) collective-permute-start(bf16[264,256]{1,0:T(8,128)(2,1)S(1)} %slice.16), channel_id=1, source_target_pairs={{0,1},{1,0},{2,3},{3,2},{4,5},{5,4},{6,7},{7,6},{8,9},{9,8},{10,11... | collective-permute-start | bytes 405512 | tf_op jit(solution)/shard_map/ppermute | solution.py:405
  12.3 2.5 %collective-permute-start.3 = (bf16[256,256]{1,0:T(8,128)(2,1)S(1)}, bf16[256,256]{1,0:T(8,128)(2,1)S(1)}, u32[]{:S(2)}, u32[]{:S(2)}) collective-permute-start(bf16[256,256]{1,0:T(8,128)(2,1)S(1)} %slice.17), channel_id=1, source_target_pairs={{0,1},{1,0},{2,3},{3,2},{4,5},{5,4},{6,7},{7,6},{8,9},{9,8},{10,11... | collective-permute-start | bytes 393224 | tf_op jit(solution)/shard_map/ppermute | solution.py:405
  22.0 11.4 %all-to-all-start.1 = ((bf16[8,136,128]{2,1,0:T(8,128)(2,1)}), bf16[8,136,128]{2,1,0:T(8,128)(2,1)S(1)}, u32[]{:S(2)}, u32[]{:S(2)}) async-start(bf16[8,136,128]{2,1,0:T(8,128)(2,1)} %attention.1), calls=%async_computation.1 | async-start | bytes 557056 | tf_op jit(solution)/shard_map/all_to_all | solution.py:490
  25.8 26.8 %copy-start.1 = (f32[2048]{0:T(1024)S(1)}, f32[2048]{0:T(1024)}, u32[]{:S(2)}) copy-start(f32[2048]{0:T(1024)} %param.25) | copy-start | bytes 24580
  25.8 32.5 %copy-start.2 = (s32[2048]{0:T(1024)S(1)}, s32[2048]{0:T(1024)}, u32[]{:S(2)}) copy-start(s32[2048]{0:T(1024)} %param.32) | copy-start | bytes 24580
  34.5 18.0 %all-to-all-start.2 = ((bf16[8,8,2048]{2,1,0:T(8,128)(2,1)}), bf16[8,8,2048]{2,1,0:T(8,128)(2,1)S(1)}, u32[]{:S(2)}, u32[]{:S(2)}) async-start(bf16[8,8,2048]{2,1,0:T(8,128)(2,1)} %bitcast.8), calls=%async_computation.2 | async-start | bytes 524288 | tf_op jit(solution)/shard_map/all_to_all | solution.py:498
  53.5 13.5 %all-to-all-start.3 = ((bf16[8,8,2048]{2,1,0:T(8,128)(2,1)}), bf16[8,8,2048]{2,1,0:T(8,128)(2,1)S(1)}, u32[]{:S(2)}, u32[]{:S(2)}) async-start(bf16[8,8,2048]{2,1,0:T(8,128)(2,1)} %get-tuple-element.33), calls=%async_computation.3 | async-start | bytes 524288 | tf_op jit(solution)/shard_map/all_to_all | solution.py:512
  70.4 12.2 %all-to-all-start.4 = ((f32[32,1,128]{2,1,0:T(1,128)}), f32[32,1,128]{2,1,0:T(1,128)S(1)}, u32[]{:S(2)}, u32[]{:S(2)}) async-start(f32[32,1,128]{2,1,0:T(1,128)} %bitcast.12), calls=%async_computation.4 | async-start | bytes 32768 | tf_op jit(solution)/shard_map/all_to_all | solution.py:523
  83.3 11.1 %all-to-all-start.5 = ((f32[8,1,128]{2,1,0:T(1,128)}), f32[8,1,128]{2,1,0:T(1,128)S(1)}, u32[]{:S(2)}, u32[]{:S(2)}) async-start(f32[8,1,128]{2,1,0:T(1,128)} %fold.1), calls=%async_computation.5 | async-start | bytes 8192 | tf_op jit(solution)/shard_map/all_to_all | solution.py:525

commit v9 on v7

--- a/solution.py
+++ b/solution.py
@@ -462,9 +462,13 @@
     returned = lax.all_to_all(partials, "page", 0, 0, axis_index_groups=groups, tiled=True)
     projected = call(combine_kernel, "combine", shape((tok_dev, model), BF), [vmem()] * 2)(returned, fetched)
 
+    doc_dev = doc_query.shape[0] // page_size
+    mine_docs = page_rank * doc_dev + jnp.arange(doc_dev, dtype=jnp.int32)
+    counts = jnp.sum((doc_of_token[:, None] == mine_docs[None, :]).astype(F32), axis=0)
     own = tok_dev // head_size
+    own_states = lax.dynamic_slice_in_dim(doc_states, head_rank * own, own, 0)
+    projected, counts, own_states = lax.optimization_barrier((projected, counts, own_states))
     terms = lax.all_to_all(projected.reshape(head_size, own, model), "head", 0, 0, tiled=True)
-    own_states = lax.dynamic_slice_in_dim(doc_states, head_rank * own, own, 0)
     spread, hidden_score = call(
         norm_kernel,
         "norm",
@@ -479,7 +483,6 @@
     token = jnp.arange(tok_dev, dtype=jnp.int32)[:, None]
     own_score = jnp.where(token // own == head_rank, jnp.tile(hidden_score[:, :1], (head_size, 1)), 0.0)
     own_docs = lax.dynamic_slice_in_dim(doc_of_token, page_rank * tok_dev, tok_dev, 0)[:, None]
-    doc_dev = doc_query.shape[0] // page_size
     steps = 4
     doc_sums = call(
         feed_kernel, "feed", shape((page_size, 128), F32), [vmem(), vmem(), hbm(), vmem(), vmem(), vmem()],
@@ -489,8 +492,6 @@
     arrived = lax.all_to_all(doc_sums, "page", 0, 0, tiled=True)
     pooled = call(fold_kernel, "fold", shape((head_size, 1, 128), F32), [vmem()])(arrived)
     pooled = jnp.sum(lax.all_to_all(pooled, "head", 0, 0, tiled=True), axis=(0, 1))[:doc_dev]
-    mine_docs = page_rank * doc_dev + jnp.arange(doc_dev, dtype=jnp.int32)
-    counts = jnp.sum((doc_of_token[:, None] == mine_docs[None, :]).astype(F32), axis=0)
     return pooled / counts
 
 

time: 96.7 us -> 93.4 us (0.966)
  blocking collectives: 0 us -> 40 us
  waiting for transfers between devices: 37.1 us -> 14.1 us
  starting transfers between devices: 35.1 us -> 16.8 us
  Pallas kernels: 20.5 us -> 18.7 us
    all_to_all x0 -> x3, blocking collectives: none -> 40 us  [the longest x1 17.8 us: per_device(): lax.all_to_all(projected.reshape(head_size, own, model), 'head', 0, 0, ti...]
    all_to_all x3 -> x0, waiting for transfers between devices: 22.1 us -> none  [the longest x1 8.69 us: per_device(): lax.all_to_all(projected.reshape(head_size, own, model), 'head', 0, 0, ti...]
    all_to_all x3 -> x0, starting transfers between devices: 18.3 us -> none  [the longest x1 8.57 us: per_device(): lax.all_to_all(projected.reshape(head_size, own, model), 'head', 0, 0, ti...]
  transfers between devices with their start and end apart: 10 -> 7, of which waited for: 7 -> 4; matrix products, arithmetic and copies ran while one was open for 1% -> 1% of each run, Pallas kernels for 9% -> 9%
where the time goes in v9:
time: 93.4 us; the launch traced here: 91.7 us
  blocking collectives  40 us (43%)
  Pallas kernels  18.7 us (20%)
  starting transfers between devices  16.8 us (18%)
  waiting for transfers between devices  14.1 us (15%)
  local copies, waits for them, and re-layouts  1.17 us (1%)
    all_to_all x1, blocking collectives, per_device(): lax.all_to_all(projected.reshape(head_size, own, model), 'head', 0, 0, ti...  17.8 us
    all_to_all x1, blocking collectives, per_device(): arrived = lax.all_to_all(doc_sums, 'page', 0, 0, tiled=True)  12 us
    all_to_all x1, blocking collectives, per_device(): lax.all_to_all(pooled, 'head', 0, 0, tiled=True)  10.2 us
    all_to_all x1, waiting for transfers between devices, per_device(): lax.all_to_all(spread, 'head', 0, 0, tiled=True).reshape(tok_dev, model)  6.54 us
    all_to_all x1, starting transfers between devices, per_device(): lax.all_to_all(spread, 'head', 0, 0, tiled=True).reshape(tok_dev, model)  4.77 us
    all_to_all x1, starting transfers between devices, per_device(): lax.all_to_all(copies, 'page', 0, 0, axis_index_groups=groups, tiled=True)  4.5 us
    pallas_call x1, Pallas kernels, per_device(): call(attention_kernel, 'attention', shape((group, 136, 128), BF), [vmem()...  3.95 us
    ppermute x4, starting transfers between devices, swap(): return lax.ppermute(value, 'page', pairs)  3.78 us
  transfers between devices with their start and end apart: 7, of which 4 were waited for; matrix products, arithmetic and copies ran while one was open for 1% of the time, Pallas kernels for 9%

profile of v9, /device:TPU:32, one launch (start us, length us, event | category | flops | bytes accessed | tf_op | source)
XLA Modules:
  0.0 91.7 jit_solution(13693872713658406399)
XLA Ops:
  0.0 2.4 %project.1 = (bf16[8,64,256]{2,1,0:T(8,128)(2,1)}, bf16[520,256]{1,0:T(8,128)(2,1)S(1)}) custom-call(bf16[64,2048]{1,0:T(8,128)(2,1)} %states.1, f32[1,2048]{1,0:T(1,128)} %bitcast.23, bf16[2048,256]{1,0:T(8,128)(2,1)} %weight.1, bf16[256,256]{1,0:T(8,128)(2,1)} %bitcast.20, bf16[256,256]{1,0:T(8,128)(2,1)} %bitcast.21, s32[2,128]{1,0:T(2,128)} %buckets.1), custom_call_target="tpu_custom_call" | custom-call | tf_op jit(solution)/shard_map/project/pallas_call | solution.py:388
  2.4 0.0 copy-start.2
  2.4 0.0 copy-start
  2.4 3.1 %collective-permute-start.1 = (bf16[520,256]{1,0:T(8,128)(2,1)S(1)}, bf16[520,256]{1,0:T(8,128)(2,1)S(1)}, u32[]{:S(2)}, u32[]{:S(2)}) collective-permute-start(bf16[520,256]{1,0:T(8,128)(2,1)S(1)} %get-tuple-element.25.first), channel_id=1, source_target_pairs={{0,4},{1,5},{2,6},{3,7},{4,0},{5,1},{6,2},{7,3},{8,12},{9,13},{10,... | collective-permute-start | bytes 798728 | tf_op jit(solution)/shard_map/ppermute | solution.py:385
  5.5 0.0 collective-permute-start
  5.5 4.5 %all-to-all-start = ((bf16[8,64,256]{2,1,0:T(8,128)(2,1)}), bf16[8,64,256]{2,1,0:T(8,128)(2,1)S(1)}, u32[]{:S(2)}, u32[]{:S(2)}) async-start(bf16[8,64,256]{2,1,0:T(8,128)(2,1)} %get-tuple-element.24), calls=%async_computation | async-start | bytes 524288 | tf_op jit(solution)/shard_map/all_to_all | solution.py:412
  10.0 2.1 %collective-permute-done.1.first = bf16[520,256]{1,0:T(8,128)(2,1)S(1)} collective-permute-done((bf16[520,256]{1,0:T(8,128)(2,1)S(1)}, bf16[520,256]{1,0:T(8,128)(2,1)S(1)}, u32[]{:S(2)}, u32[]{:S(2)}) %collective-permute-start.1) | collective-permute-done | bytes 266272 | tf_op jit(solution)/shard_map/ppermute | solution.py:385
  12.2 0.1 collective-permute-start.2
  12.3 0.6 collective-permute-start.3
  12.9 0.0 collective-permute-done.second
  12.9 1.9 %near.1 = (bf16[4,512,128]{2,1,0:T(8,128)(2,1)S(1)}, bf16[256,512]{1,0:T(8,128)(2,1)S(1)}, bf16[512,128]{1,0:T(8,128)(2,1)S(1)}) custom-call(s32[1]{0:T(128)} %bitcast.3.rank, bf16[520,256]{1,0:T(8,128)(2,1)S(1)} %get-tuple-element.25.first, bf16[520,256]{1,0:T(8,128)(2,1)S(1)} %collective-permute-done.second, f32[4,32]{1,0:T(4,128)} %bitcast.24, ...), custom_call_target="tpu_custom_call" | custom-call | tf_op jit(solution)/shard_map/near/pallas_call | solution.py:427
  14.8 0.0 collective-permute-done.3.third
  14.8 0.0 collective-permute-done.2.second
  14.8 1.5 %away.1 = (bf16[4,512,128]{2,1,0:T(8,128)(2,1)S(1)}, bf16[256,512]{1,0:T(8,128)(2,1)S(1)}) custom-call(s32[1]{0:T(128)} %bitcast.3.rank, bf16[520,256]{1,0:T(8,128)(2,1)S(1)} %collective-permute-done.1.first, bf16[264,256]{1,0:T(8,128)(2,1)S(1)} %collective-permute-done.2.second, bf16[256,256]{1,0:T(8,128)(2,1)S(1)} %collective-permute-done.3.third, ...), custom_call_target="tpu_custom_call" | custom-call | tf_op jit(solution)/shard_map/away/pallas_call | solution.py:439
  16.3 1.6 %all-to-all-done.queries = bf16[8,64,256]{2,1,0:T(8,128)(2,1)S(1)} async-done(((bf16[8,64,256]{2,1,0:T(8,128)(2,1)}), bf16[8,64,256]{2,1,0:T(8,128)(2,1)S(1)}, u32[]{:S(2)}, u32[]{:S(2)}) %all-to-all-start) | async-done | bytes 262176 | tf_op jit(solution)/shard_map/all_to_all | solution.py:412
  18.0 4.0 %attention.1 = bf16[8,136,128]{2,1,0:T(8,128)(2,1)} custom-call(bf16[8,64,256]{2,1,0:T(8,128)(2,1)S(1)} %all-to-all-done.queries, bf16[4,512,128]{2,1,0:T(8,128)(2,1)S(1)} %get-tuple-element.26.keys_near, bf16[4,512,128]{2,1,0:T(8,128)(2,1)S(1)} %get-tuple-element.27.keys_far, bf16[256,512]{1,0:T(8,128)(2,1)S(1)} %get-tuple-element.28.values_near, ...), custom_call_target="tpu_custom_call" | custom-call | tf_op jit(solution)/shard_map/attention/pallas_call | solution.py:446
  21.9 3.8 %all-to-all-start.1 = ((bf16[8,136,128]{2,1,0:T(8,128)(2,1)}), bf16[8,136,128]{2,1,0:T(8,128)(2,1)S(1)}, u32[]{:S(2)}, u32[]{:S(2)}) async-start(bf16[8,136,128]{2,1,0:T(8,128)(2,1)} %attention.1), calls=%async_computation.1 | async-start | bytes 557056 | tf_op jit(solution)/shard_map/all_to_all | solution.py:462
  25.7 0.0 copy-done.2
  25.7 0.2 convert_reduce_fusion
  25.9 0.8 constant_dynamic-slice_fusion.states
  26.7 0.0 copy-done
  26.7 0.0 copy-start.1
  26.7 2.9 %down.1 = (f32[1,640]{1,0:T(1,128)S(1)}, bf16[256,2048]{1,0:T(8,128)(2,1)S(1)}) custom-call(bf16[640,2048]{1,0:T(8,128)(2,1)} %weight.2, f32[1,2048]{1,0:T(1,128)S(1)} %bitcast.17, bf16[256,2048]{1,0:T(8,128)(2,1)} %out_weight), custom_call_target="tpu_custom_call" | custom-call | tf_op jit(solution)/shard_map/down/pallas_call | solution.py:455
  29.6 3.8 %all-to-all-done.1.parts = bf16[8,136,128]{2,1,0:T(8,128)(2,1)S(1)} async-done(((bf16[8,136,128]{2,1,0:T(8,128)(2,1)}), bf16[8,136,128]{2,1,0:T(8,128)(2,1)S(1)}, u32[]{:S(2)}, u32[]{:S(2)}) %all-to-all-start.1) | async-done | bytes 278560 | tf_op jit(solution)/shard_map/all_to_all | solution.py:462
  33.4 0.4 combine.1
  33.8 17.8 %all_to_all.30.terms = bf16[8,8,2048]{2,1,0:T(8,128)(2,1)S(1)} all-to-all(bf16[8,8,2048]{2,1,0:T(8,128)(2,1)S(1)} %bitcast.14), channel_id=1, replica_groups=mesh['head'=8,'page'=32] {'head'}, dimensions={0} | all-to-all | bytes 524288 | tf_op jit(solution)/shard_map/all_to_all | solution.py:471
  51.6 0.0 copy-done.1
  51.6 0.9 norm.1
  52.4 4.8 %all-to-all-start.3 = ((bf16[8,8,2048]{2,1,0:T(8,128)(2,1)}), bf16[8,8,2048]{2,1,0:T(8,128)(2,1)S(1)}, u32[]{:S(2)}, u32[]{:S(2)}) async-start(bf16[8,8,2048]{2,1,0:T(8,128)(2,1)} %get-tuple-element.38), calls=%async_computation.3 | async-start | bytes 524288 | tf_op jit(solution)/shard_map/all_to_all | solution.py:482
  57.2 0.1 dynamic-slice_bitcast_fusion
  57.3 0.1 copy.23.own_docs
  57.4 0.1 slice_reduce_fusion
  57.5 0.1 tile.14
  57.6 1.8 %fetch.1.gate_weight = bf16[2048,640]{1,0:T(8,128)(2,1)S(1)} custom-call(bf16[2048,640]{1,0:T(8,128)(2,1)} %weight.3), custom_call_target="tpu_custom_call" | custom-call | tf_op jit(solution)/shard_map/fetch/pallas_call | solution.py:479
  59.4 6.5 %all-to-all-done.3 = bf16[8,8,2048]{2,1,0:T(8,128)(2,1)S(1)} async-done(((bf16[8,8,2048]{2,1,0:T(8,128)(2,1)}), bf16[8,8,2048]{2,1,0:T(8,128)(2,1)S(1)}, u32[]{:S(2)}, u32[]{:S(2)}) %all-to-all-start.3) | async-done | bytes 262176 | tf_op jit(solution)/shard_map/all_to_all | solution.py:482
  65.9 2.9 %feed.1 = f32[32,128]{1,0:T(8,128)S(1)} custom-call(bf16[64,2048]{1,0:T(8,128)(2,1)S(1)} %bitcast.15, bf16[2048,640]{1,0:T(8,128)(2,1)S(1)} %fetch.1.gate_weight, bf16[2048,640]{1,0:T(8,128)(2,1)} %up_weight.1, f32[1,640]{1,0:T(1,128)S(1)} %get-tuple-element.40.down_score, f32[64,1]{1,0:T(8,128)S(1)} %fusion.4.own_score, s32[64,1]{1,0:T(8,128)S(1)} %copy.23.own_docs), custom_call_target="tpu_custom_call" | custom-call | tf_op jit(solution)/shard_map/feed/pallas_call | solution.py:487
  68.8 12.0 %all_to_all.31.terms = f32[32,1,128]{2,1,0:T(1,128)S(1)} all-to-all(f32[32,1,128]{2,1,0:T(1,128)S(1)} %bitcast.16), channel_id=1, replica_groups=mesh['head'=8,'page'=32] {'page'}, dimensions={0} | all-to-all | bytes 32768 | tf_op jit(solution)/shard_map/all_to_all | solution.py:492
  80.9 10.2 %all_to_all.32 = f32[8,1,128]{2,1,0:T(1,128)S(1)} all-to-all(f32[8,1,128]{2,1,0:T(1,128)S(1)} %fold.1), channel_id=1, replica_groups=mesh['head'=8,'page'=32] {'head'}, dimensions={0} | all-to-all | bytes 8192 | tf_op jit(solution)/shard_map/all_to_all | solution.py:494
  91.1 0.5 slice_divide_fusion
  (7 shorter events, 0.1 us)
Async XLA Ops:
  2.4 23.3 %copy-start.2 = (s32[2048]{0:T(1024)S(1)}, s32[2048]{0:T(1024)}, u32[]{:S(2)}) copy-start(s32[2048]{0:T(1024)} %param.32) | copy-start | bytes 24580
  2.4 24.3 %copy-start = (f32[2048]{0:T(1024)S(1)}, f32[2048]{0:T(1024)}, u32[]{:S(2)}) copy-start(f32[2048]{0:T(1024)} %param.29) | copy-start | bytes 24580
  2.4 9.7 %collective-permute-start.1 = (bf16[520,256]{1,0:T(8,128)(2,1)S(1)}, bf16[520,256]{1,0:T(8,128)(2,1)S(1)}, u32[]{:S(2)}, u32[]{:S(2)}) collective-permute-start(bf16[520,256]{1,0:T(8,128)(2,1)S(1)} %get-tuple-element.25.first), channel_id=1, source_target_pairs={{0,4},{1,5},{2,6},{3,7},{4,0},{5,1},{6,2},{7,3},{8,12},{9,13},{10,... | collective-permute-start | bytes 798728 | tf_op jit(solution)/shard_map/ppermute | solution.py:385
  5.5 7.3 %collective-permute-start = (bf16[520,256]{1,0:T(8,128)(2,1)S(1)}, bf16[520,256]{1,0:T(8,128)(2,1)S(1)}, u32[]{:S(2)}, u32[]{:S(2)}) collective-permute-start(bf16[520,256]{1,0:T(8,128)(2,1)S(1)} %get-tuple-element.25.first), channel_id=1, source_target_pairs={{0,1},{1,0},{2,3},{3,2},{4,5},{5,4},{6,7},{7,6},{8,9},{9,8},{10,11... | collective-permute-start | bytes 798728 | tf_op jit(solution)/shard_map/ppermute | solution.py:385
  5.5 12.4 %all-to-all-start = ((bf16[8,64,256]{2,1,0:T(8,128)(2,1)}), bf16[8,64,256]{2,1,0:T(8,128)(2,1)S(1)}, u32[]{:S(2)}, u32[]{:S(2)}) async-start(bf16[8,64,256]{2,1,0:T(8,128)(2,1)} %get-tuple-element.24), calls=%async_computation | async-start | bytes 524288 | tf_op jit(solution)/shard_map/all_to_all | solution.py:412
  12.2 2.6 %collective-permute-start.2 = (bf16[264,256]{1,0:T(8,128)(2,1)S(1)}, bf16[264,256]{1,0:T(8,128)(2,1)S(1)}, u32[]{:S(2)}, u32[]{:S(2)}) collective-permute-start(bf16[264,256]{1,0:T(8,128)(2,1)S(1)} %slice.16), channel_id=1, source_target_pairs={{0,1},{1,0},{2,3},{3,2},{4,5},{5,4},{6,7},{7,6},{8,9},{9,8},{10,11... | collective-permute-start | bytes 405512 | tf_op jit(solution)/shard_map/ppermute | solution.py:385
  12.3 2.5 %collective-permute-start.3 = (bf16[256,256]{1,0:T(8,128)(2,1)S(1)}, bf16[256,256]{1,0:T(8,128)(2,1)S(1)}, u32[]{:S(2)}, u32[]{:S(2)}) collective-permute-start(bf16[256,256]{1,0:T(8,128)(2,1)S(1)} %slice.17), channel_id=1, source_target_pairs={{0,1},{1,0},{2,3},{3,2},{4,5},{5,4},{6,7},{7,6},{8,9},{9,8},{10,11... | collective-permute-start | bytes 393224 | tf_op jit(solution)/shard_map/ppermute | solution.py:385
  21.9 11.4 %all-to-all-start.1 = ((bf16[8,136,128]{2,1,0:T(8,128)(2,1)}), bf16[8,136,128]{2,1,0:T(8,128)(2,1)S(1)}, u32[]{:S(2)}, u32[]{:S(2)}) async-start(bf16[8,136,128]{2,1,0:T(8,128)(2,1)} %attention.1), calls=%async_computation.1 | async-start | bytes 557056 | tf_op jit(solution)/shard_map/all_to_all | solution.py:462
  26.7 24.9 %copy-start.1 = (f32[2048]{0:T(1024)S(1)}, f32[2048]{0:T(1024)}, u32[]{:S(2)}) copy-start(f32[2048]{0:T(1024)} %param.25) | copy-start | bytes 24580
  52.4 13.5 %all-to-all-start.3 = ((bf16[8,8,2048]{2,1,0:T(8,128)(2,1)}), bf16[8,8,2048]{2,1,0:T(8,128)(2,1)S(1)}, u32[]{:S(2)}, u32[]{:S(2)}) async-start(bf16[8,8,2048]{2,1,0:T(8,128)(2,1)} %get-tuple-element.38), calls=%async_computation.3 | async-start | bytes 524288 | tf_op jit(solution)/shard_map/all_to_all | solution.py:482

commit v10 on v9

--- a/solution.py
+++ b/solution.py
@@ -173,7 +173,15 @@
                 keys_aug[h, span, :] = jnp.where(keep, half, bias[:, h * 128 : (h + 1) * 128] + marks).astype(BF)
 
 
-def attention_kernel(queries, keys_near, keys_far, values_near, values_far, extra, out, rows_aug):
+def attention_kernel(rank, queries, keys_near, keys_far, values_near, values_far, extra, states, out_weight, out, own, fetched,
+                     rows_aug, arrivals):
+    start = pl.multiple_of(rank[0] * own.shape[0], own.shape[0])
+    copies = [
+        pltpu.make_async_copy(out_weight, fetched, arrivals.at[0]),
+        pltpu.make_async_copy(states.at[pl.ds(start, own.shape[0])], own, arrivals.at[1]),
+    ]
+    for copy in copies:
+        copy.start()
     chips, tok_dev, width = queries.shape
     heads = keys_near.shape[0]
     depth = width // heads
@@ -230,6 +238,8 @@
             packed = [a[0:2].astype(F32), b[0:2].astype(F32), c[0:2].astype(F32), jnp.zeros((2, 128), F32)]
             out[duo * 2 + which, 0:128, :] = block[which].astype(BF)
             out[duo * 2 + which, 128:136, :] = jnp.concatenate(packed, axis=0).astype(BF)
+    for copy in copies:
+        copy.wait()
 
 
 def combine_kernel(parts, out_weight, out):
@@ -265,23 +275,17 @@
     score[...] = jnp.broadcast_to(jnp.sum(hidden * score_vector[...], axis=-1, keepdims=True), score.shape)
 
 
-def down_kernel(weight, score_vector, out_weight, out, fetched, weight_here, arrivals):
+def down_kernel(weight, score_vector, gate_weight, out, fetched, weight_here, arrivals):
     copy = pltpu.make_async_copy(weight, weight_here, arrivals.at[0])
-    fetch = pltpu.make_async_copy(out_weight, fetched, arrivals.at[1])
+    fetch = pltpu.make_async_copy(gate_weight, fetched, arrivals.at[1])
+    copy.start()
     fetch.start()
-    copy.start()
     pieces = [piece.astype(F32) for piece in split_three(score_vector[...])]
     rows = jnp.concatenate(pieces + [jnp.zeros((5, score_vector.shape[1]), F32)], axis=0).astype(BF)
     copy.wait()
     terms = lax.dot_general(rows, weight_here[...], (((1,), (1,)), ((), ())), preferred_element_type=F32)
     out[...] = terms[0:1] + terms[1:2] + terms[2:3]
     fetch.wait()
-
-
-def fetch_kernel(weight, out, arrival):
-    copy = pltpu.make_async_copy(weight, out, arrival)
-    copy.start()
-    copy.wait()
 
 
 def feed_kernel(rows, gate_weight, up_weight, down_score, own_score, own_docs, out, up_here, arrivals):
@@ -443,31 +447,22 @@
         [smem()] + [vmem()] * 3 + [hbm()] * 3,
         scratch,
     )(rank, payload_side, keys_far, values_far, *tables)
-    partials = call(
+    own = tok_dev // head_size
+    partials, own_states, fetched = call(
         attention_kernel,
         "attention",
-        shape((group, 136, 128), BF),
-        [vmem()] * 6,
-        [pltpu.VMEM((local_heads, group * tok_dev, 128), BF)],
-    )(gathered, keys_near, keys_away, values_near, values_away, extra)
-    partials, down_weight, late_weight = lax.optimization_barrier((partials, wo_ffn, out_weight))
+        [shape((group, 136, 128), BF), shape((own, model), BF), shape(out_weight.shape, BF)],
+        [smem()] + [vmem()] * 6 + [hbm()] * 2,
+        [pltpu.VMEM((local_heads, group * tok_dev, 128), BF), pltpu.SemaphoreType.DMA((2,))],
+    )(
+        head_rank.reshape(1), gathered, keys_near, keys_away, values_near, values_away, extra,
+        in_hbm(doc_states), in_hbm(out_weight),
+    )
     hidden_units = wi_gate.shape[1]
-    down_score, fetched = call(
-        down_kernel,
-        "down",
-        [shape((1, hidden_units), F32), shape(out_weight.shape, BF)],
-        [hbm(), vmem(), hbm()],
-        [pltpu.VMEM(wo_ffn.shape, BF), pltpu.SemaphoreType.DMA((2,))],
-    )(in_hbm(down_weight), score_vector.reshape(1, model), in_hbm(late_weight))
     returned = lax.all_to_all(partials, "page", 0, 0, axis_index_groups=groups, tiled=True)
     projected = call(combine_kernel, "combine", shape((tok_dev, model), BF), [vmem()] * 2)(returned, fetched)
 
     doc_dev = doc_query.shape[0] // page_size
-    mine_docs = page_rank * doc_dev + jnp.arange(doc_dev, dtype=jnp.int32)
-    counts = jnp.sum((doc_of_token[:, None] == mine_docs[None, :]).astype(F32), axis=0)
-    own = tok_dev // head_size
-    own_states = lax.dynamic_slice_in_dim(doc_states, head_rank * own, own, 0)
-    projected, counts, own_states = lax.optimization_barrier((projected, counts, own_states))
     terms = lax.all_to_all(projected.reshape(head_size, own, model), "head", 0, 0, tiled=True)
     spread, hidden_score = call(
         norm_kernel,
@@ -475,14 +470,23 @@
         [shape((head_size, own, model), BF), shape((own, 128), F32)],
         [vmem()] * 4,
     )(terms, own_states, gain_ffn.reshape(1, model), score_vector.reshape(1, model))
-    spread, late_gate = lax.optimization_barrier((spread, wi_gate))
-    gate_here = call(
-        fetch_kernel, "fetch", shape(wi_gate.shape, BF), [hbm()], [pltpu.SemaphoreType.DMA(())]
-    )(in_hbm(late_gate))
+    spread, late_gate, down_weight, late_docs, late_rank = lax.optimization_barrier(
+        (spread, wi_gate, wo_ffn, doc_of_token, page_rank)
+    )
+    down_score, gate_here = call(
+        down_kernel,
+        "down",
+        [shape((1, hidden_units), F32), shape(wi_gate.shape, BF)],
+        [hbm(), vmem(), hbm()],
+        [pltpu.VMEM(wo_ffn.shape, BF), pltpu.SemaphoreType.DMA((2,))],
+    )(in_hbm(down_weight), score_vector.reshape(1, model), in_hbm(late_gate))
+    mine_docs = late_rank * doc_dev + jnp.arange(doc_dev, dtype=jnp.int32)
+    counts = jnp.sum((late_docs[:, None] == mine_docs[None, :]).astype(F32), axis=0)
     rows = lax.all_to_all(spread, "head", 0, 0, tiled=True).reshape(tok_dev, model)
+    rows, counts = lax.optimization_barrier((rows, counts))
     token = jnp.arange(tok_dev, dtype=jnp.int32)[:, None]
     own_score = jnp.where(token // own == head_rank, jnp.tile(hidden_score[:, :1], (head_size, 1)), 0.0)
-    own_docs = lax.dynamic_slice_in_dim(doc_of_token, page_rank * tok_dev, tok_dev, 0)[:, None]
+    own_docs = lax.dynamic_slice_in_dim(late_docs, page_rank * tok_dev, tok_dev, 0)[:, None]
     steps = 4
     doc_sums = call(
         feed_kernel, "feed", shape((page_size, 128), F32), [vmem(), vmem(), hbm(), vmem(), vmem(), vmem()],

time: 93.4 us -> 94.5 us (1.012)
  blocking collectives: 40 us -> 34.2 us
  starting transfers between devices: 16.8 us -> 21.6 us
  waiting for transfers between devices: 14.1 us -> 18.6 us
  Pallas kernels: 18.7 us -> 17.1 us
    all_to_all x1, blocking collectives: 17.8 us -> 11.5 us  [per_device(): lax.all_to_all(partials, 'page', 0, 0, axis_index_groups=groups, tiled=True)]
    all_to_all x1, waiting for transfers between devices: 3.78 us -> 9.2 us  [per_device(): lax.all_to_all(projected.reshape(head_size, own, model), 'head', 0, 0, ti...]
    all_to_all x1, starting transfers between devices: 3.77 us -> 8.57 us  [per_device(): lax.all_to_all(projected.reshape(head_size, own, model), 'head', 0, 0, ti...]
    pallas_call x3 -> x2, Pallas kernels: 8.6 us -> 6.28 us  [the longest x1 3.72 us: per_device(): call(attention_kernel, 'attention', [shape((group, 136, 128), BF), shape(...]
  transfers between devices with their start and end apart: 7 -> 7, of which waited for: 4 -> 4; matrix products, arithmetic and copies ran while one was open for 1% -> 1% of each run, Pallas kernels for 9% -> 6%
where the time goes in v10:
time: 94.5 us; the launch traced here: 92.8 us
  blocking collectives  34.2 us (36%)
  starting transfers between devices  21.6 us (23%)
  waiting for transfers between devices  18.6 us (20%)
  Pallas kernels  17.1 us (18%)
    all_to_all x1, blocking collectives, per_device(): arrived = lax.all_to_all(doc_sums, 'page', 0, 0, tiled=True)  12.3 us
    all_to_all x1, blocking collectives, per_device(): lax.all_to_all(partials, 'page', 0, 0, axis_index_groups=groups, tiled=True)  11.5 us
    all_to_all x1, blocking collectives, per_device(): lax.all_to_all(pooled, 'head', 0, 0, tiled=True)  10.4 us
    all_to_all x1, waiting for transfers between devices, per_device(): lax.all_to_all(projected.reshape(head_size, own, model), 'head', 0, 0, ti...  9.2 us
    all_to_all x1, starting transfers between devices, per_device(): lax.all_to_all(projected.reshape(head_size, own, model), 'head', 0, 0, ti...  8.57 us
    all_to_all x1, waiting for transfers between devices, per_device(): lax.all_to_all(spread, 'head', 0, 0, tiled=True).reshape(tok_dev, model)  5.66 us
    all_to_all x1, starting transfers between devices, per_device(): lax.all_to_all(spread, 'head', 0, 0, tiled=True).reshape(tok_dev, model)  4.78 us
    all_to_all x1, starting transfers between devices, per_device(): lax.all_to_all(copies, 'page', 0, 0, axis_index_groups=groups, tiled=True)  4.5 us
  transfers between devices with their start and end apart: 7, of which 4 were waited for; matrix products, arithmetic and copies ran while one was open for 1% of the time, Pallas kernels for 6%

profile of v10, /device:TPU:32, one launch (start us, length us, event | category | flops | bytes accessed | tf_op | source)
XLA Modules:
  0.0 92.8 jit_solution(10471519179284761454)
XLA Ops:
  0.0 2.4 %project.1 = (bf16[8,64,256]{2,1,0:T(8,128)(2,1)}, bf16[520,256]{1,0:T(8,128)(2,1)S(1)}) custom-call(bf16[64,2048]{1,0:T(8,128)(2,1)} %states.3, f32[1,2048]{1,0:T(1,128)} %bitcast.23, bf16[2048,256]{1,0:T(8,128)(2,1)} %weight.1, bf16[256,256]{1,0:T(8,128)(2,1)} %bitcast.20, bf16[256,256]{1,0:T(8,128)(2,1)} %bitcast.21, s32[2,128]{1,0:T(2,128)} %buckets.1), custom_call_target="tpu_custom_call" | custom-call | tf_op jit(solution)/shard_map/project/pallas_call | solution.py:392
  2.4 3.1 %collective-permute-start.1 = (bf16[520,256]{1,0:T(8,128)(2,1)S(1)}, bf16[520,256]{1,0:T(8,128)(2,1)S(1)}, u32[]{:S(2)}, u32[]{:S(2)}) collective-permute-start(bf16[520,256]{1,0:T(8,128)(2,1)S(1)} %get-tuple-element.27.first), channel_id=1, source_target_pairs={{0,4},{1,5},{2,6},{3,7},{4,0},{5,1},{6,2},{7,3},{8,12},{9,13},{10,... | collective-permute-start | bytes 798728 | tf_op jit(solution)/shard_map/ppermute | solution.py:389
  5.5 0.0 collective-permute-start
  5.5 4.5 %all-to-all-start = ((bf16[8,64,256]{2,1,0:T(8,128)(2,1)}), bf16[8,64,256]{2,1,0:T(8,128)(2,1)S(1)}, u32[]{:S(2)}, u32[]{:S(2)}) async-start(bf16[8,64,256]{2,1,0:T(8,128)(2,1)} %get-tuple-element.26), calls=%async_computation | async-start | bytes 524288 | tf_op jit(solution)/shard_map/all_to_all | solution.py:416
  10.0 2.1 %collective-permute-done.1.first = bf16[520,256]{1,0:T(8,128)(2,1)S(1)} collective-permute-done((bf16[520,256]{1,0:T(8,128)(2,1)S(1)}, bf16[520,256]{1,0:T(8,128)(2,1)S(1)}, u32[]{:S(2)}, u32[]{:S(2)}) %collective-permute-start.1) | collective-permute-done | bytes 266272 | tf_op jit(solution)/shard_map/ppermute | solution.py:389
  12.1 0.1 collective-permute-start.2
  12.3 0.6 collective-permute-start.3
  12.8 0.0 collective-permute-done.second
  12.8 1.9 %near.1 = (bf16[4,512,128]{2,1,0:T(8,128)(2,1)S(1)}, bf16[256,512]{1,0:T(8,128)(2,1)S(1)}, bf16[512,128]{1,0:T(8,128)(2,1)S(1)}) custom-call(s32[1]{0:T(128)} %bitcast.4.rank, bf16[520,256]{1,0:T(8,128)(2,1)S(1)} %get-tuple-element.27.first, bf16[520,256]{1,0:T(8,128)(2,1)S(1)} %collective-permute-done.second, f32[4,32]{1,0:T(4,128)} %bitcast.24, ...), custom_call_target="tpu_custom_call" | custom-call | tf_op jit(solution)/shard_map/near/pallas_call | solution.py:431
  14.8 0.0 collective-permute-done.3.third
  14.8 0.0 collective-permute-done.2.second
  14.8 1.5 %away.1 = (bf16[4,512,128]{2,1,0:T(8,128)(2,1)S(1)}, bf16[256,512]{1,0:T(8,128)(2,1)S(1)}) custom-call(s32[1]{0:T(128)} %bitcast.4.rank, bf16[520,256]{1,0:T(8,128)(2,1)S(1)} %collective-permute-done.1.first, bf16[264,256]{1,0:T(8,128)(2,1)S(1)} %collective-permute-done.2.second, bf16[256,256]{1,0:T(8,128)(2,1)S(1)} %collective-permute-done.3.third, ...), custom_call_target="tpu_custom_call" | custom-call | tf_op jit(solution)/shard_map/away/pallas_call | solution.py:443
  16.3 1.6 %all-to-all-done.queries = bf16[8,64,256]{2,1,0:T(8,128)(2,1)S(1)} async-done(((bf16[8,64,256]{2,1,0:T(8,128)(2,1)}), bf16[8,64,256]{2,1,0:T(8,128)(2,1)S(1)}, u32[]{:S(2)}, u32[]{:S(2)}) %all-to-all-start) | async-done | bytes 262176 | tf_op jit(solution)/shard_map/all_to_all | solution.py:416
  18.0 0.0 copy-start
  18.0 0.0 copy-start.1
  18.0 0.0 copy-start.2
  18.0 3.7 %attention.1 = (bf16[8,136,128]{2,1,0:T(8,128)(2,1)S(1)}, bf16[8,2048]{1,0:T(8,128)(2,1)S(1)}, bf16[256,2048]{1,0:T(8,128)(2,1)S(1)}) custom-call(s32[1]{0:T(128)} %bitcast.rank, bf16[8,64,256]{2,1,0:T(8,128)(2,1)S(1)} %all-to-all-done.queries, bf16[4,512,128]{2,1,0:T(8,128)(2,1)S(1)} %get-tuple-element.28.keys_near, ...), custom_call_target="tpu_custom_call" | custom-call | tf_op jit(solution)/shard_map/attention/pallas_call | solution.py:451
  21.7 11.5 %all_to_all.30.parts = bf16[8,136,128]{2,1,0:T(8,128)(2,1)S(1)} all-to-all(bf16[8,136,128]{2,1,0:T(8,128)(2,1)S(1)} %get-tuple-element.33), channel_id=1, replica_groups={{0,2,8,10,16,18,24,26},{1,3,9,11,17,19,25,27},{4,6,12,14,20,22,28,30},{..., dimensions={0} | all-to-all | bytes 557056 | tf_op jit(solution)/shard_map/all_to_all | solution.py:462
  33.2 1.1 %combine.1 = bf16[64,2048]{1,0:T(8,128)(2,1)} custom-call(bf16[8,136,128]{2,1,0:T(8,128)(2,1)S(1)} %all_to_all.30.parts, bf16[256,2048]{1,0:T(8,128)(2,1)S(1)} %get-tuple-element.34.out_weight), custom_call_target="tpu_custom_call" | custom-call | tf_op jit(solution)/shard_map/combine/pallas_call | solution.py:463
  34.3 8.6 %all-to-all-start.2 = ((bf16[8,8,2048]{2,1,0:T(8,128)(2,1)}), bf16[8,8,2048]{2,1,0:T(8,128)(2,1)S(1)}, u32[]{:S(2)}, u32[]{:S(2)}) async-start(bf16[8,8,2048]{2,1,0:T(8,128)(2,1)} %bitcast.8), calls=%async_computation.2 | async-start | bytes 524288 | tf_op jit(solution)/shard_map/all_to_all | solution.py:466
  42.9 9.2 %all-to-all-done.2.terms = bf16[8,8,2048]{2,1,0:T(8,128)(2,1)S(1)} async-done(((bf16[8,8,2048]{2,1,0:T(8,128)(2,1)}), bf16[8,8,2048]{2,1,0:T(8,128)(2,1)S(1)}, u32[]{:S(2)}, u32[]{:S(2)}) %all-to-all-start.2) | async-done | bytes 262176 | tf_op jit(solution)/shard_map/all_to_all | solution.py:466
  52.1 0.0 copy-done
  52.1 0.0 copy-done.1
  52.1 0.9 norm.1
  53.0 0.1 slice_reduce_fusion
  53.1 4.8 %all-to-all-start.3 = ((bf16[8,8,2048]{2,1,0:T(8,128)(2,1)}), bf16[8,8,2048]{2,1,0:T(8,128)(2,1)S(1)}, u32[]{:S(2)}, u32[]{:S(2)}) async-start(bf16[8,8,2048]{2,1,0:T(8,128)(2,1)} %get-tuple-element.37), calls=%async_computation.3 | async-start | bytes 524288 | tf_op jit(solution)/shard_map/all_to_all | solution.py:485
  57.9 0.0 copy-done.2
  57.9 0.1 dynamic-slice_bitcast_fusion
  57.9 0.1 tile.14
  58.0 0.1 copy.23.own_docs
  58.1 2.6 %down.1 = (f32[1,640]{1,0:T(1,128)S(1)}, bf16[2048,640]{1,0:T(8,128)(2,1)S(1)}) custom-call(bf16[640,2048]{1,0:T(8,128)(2,1)} %weight.2, f32[1,2048]{1,0:T(1,128)S(1)} %bitcast.18, bf16[2048,640]{1,0:T(8,128)(2,1)} %gate_weight), custom_call_target="tpu_custom_call" | custom-call | tf_op jit(solution)/shard_map/down/pallas_call | solution.py:476
  60.7 0.2 convert_reduce_fusion
  60.9 5.7 %all-to-all-done.3 = bf16[8,8,2048]{2,1,0:T(8,128)(2,1)S(1)} async-done(((bf16[8,8,2048]{2,1,0:T(8,128)(2,1)}), bf16[8,8,2048]{2,1,0:T(8,128)(2,1)S(1)}, u32[]{:S(2)}, u32[]{:S(2)}) %all-to-all-start.3) | async-done | bytes 262176 | tf_op jit(solution)/shard_map/all_to_all | solution.py:485
  66.6 2.9 %feed.1 = f32[32,128]{1,0:T(8,128)S(1)} custom-call(bf16[64,2048]{1,0:T(8,128)(2,1)S(1)} %bitcast.15, bf16[2048,640]{1,0:T(8,128)(2,1)S(1)} %get-tuple-element.43.gate_weight, bf16[2048,640]{1,0:T(8,128)(2,1)} %up_weight.1, f32[1,640]{1,0:T(1,128)S(1)} %get-tuple-element.44.down_score, f32[64,1]{1,0:T(8,128)S(1)} %fusion.4.own_score, s32[64,1]{1,0:T(8,128)S(1)} %copy.23.own_docs), custom_call_target="tpu_custom_call" | custom-call | tf_op jit(solution)/shard_map/feed/pallas_call | solution.py:491
  69.5 12.3 %all_to_all.31.terms = f32[32,1,128]{2,1,0:T(1,128)S(1)} all-to-all(f32[32,1,128]{2,1,0:T(1,128)S(1)} %bitcast.16), channel_id=1, replica_groups=mesh['head'=8,'page'=32] {'page'}, dimensions={0} | all-to-all | bytes 32768 | tf_op jit(solution)/shard_map/all_to_all | solution.py:496
  81.9 10.4 %all_to_all.32 = f32[8,1,128]{2,1,0:T(1,128)S(1)} all-to-all(f32[8,1,128]{2,1,0:T(1,128)S(1)} %fold.1), channel_id=1, replica_groups=mesh['head'=8,'page'=32] {'head'}, dimensions={0} | all-to-all | bytes 8192 | tf_op jit(solution)/shard_map/all_to_all | solution.py:498
  92.3 0.5 slice_divide_fusion
  (7 shorter events, 0.1 us)
Async XLA Ops:
  2.4 9.7 %collective-permute-start.1 = (bf16[520,256]{1,0:T(8,128)(2,1)S(1)}, bf16[520,256]{1,0:T(8,128)(2,1)S(1)}, u32[]{:S(2)}, u32[]{:S(2)}) collective-permute-start(bf16[520,256]{1,0:T(8,128)(2,1)S(1)} %get-tuple-element.27.first), channel_id=1, source_target_pairs={{0,4},{1,5},{2,6},{3,7},{4,0},{5,1},{6,2},{7,3},{8,12},{9,13},{10,... | collective-permute-start | bytes 798728 | tf_op jit(solution)/shard_map/ppermute | solution.py:389
  5.5 7.3 %collective-permute-start = (bf16[520,256]{1,0:T(8,128)(2,1)S(1)}, bf16[520,256]{1,0:T(8,128)(2,1)S(1)}, u32[]{:S(2)}, u32[]{:S(2)}) collective-permute-start(bf16[520,256]{1,0:T(8,128)(2,1)S(1)} %get-tuple-element.27.first), channel_id=1, source_target_pairs={{0,1},{1,0},{2,3},{3,2},{4,5},{5,4},{6,7},{7,6},{8,9},{9,8},{10,11... | collective-permute-start | bytes 798728 | tf_op jit(solution)/shard_map/ppermute | solution.py:389
  5.5 12.4 %all-to-all-start = ((bf16[8,64,256]{2,1,0:T(8,128)(2,1)}), bf16[8,64,256]{2,1,0:T(8,128)(2,1)S(1)}, u32[]{:S(2)}, u32[]{:S(2)}) async-start(bf16[8,64,256]{2,1,0:T(8,128)(2,1)} %get-tuple-element.26), calls=%async_computation | async-start | bytes 524288 | tf_op jit(solution)/shard_map/all_to_all | solution.py:416
  12.1 2.6 %collective-permute-start.2 = (bf16[264,256]{1,0:T(8,128)(2,1)S(1)}, bf16[264,256]{1,0:T(8,128)(2,1)S(1)}, u32[]{:S(2)}, u32[]{:S(2)}) collective-permute-start(bf16[264,256]{1,0:T(8,128)(2,1)S(1)} %slice.16), channel_id=1, source_target_pairs={{0,1},{1,0},{2,3},{3,2},{4,5},{5,4},{6,7},{7,6},{8,9},{9,8},{10,11... | collective-permute-start | bytes 405512 | tf_op jit(solution)/shard_map/ppermute | solution.py:389
  12.3 2.5 %collective-permute-start.3 = (bf16[256,256]{1,0:T(8,128)(2,1)S(1)}, bf16[256,256]{1,0:T(8,128)(2,1)S(1)}, u32[]{:S(2)}, u32[]{:S(2)}) collective-permute-start(bf16[256,256]{1,0:T(8,128)(2,1)S(1)} %slice.17), channel_id=1, source_target_pairs={{0,1},{1,0},{2,3},{3,2},{4,5},{5,4},{6,7},{7,6},{8,9},{9,8},{10,11... | collective-permute-start | bytes 393224 | tf_op jit(solution)/shard_map/ppermute | solution.py:389
  18.0 34.1 %copy-start = (f32[2048]{0:T(1024)S(1)}, f32[2048]{0:T(1024)}, u32[]{:S(2)}) copy-start(f32[2048]{0:T(1024)} %param.29) | copy-start | bytes 24580
  18.0 34.1 %copy-start.1 = (f32[2048]{0:T(1024)S(1)}, f32[2048]{0:T(1024)}, u32[]{:S(2)}) copy-start(f32[2048]{0:T(1024)} %param.25) | copy-start | bytes 24580
  18.0 39.9 %copy-start.2 = (s32[2048]{0:T(1024)S(1)}, s32[2048]{0:T(1024)}, u32[]{:S(2)}) copy-start(s32[2048]{0:T(1024)} %param.32) | copy-start | bytes 24580
  34.3 17.8 %all-to-all-start.2 = ((bf16[8,8,2048]{2,1,0:T(8,128)(2,1)}), bf16[8,8,2048]{2,1,0:T(8,128)(2,1)S(1)}, u32[]{:S(2)}, u32[]{:S(2)}) async-start(bf16[8,8,2048]{2,1,0:T(8,128)(2,1)} %bitcast.8), calls=%async_computation.2 | async-start | bytes 524288 | tf_op jit(solution)/shard_map/all_to_all | solution.py:466
  53.1 13.5 %all-to-all-start.3 = ((bf16[8,8,2048]{2,1,0:T(8,128)(2,1)}), bf16[8,8,2048]{2,1,0:T(8,128)(2,1)S(1)}, u32[]{:S(2)}, u32[]{:S(2)}) async-start(bf16[8,8,2048]{2,1,0:T(8,128)(2,1)} %get-tuple-element.37), calls=%async_computation.3 | async-start | bytes 524288 | tf_op jit(solution)/shard_map/all_to_all | solution.py:485

commit v11 on v10

--- a/solution.py
+++ b/solution.py
@@ -486,7 +486,7 @@
     rows, counts = lax.optimization_barrier((rows, counts))
     token = jnp.arange(tok_dev, dtype=jnp.int32)[:, None]
     own_score = jnp.where(token // own == head_rank, jnp.tile(hidden_score[:, :1], (head_size, 1)), 0.0)
-    own_docs = lax.dynamic_slice_in_dim(late_docs, page_rank * tok_dev, tok_dev, 0)[:, None]
+    own_docs = lax.dynamic_slice_in_dim(late_docs, late_rank * tok_dev, tok_dev, 0)[:, None]
     steps = 4
     doc_sums = call(
         feed_kernel, "feed", shape((page_size, 128), F32), [vmem(), vmem(), hbm(), vmem(), vmem(), vmem()],

time: 94.5 us -> 93.5 us (0.989)
  blocking collectives: 34.2 us -> 51.8 us
  waiting for transfers between devices: 18.6 us -> 9.4 us
  starting transfers between devices: 21.6 us -> 13.1 us
    all_to_all x0 -> x1, blocking collectives: none -> 17.6 us  [per_device(): lax.all_to_all(projected.reshape(head_size, own, model), 'head', 0, 0, ti...]
    all_to_all x1 -> x0, waiting for transfers between devices: 9.2 us -> none  [per_device(): lax.all_to_all(projected.reshape(head_size, own, model), 'head', 0, 0, ti...]
    all_to_all x1 -> x0, starting transfers between devices: 8.57 us -> none  [per_device(): lax.all_to_all(projected.reshape(head_size, own, model), 'head', 0, 0, ti...]
  transfers between devices with their start and end apart: 7 -> 6, of which waited for: 4 -> 3; matrix products, arithmetic and copies ran while one was open for 1% -> 1% of each run, Pallas kernels for 6% -> 7%
where the time goes in v11:
time: 93.5 us; the launch traced here: 91.8 us
  blocking collectives  51.8 us (55%)
  Pallas kernels  16.3 us (17%)
  starting transfers between devices  13.1 us (14%)
  waiting for transfers between devices  9.4 us (10%)
    all_to_all x1, blocking collectives, per_device(): lax.all_to_all(projected.reshape(head_size, own, model), 'head', 0, 0, ti...  17.6 us
    all_to_all x1, blocking collectives, per_device(): arrived = lax.all_to_all(doc_sums, 'page', 0, 0, tiled=True)  12.3 us
    all_to_all x1, blocking collectives, per_device(): lax.all_to_all(partials, 'page', 0, 0, axis_index_groups=groups, tiled=True)  11.5 us
    all_to_all x1, blocking collectives, per_device(): lax.all_to_all(pooled, 'head', 0, 0, tiled=True)  10.4 us
    all_to_all x1, waiting for transfers between devices, per_device(): lax.all_to_all(spread, 'head', 0, 0, tiled=True).reshape(tok_dev, model)  5.64 us
    all_to_all x1, starting transfers between devices, per_device(): lax.all_to_all(spread, 'head', 0, 0, tiled=True).reshape(tok_dev, model)  4.78 us
    all_to_all x1, starting transfers between devices, per_device(): lax.all_to_all(copies, 'page', 0, 0, axis_index_groups=groups, tiled=True)  4.5 us
    ppermute x4, starting transfers between devices, swap(): return lax.ppermute(value, 'page', pairs)  3.78 us
  transfers between devices with their start and end apart: 6, of which 3 were waited for; matrix products, arithmetic and copies ran while one was open for 1% of the time, Pallas kernels for 7%

profile of v11, /device:TPU:32, one launch (start us, length us, event | category | flops | bytes accessed | tf_op | source)
XLA Modules:
  0.0 91.8 jit_solution(12841467752683281397)
XLA Ops:
  0.0 2.4 %project.1 = (bf16[8,64,256]{2,1,0:T(8,128)(2,1)}, bf16[520,256]{1,0:T(8,128)(2,1)S(1)}) custom-call(bf16[64,2048]{1,0:T(8,128)(2,1)} %states.3, f32[1,2048]{1,0:T(1,128)} %bitcast.24, bf16[2048,256]{1,0:T(8,128)(2,1)} %weight.1, bf16[256,256]{1,0:T(8,128)(2,1)} %bitcast.21, bf16[256,256]{1,0:T(8,128)(2,1)} %bitcast.22, s32[2,128]{1,0:T(2,128)} %buckets.1), custom_call_target="tpu_custom_call" | custom-call | tf_op jit(solution)/shard_map/project/pallas_call | solution.py:392
  2.4 3.1 %collective-permute-start.1 = (bf16[520,256]{1,0:T(8,128)(2,1)S(1)}, bf16[520,256]{1,0:T(8,128)(2,1)S(1)}, u32[]{:S(2)}, u32[]{:S(2)}) collective-permute-start(bf16[520,256]{1,0:T(8,128)(2,1)S(1)} %get-tuple-element.27.first), channel_id=1, source_target_pairs={{0,4},{1,5},{2,6},{3,7},{4,0},{5,1},{6,2},{7,3},{8,12},{9,13},{10,... | collective-permute-start | bytes 798728 | tf_op jit(solution)/shard_map/ppermute | solution.py:389
  5.5 0.0 collective-permute-start
  5.5 4.5 %all-to-all-start = ((bf16[8,64,256]{2,1,0:T(8,128)(2,1)}), bf16[8,64,256]{2,1,0:T(8,128)(2,1)S(1)}, u32[]{:S(2)}, u32[]{:S(2)}) async-start(bf16[8,64,256]{2,1,0:T(8,128)(2,1)} %get-tuple-element.26), calls=%async_computation | async-start | bytes 524288 | tf_op jit(solution)/shard_map/all_to_all | solution.py:416
  10.0 2.1 %collective-permute-done.1.first = bf16[520,256]{1,0:T(8,128)(2,1)S(1)} collective-permute-done((bf16[520,256]{1,0:T(8,128)(2,1)S(1)}, bf16[520,256]{1,0:T(8,128)(2,1)S(1)}, u32[]{:S(2)}, u32[]{:S(2)}) %collective-permute-start.1) | collective-permute-done | bytes 266272 | tf_op jit(solution)/shard_map/ppermute | solution.py:389
  12.1 0.1 collective-permute-start.2
  12.2 0.6 collective-permute-start.3
  12.8 0.0 collective-permute-done.second
  12.8 1.9 %near.1 = (bf16[4,512,128]{2,1,0:T(8,128)(2,1)S(1)}, bf16[256,512]{1,0:T(8,128)(2,1)S(1)}, bf16[512,128]{1,0:T(8,128)(2,1)S(1)}) custom-call(s32[1]{0:T(128)} %bitcast.4.rank, bf16[520,256]{1,0:T(8,128)(2,1)S(1)} %get-tuple-element.27.first, bf16[520,256]{1,0:T(8,128)(2,1)S(1)} %collective-permute-done.second, f32[4,32]{1,0:T(4,128)} %bitcast.25, ...), custom_call_target="tpu_custom_call" | custom-call | tf_op jit(solution)/shard_map/near/pallas_call | solution.py:431
  14.8 0.0 collective-permute-done.3.third
  14.8 0.0 collective-permute-done.2.second
  14.8 1.5 %away.1 = (bf16[4,512,128]{2,1,0:T(8,128)(2,1)S(1)}, bf16[256,512]{1,0:T(8,128)(2,1)S(1)}) custom-call(s32[1]{0:T(128)} %bitcast.4.rank, bf16[520,256]{1,0:T(8,128)(2,1)S(1)} %collective-permute-done.1.first, bf16[264,256]{1,0:T(8,128)(2,1)S(1)} %collective-permute-done.2.second, bf16[256,256]{1,0:T(8,128)(2,1)S(1)} %collective-permute-done.3.third, ...), custom_call_target="tpu_custom_call" | custom-call | tf_op jit(solution)/shard_map/away/pallas_call | solution.py:443
  16.3 1.6 %all-to-all-done.queries = bf16[8,64,256]{2,1,0:T(8,128)(2,1)S(1)} async-done(((bf16[8,64,256]{2,1,0:T(8,128)(2,1)}), bf16[8,64,256]{2,1,0:T(8,128)(2,1)S(1)}, u32[]{:S(2)}, u32[]{:S(2)}) %all-to-all-start) | async-done | bytes 262176 | tf_op jit(solution)/shard_map/all_to_all | solution.py:416
  17.9 0.0 copy-start
  17.9 0.0 copy-start.1
  18.0 0.0 copy-start.2
  18.0 3.7 %attention.1 = (bf16[8,136,128]{2,1,0:T(8,128)(2,1)S(1)}, bf16[8,2048]{1,0:T(8,128)(2,1)S(1)}, bf16[256,2048]{1,0:T(8,128)(2,1)S(1)}) custom-call(s32[1]{0:T(128)} %bitcast.rank, bf16[8,64,256]{2,1,0:T(8,128)(2,1)S(1)} %all-to-all-done.queries, bf16[4,512,128]{2,1,0:T(8,128)(2,1)S(1)} %get-tuple-element.28.keys_near, ...), custom_call_target="tpu_custom_call" | custom-call | tf_op jit(solution)/shard_map/attention/pallas_call | solution.py:451
  21.7 11.5 %all_to_all.30.parts = bf16[8,136,128]{2,1,0:T(8,128)(2,1)S(1)} all-to-all(bf16[8,136,128]{2,1,0:T(8,128)(2,1)S(1)} %get-tuple-element.33), channel_id=1, replica_groups={{0,2,8,10,16,18,24,26},{1,3,9,11,17,19,25,27},{4,6,12,14,20,22,28,30},{..., dimensions={0} | all-to-all | bytes 557056 | tf_op jit(solution)/shard_map/all_to_all | solution.py:462
  33.2 0.4 combine.1
  33.6 17.6 %all_to_all.31.terms = bf16[8,8,2048]{2,1,0:T(8,128)(2,1)S(1)} all-to-all(bf16[8,8,2048]{2,1,0:T(8,128)(2,1)S(1)} %bitcast.15), channel_id=1, replica_groups=mesh['head'=8,'page'=32] {'head'}, dimensions={0} | all-to-all | bytes 524288 | tf_op jit(solution)/shard_map/all_to_all | solution.py:466
  51.2 0.0 copy-done
  51.2 0.0 copy-done.1
  51.2 0.8 norm.1
  52.0 0.1 slice_reduce_fusion
  52.1 4.8 %all-to-all-start.3 = ((bf16[8,8,2048]{2,1,0:T(8,128)(2,1)}), bf16[8,8,2048]{2,1,0:T(8,128)(2,1)S(1)}, u32[]{:S(2)}, u32[]{:S(2)}) async-start(bf16[8,8,2048]{2,1,0:T(8,128)(2,1)} %get-tuple-element.37), calls=%async_computation.3 | async-start | bytes 524288 | tf_op jit(solution)/shard_map/all_to_all | solution.py:485
  56.9 0.0 copy-done.2
  56.9 0.1 dynamic-slice_bitcast_fusion
  57.0 0.1 tile.14
  57.1 0.1 copy.23.own_docs
  57.2 2.6 %down.1 = (f32[1,640]{1,0:T(1,128)S(1)}, bf16[2048,640]{1,0:T(8,128)(2,1)S(1)}) custom-call(bf16[640,2048]{1,0:T(8,128)(2,1)} %weight.2, f32[1,2048]{1,0:T(1,128)S(1)} %bitcast.19, bf16[2048,640]{1,0:T(8,128)(2,1)} %gate_weight), custom_call_target="tpu_custom_call" | custom-call | tf_op jit(solution)/shard_map/down/pallas_call | solution.py:476
  59.7 0.2 convert_reduce_fusion
  60.0 5.6 %all-to-all-done.3 = bf16[8,8,2048]{2,1,0:T(8,128)(2,1)S(1)} async-done(((bf16[8,8,2048]{2,1,0:T(8,128)(2,1)}), bf16[8,8,2048]{2,1,0:T(8,128)(2,1)S(1)}, u32[]{:S(2)}, u32[]{:S(2)}) %all-to-all-start.3) | async-done | bytes 262176 | tf_op jit(solution)/shard_map/all_to_all | solution.py:485
  65.6 2.9 %feed.1 = f32[32,128]{1,0:T(8,128)S(1)} custom-call(bf16[64,2048]{1,0:T(8,128)(2,1)S(1)} %bitcast.16, bf16[2048,640]{1,0:T(8,128)(2,1)S(1)} %get-tuple-element.43.gate_weight, bf16[2048,640]{1,0:T(8,128)(2,1)} %up_weight.1, f32[1,640]{1,0:T(1,128)S(1)} %get-tuple-element.44.down_score, f32[64,1]{1,0:T(8,128)S(1)} %fusion.4.own_score, s32[64,1]{1,0:T(8,128)S(1)} %copy.23.own_docs), custom_call_target="tpu_custom_call" | custom-call | tf_op jit(solution)/shard_map/feed/pallas_call | solution.py:491
  68.5 12.3 %all_to_all.32.terms = f32[32,1,128]{2,1,0:T(1,128)S(1)} all-to-all(f32[32,1,128]{2,1,0:T(1,128)S(1)} %bitcast.17), channel_id=1, replica_groups=mesh['head'=8,'page'=32] {'page'}, dimensions={0} | all-to-all | bytes 32768 | tf_op jit(solution)/shard_map/all_to_all | solution.py:496
  80.9 10.4 %all_to_all.33 = f32[8,1,128]{2,1,0:T(1,128)S(1)} all-to-all(f32[8,1,128]{2,1,0:T(1,128)S(1)} %fold.1), channel_id=1, replica_groups=mesh['head'=8,'page'=32] {'head'}, dimensions={0} | all-to-all | bytes 8192 | tf_op jit(solution)/shard_map/all_to_all | solution.py:498
  91.3 0.5 slice_divide_fusion
  (7 shorter events, 0.1 us)
Async XLA Ops:
  2.4 9.7 %collective-permute-start.1 = (bf16[520,256]{1,0:T(8,128)(2,1)S(1)}, bf16[520,256]{1,0:T(8,128)(2,1)S(1)}, u32[]{:S(2)}, u32[]{:S(2)}) collective-permute-start(bf16[520,256]{1,0:T(8,128)(2,1)S(1)} %get-tuple-element.27.first), channel_id=1, source_target_pairs={{0,4},{1,5},{2,6},{3,7},{4,0},{5,1},{6,2},{7,3},{8,12},{9,13},{10,... | collective-permute-start | bytes 798728 | tf_op jit(solution)/shard_map/ppermute | solution.py:389
  5.5 7.3 %collective-permute-start = (bf16[520,256]{1,0:T(8,128)(2,1)S(1)}, bf16[520,256]{1,0:T(8,128)(2,1)S(1)}, u32[]{:S(2)}, u32[]{:S(2)}) collective-permute-start(bf16[520,256]{1,0:T(8,128)(2,1)S(1)} %get-tuple-element.27.first), channel_id=1, source_target_pairs={{0,1},{1,0},{2,3},{3,2},{4,5},{5,4},{6,7},{7,6},{8,9},{9,8},{10,11... | collective-permute-start | bytes 798728 | tf_op jit(solution)/shard_map/ppermute | solution.py:389
  5.5 12.4 %all-to-all-start = ((bf16[8,64,256]{2,1,0:T(8,128)(2,1)}), bf16[8,64,256]{2,1,0:T(8,128)(2,1)S(1)}, u32[]{:S(2)}, u32[]{:S(2)}) async-start(bf16[8,64,256]{2,1,0:T(8,128)(2,1)} %get-tuple-element.26), calls=%async_computation | async-start | bytes 524288 | tf_op jit(solution)/shard_map/all_to_all | solution.py:416
  12.1 2.6 %collective-permute-start.2 = (bf16[264,256]{1,0:T(8,128)(2,1)S(1)}, bf16[264,256]{1,0:T(8,128)(2,1)S(1)}, u32[]{:S(2)}, u32[]{:S(2)}) collective-permute-start(bf16[264,256]{1,0:T(8,128)(2,1)S(1)} %slice.16), channel_id=1, source_target_pairs={{0,1},{1,0},{2,3},{3,2},{4,5},{5,4},{6,7},{7,6},{8,9},{9,8},{10,11... | collective-permute-start | bytes 405512 | tf_op jit(solution)/shard_map/ppermute | solution.py:389
  12.2 2.5 %collective-permute-start.3 = (bf16[256,256]{1,0:T(8,128)(2,1)S(1)}, bf16[256,256]{1,0:T(8,128)(2,1)S(1)}, u32[]{:S(2)}, u32[]{:S(2)}) collective-permute-start(bf16[256,256]{1,0:T(8,128)(2,1)S(1)} %slice.17), channel_id=1, source_target_pairs={{0,1},{1,0},{2,3},{3,2},{4,5},{5,4},{6,7},{7,6},{8,9},{9,8},{10,11... | collective-permute-start | bytes 393224 | tf_op jit(solution)/shard_map/ppermute | solution.py:389
  17.9 33.2 %copy-start = (f32[2048]{0:T(1024)S(1)}, f32[2048]{0:T(1024)}, u32[]{:S(2)}) copy-start(f32[2048]{0:T(1024)} %param.29) | copy-start | bytes 24580
  17.9 33.2 %copy-start.1 = (f32[2048]{0:T(1024)S(1)}, f32[2048]{0:T(1024)}, u32[]{:S(2)}) copy-start(f32[2048]{0:T(1024)} %param.25) | copy-start | bytes 24580
  18.0 39.0 %copy-start.2 = (s32[2048]{0:T(1024)S(1)}, s32[2048]{0:T(1024)}, u32[]{:S(2)}) copy-start(s32[2048]{0:T(1024)} %param.32) | copy-start | bytes 24580
  52.1 13.5 %all-to-all-start.3 = ((bf16[8,8,2048]{2,1,0:T(8,128)(2,1)}), bf16[8,8,2048]{2,1,0:T(8,128)(2,1)S(1)}, u32[]{:S(2)}, u32[]{:S(2)}) async-start(bf16[8,8,2048]{2,1,0:T(8,128)(2,1)} %get-tuple-element.37), calls=%async_computation.3 | async-start | bytes 524288 | tf_op jit(solution)/shard_map/all_to_all | solution.py:485

commit v12 on v11

--- a/solution.py
+++ b/solution.py
@@ -216,7 +216,7 @@
             weights = jnp.exp(part - top)
             total += jnp.sum(weights, axis=0, keepdims=True)
             summed += jnp.dot(values[span, :], weights.astype(BF), preferred_element_type=F32)
-        sums.append(summed / total)
+        sums.append(summed * (1.0 / total))
         logs.append(top + jnp.log(total))
     for duo in range(chips // 2):
         lanes = slice(duo * 128, (duo + 1) * 128)

time: 93.5 us -> 93.5 us (level)
  no operation moved by 1% of the time
where the time goes in v12:
time: 93.5 us; the launch traced here: 91.8 us
  blocking collectives  51.8 us (55%)
  Pallas kernels  16.3 us (17%)
  starting transfers between devices  13.1 us (14%)
  waiting for transfers between devices  9.4 us (10%)
    all_to_all x1, blocking collectives, per_device(): lax.all_to_all(projected.reshape(head_size, own, model), 'head', 0, 0, ti...  17.6 us
    all_to_all x1, blocking collectives, per_device(): arrived = lax.all_to_all(doc_sums, 'page', 0, 0, tiled=True)  12.3 us
    all_to_all x1, blocking collectives, per_device(): lax.all_to_all(partials, 'page', 0, 0, axis_index_groups=groups, tiled=True)  11.5 us
    all_to_all x1, blocking collectives, per_device(): lax.all_to_all(pooled, 'head', 0, 0, tiled=True)  10.4 us
    all_to_all x1, waiting for transfers between devices, per_device(): lax.all_to_all(spread, 'head', 0, 0, tiled=True).reshape(tok_dev, model)  5.64 us
    all_to_all x1, starting transfers between devices, per_device(): lax.all_to_all(spread, 'head', 0, 0, tiled=True).reshape(tok_dev, model)  4.78 us
    all_to_all x1, starting transfers between devices, per_device(): lax.all_to_all(copies, 'page', 0, 0, axis_index_groups=groups, tiled=True)  4.5 us
    ppermute x4, starting transfers between devices, swap(): return lax.ppermute(value, 'page', pairs)  3.78 us
  transfers between devices with their start and end apart: 6, of which 3 were waited for; matrix products, arithmetic and copies ran while one was open for 1% of the time, Pallas kernels for 7%

profile of v12, /device:TPU:32, one launch (start us, length us, event | category | flops | bytes accessed | tf_op | source)
XLA Modules:
  0.0 91.8 jit_solution(12841467752683281397)
XLA Ops:
  0.0 2.4 %project.1 = (bf16[8,64,256]{2,1,0:T(8,128)(2,1)}, bf16[520,256]{1,0:T(8,128)(2,1)S(1)}) custom-call(bf16[64,2048]{1,0:T(8,128)(2,1)} %states.3, f32[1,2048]{1,0:T(1,128)} %bitcast.24, bf16[2048,256]{1,0:T(8,128)(2,1)} %weight.1, bf16[256,256]{1,0:T(8,128)(2,1)} %bitcast.21, bf16[256,256]{1,0:T(8,128)(2,1)} %bitcast.22, s32[2,128]{1,0:T(2,128)} %buckets.1), custom_call_target="tpu_custom_call" | custom-call | tf_op jit(solution)/shard_map/project/pallas_call | solution.py:392
  2.4 3.1 %collective-permute-start.1 = (bf16[520,256]{1,0:T(8,128)(2,1)S(1)}, bf16[520,256]{1,0:T(8,128)(2,1)S(1)}, u32[]{:S(2)}, u32[]{:S(2)}) collective-permute-start(bf16[520,256]{1,0:T(8,128)(2,1)S(1)} %get-tuple-element.27.first), channel_id=1, source_target_pairs={{0,4},{1,5},{2,6},{3,7},{4,0},{5,1},{6,2},{7,3},{8,12},{9,13},{10,... | collective-permute-start | bytes 798728 | tf_op jit(solution)/shard_map/ppermute | solution.py:389
  5.5 0.0 collective-permute-start
  5.5 4.5 %all-to-all-start = ((bf16[8,64,256]{2,1,0:T(8,128)(2,1)}), bf16[8,64,256]{2,1,0:T(8,128)(2,1)S(1)}, u32[]{:S(2)}, u32[]{:S(2)}) async-start(bf16[8,64,256]{2,1,0:T(8,128)(2,1)} %get-tuple-element.26), calls=%async_computation | async-start | bytes 524288 | tf_op jit(solution)/shard_map/all_to_all | solution.py:416
  10.0 2.1 %collective-permute-done.1.first = bf16[520,256]{1,0:T(8,128)(2,1)S(1)} collective-permute-done((bf16[520,256]{1,0:T(8,128)(2,1)S(1)}, bf16[520,256]{1,0:T(8,128)(2,1)S(1)}, u32[]{:S(2)}, u32[]{:S(2)}) %collective-permute-start.1) | collective-permute-done | bytes 266272 | tf_op jit(solution)/shard_map/ppermute | solution.py:389
  12.1 0.1 collective-permute-start.2
  12.2 0.6 collective-permute-start.3
  12.8 0.0 collective-permute-done.second
  12.8 1.9 %near.1 = (bf16[4,512,128]{2,1,0:T(8,128)(2,1)S(1)}, bf16[256,512]{1,0:T(8,128)(2,1)S(1)}, bf16[512,128]{1,0:T(8,128)(2,1)S(1)}) custom-call(s32[1]{0:T(128)} %bitcast.4.rank, bf16[520,256]{1,0:T(8,128)(2,1)S(1)} %get-tuple-element.27.first, bf16[520,256]{1,0:T(8,128)(2,1)S(1)} %collective-permute-done.second, f32[4,32]{1,0:T(4,128)} %bitcast.25, ...), custom_call_target="tpu_custom_call" | custom-call | tf_op jit(solution)/shard_map/near/pallas_call | solution.py:431
  14.8 0.0 collective-permute-done.3.third
  14.8 0.0 collective-permute-done.2.second
  14.8 1.5 %away.1 = (bf16[4,512,128]{2,1,0:T(8,128)(2,1)S(1)}, bf16[256,512]{1,0:T(8,128)(2,1)S(1)}) custom-call(s32[1]{0:T(128)} %bitcast.4.rank, bf16[520,256]{1,0:T(8,128)(2,1)S(1)} %collective-permute-done.1.first, bf16[264,256]{1,0:T(8,128)(2,1)S(1)} %collective-permute-done.2.second, bf16[256,256]{1,0:T(8,128)(2,1)S(1)} %collective-permute-done.3.third, ...), custom_call_target="tpu_custom_call" | custom-call | tf_op jit(solution)/shard_map/away/pallas_call | solution.py:443
  16.3 1.6 %all-to-all-done.queries = bf16[8,64,256]{2,1,0:T(8,128)(2,1)S(1)} async-done(((bf16[8,64,256]{2,1,0:T(8,128)(2,1)}), bf16[8,64,256]{2,1,0:T(8,128)(2,1)S(1)}, u32[]{:S(2)}, u32[]{:S(2)}) %all-to-all-start) | async-done | bytes 262176 | tf_op jit(solution)/shard_map/all_to_all | solution.py:416
  17.9 0.0 copy-start
  17.9 0.0 copy-start.1
  18.0 0.0 copy-start.2
  18.0 3.7 %attention.1 = (bf16[8,136,128]{2,1,0:T(8,128)(2,1)S(1)}, bf16[8,2048]{1,0:T(8,128)(2,1)S(1)}, bf16[256,2048]{1,0:T(8,128)(2,1)S(1)}) custom-call(s32[1]{0:T(128)} %bitcast.rank, bf16[8,64,256]{2,1,0:T(8,128)(2,1)S(1)} %all-to-all-done.queries, bf16[4,512,128]{2,1,0:T(8,128)(2,1)S(1)} %get-tuple-element.28.keys_near, ...), custom_call_target="tpu_custom_call" | custom-call | tf_op jit(solution)/shard_map/attention/pallas_call | solution.py:451
  21.7 11.5 %all_to_all.30.parts = bf16[8,136,128]{2,1,0:T(8,128)(2,1)S(1)} all-to-all(bf16[8,136,128]{2,1,0:T(8,128)(2,1)S(1)} %get-tuple-element.33), channel_id=1, replica_groups={{0,2,8,10,16,18,24,26},{1,3,9,11,17,19,25,27},{4,6,12,14,20,22,28,30},{..., dimensions={0} | all-to-all | bytes 557056 | tf_op jit(solution)/shard_map/all_to_all | solution.py:462
  33.2 0.4 combine.1
  33.6 17.6 %all_to_all.31.terms = bf16[8,8,2048]{2,1,0:T(8,128)(2,1)S(1)} all-to-all(bf16[8,8,2048]{2,1,0:T(8,128)(2,1)S(1)} %bitcast.15), channel_id=1, replica_groups=mesh['head'=8,'page'=32] {'head'}, dimensions={0} | all-to-all | bytes 524288 | tf_op jit(solution)/shard_map/all_to_all | solution.py:466
  51.2 0.0 copy-done
  51.2 0.0 copy-done.1
  51.2 0.8 norm.1
  52.0 0.1 slice_reduce_fusion
  52.1 4.8 %all-to-all-start.3 = ((bf16[8,8,2048]{2,1,0:T(8,128)(2,1)}), bf16[8,8,2048]{2,1,0:T(8,128)(2,1)S(1)}, u32[]{:S(2)}, u32[]{:S(2)}) async-start(bf16[8,8,2048]{2,1,0:T(8,128)(2,1)} %get-tuple-element.37), calls=%async_computation.3 | async-start | bytes 524288 | tf_op jit(solution)/shard_map/all_to_all | solution.py:485
  56.9 0.0 copy-done.2
  56.9 0.1 dynamic-slice_bitcast_fusion
  57.0 0.1 tile.14
  57.1 0.1 copy.23.own_docs
  57.2 2.6 %down.1 = (f32[1,640]{1,0:T(1,128)S(1)}, bf16[2048,640]{1,0:T(8,128)(2,1)S(1)}) custom-call(bf16[640,2048]{1,0:T(8,128)(2,1)} %weight.2, f32[1,2048]{1,0:T(1,128)S(1)} %bitcast.19, bf16[2048,640]{1,0:T(8,128)(2,1)} %gate_weight), custom_call_target="tpu_custom_call" | custom-call | tf_op jit(solution)/shard_map/down/pallas_call | solution.py:476
  59.7 0.2 convert_reduce_fusion
  60.0 5.6 %all-to-all-done.3 = bf16[8,8,2048]{2,1,0:T(8,128)(2,1)S(1)} async-done(((bf16[8,8,2048]{2,1,0:T(8,128)(2,1)}), bf16[8,8,2048]{2,1,0:T(8,128)(2,1)S(1)}, u32[]{:S(2)}, u32[]{:S(2)}) %all-to-all-start.3) | async-done | bytes 262176 | tf_op jit(solution)/shard_map/all_to_all | solution.py:485
  65.6 2.9 %feed.1 = f32[32,128]{1,0:T(8,128)S(1)} custom-call(bf16[64,2048]{1,0:T(8,128)(2,1)S(1)} %bitcast.16, bf16[2048,640]{1,0:T(8,128)(2,1)S(1)} %get-tuple-element.43.gate_weight, bf16[2048,640]{1,0:T(8,128)(2,1)} %up_weight.1, f32[1,640]{1,0:T(1,128)S(1)} %get-tuple-element.44.down_score, f32[64,1]{1,0:T(8,128)S(1)} %fusion.4.own_score, s32[64,1]{1,0:T(8,128)S(1)} %copy.23.own_docs), custom_call_target="tpu_custom_call" | custom-call | tf_op jit(solution)/shard_map/feed/pallas_call | solution.py:491
  68.5 12.3 %all_to_all.32.terms = f32[32,1,128]{2,1,0:T(1,128)S(1)} all-to-all(f32[32,1,128]{2,1,0:T(1,128)S(1)} %bitcast.17), channel_id=1, replica_groups=mesh['head'=8,'page'=32] {'page'}, dimensions={0} | all-to-all | bytes 32768 | tf_op jit(solution)/shard_map/all_to_all | solution.py:496
  80.9 10.4 %all_to_all.33 = f32[8,1,128]{2,1,0:T(1,128)S(1)} all-to-all(f32[8,1,128]{2,1,0:T(1,128)S(1)} %fold.1), channel_id=1, replica_groups=mesh['head'=8,'page'=32] {'head'}, dimensions={0} | all-to-all | bytes 8192 | tf_op jit(solution)/shard_map/all_to_all | solution.py:498
  91.3 0.5 slice_divide_fusion
  (7 shorter events, 0.1 us)
Async XLA Ops:
  2.4 9.7 %collective-permute-start.1 = (bf16[520,256]{1,0:T(8,128)(2,1)S(1)}, bf16[520,256]{1,0:T(8,128)(2,1)S(1)}, u32[]{:S(2)}, u32[]{:S(2)}) collective-permute-start(bf16[520,256]{1,0:T(8,128)(2,1)S(1)} %get-tuple-element.27.first), channel_id=1, source_target_pairs={{0,4},{1,5},{2,6},{3,7},{4,0},{5,1},{6,2},{7,3},{8,12},{9,13},{10,... | collective-permute-start | bytes 798728 | tf_op jit(solution)/shard_map/ppermute | solution.py:389
  5.5 7.3 %collective-permute-start = (bf16[520,256]{1,0:T(8,128)(2,1)S(1)}, bf16[520,256]{1,0:T(8,128)(2,1)S(1)}, u32[]{:S(2)}, u32[]{:S(2)}) collective-permute-start(bf16[520,256]{1,0:T(8,128)(2,1)S(1)} %get-tuple-element.27.first), channel_id=1, source_target_pairs={{0,1},{1,0},{2,3},{3,2},{4,5},{5,4},{6,7},{7,6},{8,9},{9,8},{10,11... | collective-permute-start | bytes 798728 | tf_op jit(solution)/shard_map/ppermute | solution.py:389
  5.5 12.4 %all-to-all-start = ((bf16[8,64,256]{2,1,0:T(8,128)(2,1)}), bf16[8,64,256]{2,1,0:T(8,128)(2,1)S(1)}, u32[]{:S(2)}, u32[]{:S(2)}) async-start(bf16[8,64,256]{2,1,0:T(8,128)(2,1)} %get-tuple-element.26), calls=%async_computation | async-start | bytes 524288 | tf_op jit(solution)/shard_map/all_to_all | solution.py:416
  12.1 2.6 %collective-permute-start.2 = (bf16[264,256]{1,0:T(8,128)(2,1)S(1)}, bf16[264,256]{1,0:T(8,128)(2,1)S(1)}, u32[]{:S(2)}, u32[]{:S(2)}) collective-permute-start(bf16[264,256]{1,0:T(8,128)(2,1)S(1)} %slice.16), channel_id=1, source_target_pairs={{0,1},{1,0},{2,3},{3,2},{4,5},{5,4},{6,7},{7,6},{8,9},{9,8},{10,11... | collective-permute-start | bytes 405512 | tf_op jit(solution)/shard_map/ppermute | solution.py:389
  12.2 2.5 %collective-permute-start.3 = (bf16[256,256]{1,0:T(8,128)(2,1)S(1)}, bf16[256,256]{1,0:T(8,128)(2,1)S(1)}, u32[]{:S(2)}, u32[]{:S(2)}) collective-permute-start(bf16[256,256]{1,0:T(8,128)(2,1)S(1)} %slice.17), channel_id=1, source_target_pairs={{0,1},{1,0},{2,3},{3,2},{4,5},{5,4},{6,7},{7,6},{8,9},{9,8},{10,11... | collective-permute-start | bytes 393224 | tf_op jit(solution)/shard_map/ppermute | solution.py:389
  17.9 33.2 %copy-start = (f32[2048]{0:T(1024)S(1)}, f32[2048]{0:T(1024)}, u32[]{:S(2)}) copy-start(f32[2048]{0:T(1024)} %param.29) | copy-start | bytes 24580
  17.9 33.2 %copy-start.1 = (f32[2048]{0:T(1024)S(1)}, f32[2048]{0:T(1024)}, u32[]{:S(2)}) copy-start(f32[2048]{0:T(1024)} %param.25) | copy-start | bytes 24580
  18.0 39.0 %copy-start.2 = (s32[2048]{0:T(1024)S(1)}, s32[2048]{0:T(1024)}, u32[]{:S(2)}) copy-start(s32[2048]{0:T(1024)} %param.32) | copy-start | bytes 24580
  52.1 13.5 %all-to-all-start.3 = ((bf16[8,8,2048]{2,1,0:T(8,128)(2,1)}), bf16[8,8,2048]{2,1,0:T(8,128)(2,1)S(1)}, u32[]{:S(2)}, u32[]{:S(2)}) async-start(bf16[8,8,2048]{2,1,0:T(8,128)(2,1)} %get-tuple-element.37), calls=%async_computation.3 | async-start | bytes 524288 | tf_op jit(solution)/shard_map/all_to_all | solution.py:485
